TPU v7x, 256 devices: a whole 4x4x8 slice. The times are simulated.
256 devices in a mesh: dp: 4 (over x), tm: 8 (over z_hi, core), space: 8 (over y, z_lo).
Axes of the slice: x: 4, y: 4, z: 8 (z_hi: 4, z_lo: 2; z = z_hi * 2 + z_lo), core: 2. Of those that a mesh axis runs over, the one named last changes fastest.
Arguments:
- feats: bfloat16 [4, 8, 64, 128, 256], P('dp', 'tm', 'space'), may hold values from -6 to 6
- w_spatial: bfloat16 [3, 3, 256, 256], replicated, may hold values from -0.125 to 0.125
- w_temporal: bfloat16 [768, 256], replicated, may hold values from -0.21875 to 0.21875
- teacher_mid: bfloat16 [4, 8, 64, 128, 256], P('dp', 'tm', 'space'), may hold values from -6 to 6
- w_down: bfloat16 [2, 2, 256, 512], replicated, may hold values from -0.1875 to 0.1875
- w_query: bfloat16 [512, 512], replicated, may hold values from -8 to 8
- w_key: bfloat16 [512, 512], replicated, may hold values from -1 to 1
- w_value: bfloat16 [512, 512], replicated, may hold values from -0.25 to 0.25
- w_out: bfloat16 [512, 512], replicated, may hold values from -0.25 to 0.25
- teacher_top: bfloat16 [4, 8, 32, 64, 512], P('dp', 'tm', 'space'), may hold values from -6 to 6
Outputs:
- student_top: bfloat16 [4, 8, 32, 64, 512], P('dp', 'tm', 'space')
- grad_temporal: float32 [768, 256], P(('tm', 'space'))
- grad_out: float32 [512, 512], P(('tm', 'space'))
All inputs are finite; a program needn't handle non-finite values.
Results may differ from a plain program's by a relative error of at most 0.0075.
Values may be sent and summed in bfloat16 or wider, within the bound.
No kernel may reach another device: no remote copies, remote signals or barrier semaphores. Data moves between devices by JAX's collectives and lax.ppermute only.
A program may use at most 64 MiB of HBM per device.

v0:
```python
import math

import jax
import jax.numpy as jnp
from jax import lax
from jax.sharding import PartitionSpec as P


def extended(cells, sides, width):
    for axis, dim in sides:
        count = lax.axis_size(axis)
        ends = count - 1
        head = lax.slice_in_dim(cells, 0, width, axis=dim)
        tail = lax.slice_in_dim(cells, cells.shape[dim] - width, cells.shape[dim], axis=dim)
        cells = jnp.concatenate(
            [
                lax.ppermute(tail, axis, [(i, (i + 1) % count) for i in range(ends)]),
                cells,
                lax.ppermute(head, axis, [((i + 1) % count, i) for i in range(ends)]),
            ],
            axis=dim,
        )
    return cells


def from_behind(block, axis, distance):
    devices = range(lax.axis_size(axis))
    route = [(i - distance, i) for i in devices if i - distance in devices]
    return lax.ppermute(block, axis, route)


def local(
    feats, w_spatial, w_temporal, teacher_mid, w_down, w_query, w_key, w_value, w_out, teacher_top
):
    numbers = ("NHWC", "HWIO", "NHWC")
    frame_in = feats[0, 0]
    rows_here, cols_here, chan = frame_in.shape
    devices_all = lax.axis_size("dp") * lax.axis_size("tm") * lax.axis_size("space")
    group = lax.axis_size("tm") * lax.axis_size("space")
    padded = extended(frame_in, (("space", 0),), 1)
    conv = lax.conv_general_dilated(
        padded[None],
        w_spatial,
        (1, 1),
        ((0, 0), (1, 1)),
        dimension_numbers=numbers,
        preferred_element_type=jnp.float32,
    )[0]
    spatial = jax.nn.silu(conv).astype(jnp.bfloat16)
    back_one = from_behind(spatial, "tm", 1)
    back_two = from_behind(spatial, "tm", 2)
    stacked = jnp.concatenate([back_two, back_one, spatial], -1).reshape(
        rows_here * cols_here, 3 * chan
    )
    temporal = jnp.dot(stacked, w_temporal, preferred_element_type=jnp.float32)
    mid = (frame_in.reshape(-1, chan).astype(jnp.float32) + temporal).astype(jnp.bfloat16)
    diff_mid = (
        mid.astype(jnp.float32) - teacher_mid[0, 0].reshape(-1, chan).astype(jnp.float32)
    ).astype(jnp.bfloat16)
    scale_mid = 1.0 / math.sqrt(rows_here * cols_here * devices_all)
    columns = stacked
    share_temporal = lax.psum_scatter(
        lax.dot_general(
            columns, diff_mid, (((0,), (0,)), ((), ())), preferred_element_type=jnp.float32
        )
        * scale_mid,
        ("tm", "space"),
        scatter_dimension=0,
        tiled=True,
    )
    coarse = lax.conv_general_dilated(
        mid.reshape(1, rows_here, cols_here, chan),
        w_down,
        (2, 2),
        "VALID",
        dimension_numbers=numbers,
        preferred_element_type=jnp.float32,
    )[0].astype(jnp.bfloat16)
    half_rows, half_cols, width = coarse.shape
    points = half_rows * half_cols
    coarse = coarse.reshape(points, width)
    score_scale = 1.0 / math.sqrt(width)
    frame_here = lax.axis_index("tm")
    query = jnp.dot(coarse, w_query, preferred_element_type=jnp.float32).astype(jnp.bfloat16)
    key = jnp.dot(coarse, w_key, preferred_element_type=jnp.float32).astype(jnp.bfloat16)
    value = jnp.dot(coarse, w_value, preferred_element_type=jnp.float32).astype(jnp.bfloat16)
    query, key, value = (query, key, value)
    query_f = query.astype(jnp.float32)
    best = jnp.full((points,), -1e30, jnp.float32)
    totals = jnp.zeros((points,), jnp.float32)
    accum = jnp.zeros((points, width), jnp.float32)
    key_piece = lax.all_gather(key[None], "tm", axis=0, tiled=True)
    value_piece = lax.all_gather(value[None], "tm", axis=0, tiled=True)
    count = key_piece.shape[0]
    scores = jnp.einsum("pd,npd->np", query_f, key_piece.astype(jnp.float32)) * score_scale
    frame_ids = jnp.arange(count, dtype=jnp.int32)
    valid = ((frame_ids <= frame_here) & (frame_ids >= 0))[:, None]
    scores = jnp.where(valid, scores, -1e30)
    new_best = jnp.maximum(best, jnp.max(scores, 0))
    weights = jnp.where(valid, jnp.exp(scores - new_best[None]), 0.0)
    shrink = jnp.exp(best - new_best)
    totals = totals * shrink + jnp.sum(weights, 0)
    accum = accum * shrink[:, None] + jnp.einsum(
        "np,npd->pd", weights, value_piece.astype(jnp.float32)
    )
    attended = (accum / totals[:, None]).astype(jnp.bfloat16)
    out = jnp.dot(attended, w_out, preferred_element_type=jnp.float32)
    student = (coarse.astype(jnp.float32) + out).astype(jnp.bfloat16)
    diff_top = (
        student.astype(jnp.float32) - teacher_top[0, 0].reshape(points, width).astype(jnp.float32)
    ).astype(jnp.bfloat16)
    scale_top = 1.0 / math.sqrt(points * devices_all)
    columns = lax.slice_in_dim(
        attended, 0, lax.axis_size(("tm", "space")) * (width // group), axis=1
    )
    share_out = lax.psum_scatter(
        lax.dot_general(
            columns, diff_top, (((0,), (0,)), ((), ())), preferred_element_type=jnp.float32
        )
        * scale_top,
        ("tm", "space"),
        scatter_dimension=0,
        tiled=True,
    )
    grad_temporal, grad_out = lax.psum((share_temporal, share_out), "dp")
    return (student.reshape(1, 1, half_rows, half_cols, width), grad_temporal, grad_out)


def solution(mesh):
    return jax.shard_map(
        local,
        mesh=mesh,
        in_specs=(
            P("dp", "tm", "space", None, None),
            P(),
            P(),
            P("dp", "tm", "space", None, None),
            P(),
            P(),
            P(),
            P(),
            P(),
            P("dp", "tm", "space", None, None),
        ),
        out_specs=(
            P("dp", "tm", "space", None, None),
            P(("tm", "space"), None),
            P(("tm", "space"), None),
        ),
        check_vma=False,
    )
```

profile of v0, /device:TPU:4, one launch (start us, length us, event | category | flops | bytes accessed | tf_op | source)
XLA Modules:
  0.0 433.1 jit_solution(17433136230925251478)
XLA Ops:
  7.2 1.0 slice_bitcast_fusion.2
  8.2 3.8 collective-permute-start
  12.0 1.3 collective-permute-start.1
  13.3 0.6 collective-permute-done
  13.9 4.3 collective-permute-done.1
  18.2 1.1 maximum_bitcast_fusion
  19.3 0.2 pad
  19.5 0.2 reshape.49
  19.8 0.1 copy.36
  19.9 0.2 copy-done.11
  20.2 1.5 convolution_select_fusion
  21.7 0.4 copy.37
  22.0 0.3 multiply_convert_fusion
  22.3 1.3 collective-permute-start.3
  23.6 5.8 %collective-permute-start.2 = (bf16[8,128,256]{2,0,1:T(8,128)(2,1)S(1)}, bf16[8,128,256]{2,0,1:T(8,128)(2,1)S(1)}, u32[]{:S(2)}, u32[]{:S(2)}) collective-permute-start(bf16[8,128,256]{2,0,1:T(8,128)(2,1)S(1)} %multiply_convert_fusion), channel_id=1, source_target_pairs={{0,16},{8,24},{16,32},{24,40},{32,48},{40,56},{1,17},{9,25},{17,33... | collective-permute-start | bytes 1572872 | tf_op jit(solution)/shard_map/ppermute | solution.py:29
  29.5 12.3 %collective-permute-done.2 = bf16[8,128,256]{2,0,1:T(8,128)(2,1)S(1)} collective-permute-done((bf16[8,128,256]{2,0,1:T(8,128)(2,1)S(1)}, bf16[8,128,256]{2,0,1:T(8,128)(2,1)S(1)}, u32[]{:S(2)}, u32[]{:S(2)}) %collective-permute-start.2) | collective-permute-done | bytes 524320 | tf_op jit(solution)/shard_map/ppermute | solution.py:29
  41.7 0.1 pad_maximum_fusion
  41.9 0.3 copy.38
  42.2 0.7 copy-done.1
  42.9 0.1 copy-done.8
  43.0 0.6 fusion.6
  43.6 0.8 copy-done.4
  44.4 0.2 copy.40
  44.6 0.4 convolution_convert_fusion.3
  45.1 0.1 copy.41
  45.1 0.5 copy-done.2
  45.6 1.0 convolution_convert_fusion.2
  46.7 1.0 convolution_convert_fusion
  47.8 1.3 fusion.8
  49.1 56.7 %all-gather.5.cloned.1.call-done = bf16[2048,512]{1,0:T(8,128)(2,1)} async-done(((bf16[256,512]{1,0:T(8,128)(2,1)}), bf16[2048,512]{1,0:T(8,128)(2,1)}) %all-gather.5.cloned.1.call-update) | async-done | bytes 2097168 | tf_op jit(solution)/shard_map/all_gather | solution.py:92
  105.8 3.3 fusion.3
  109.1 0.1 copy.44
  109.1 0.1 fusion.32
  109.2 0.1 fusion.34
  109.3 0.2 copy.45
  109.5 0.1 fusion.33
  109.6 32.6 %all-gather.7.cloned.1.call-done = bf16[2048,512]{1,0:T(8,128)(2,1)} async-done(((bf16[256,512]{1,0:T(8,128)(2,1)}), bf16[2048,512]{1,0:T(8,128)(2,1)}) %all-gather.7.cloned.1.call-update) | async-done | bytes 2097168 | tf_op jit(solution)/shard_map/all_gather | solution.py:93
  142.2 3.2 fusion.1
  145.4 0.4 fusion.7
  145.8 0.7 copy-done.10
  146.5 1.4 convolution_multiply_fusion
  148.0 1.8 convolution_multiply_fusion.1
  149.8 133.7 %fusion = f32[16,256]{1,0:T(8,128)S(1)} fusion(f32[768,256]{1,0:T(8,128)S(1)} %convolution_multiply_fusion.1), kind=kCustom, calls=%all-reduce-scatter | all-reduce-scatter fusion | flops 262145 | bytes 803840
  283.5 1.3 collective-permute-start.19
  284.8 2.3 collective-permute-start.18
  287.1 1.3 collective-permute-start.17
  288.4 1.3 collective-permute-start.16
  289.7 3.6 collective-permute-start.15
  293.4 3.2 collective-permute-start.14
  296.6 6.0 %collective-permute-start.13 = (f32[16,256]{1,0:T(8,128)S(1)}, f32[16,256]{1,0:T(8,128)S(1)}, u32[]{:S(2)}, u32[]{:S(2)}) collective-permute-start(f32[16,256]{1,0:T(8,128)S(1)} %fusion), channel_id=1, source_target_pairs={{0,10},{1,11},{2,12},{3,13},{4,14},{5,15},{6,16},{7,17},{8,18},{9,... | collective-permute-start | bytes 49160
  302.6 1.9 collective-permute-start.12
  304.5 1.3 collective-permute-start.11
  305.9 5.0 %collective-permute-start.10 = (f32[16,256]{1,0:T(8,128)S(1)}, f32[16,256]{1,0:T(8,128)S(1)}, u32[]{:S(2)}, u32[]{:S(2)}) collective-permute-start(f32[16,256]{1,0:T(8,128)S(1)} %fusion), channel_id=1, source_target_pairs={{0,7},{1,8},{2,9},{3,10},{4,11},{5,12},{6,13},{7,14},{8,15},{9,16}... | collective-permute-start | bytes 49160
  310.9 1.8 collective-permute-start.9
  312.7 2.8 collective-permute-start.8
  315.5 4.0 collective-permute-start.7
  319.6 1.8 collective-permute-start.6
  321.4 2.2 collective-permute-start.5
  323.6 4.0 collective-permute-start.4
  327.7 0.6 dynamic-slice.4
  328.9 0.1 collective-permute-done.4
  329.1 1.8 concatenate.10
  330.9 79.0 %reduce-scatter.4.cloned.1.call-done = f32[8,512]{1,0:T(8,128)} async-done(((f32[512,512]{1,0:T(8,128)}), f32[8,512]{1,0:T(8,128)}) %reduce-scatter.4.cloned.1.call-update) | async-done | bytes 16400 | tf_op jit(solution)/shard_map/reduce_scatter | solution.py:116
  409.9 16.7 %all-reduce.2 = (f32[12,256]{1,0:T(8,128)}, f32[8,512]{1,0:T(8,128)}) all-reduce(f32[12,256]{1,0:T(8,128)S(1)} %constant_dynamic-slice_fusion, f32[8,512]{1,0:T(8,128)} %reduce-scatter.4.cloned.1.call-done), channel_id=1, replica_groups=mesh['dp'=4,'tm'=8,'space'=8] {'dp'}, use_global_device_ids=true, to_apply=%region_3.4 | all-reduce | flops 7168 | bytes 57344 | tf_op jit(solution)/shard_map/psum | solution.py:125
  (47 shorter events, 0.3 us)
Async XLA Ops:
  7.2 12.8 %copy-start = (bf16[3,3,256,256]{3,2,1,0:T(8,128)(2,1)S(1)}, bf16[3,3,256,256]{3,2,1,0:T(8,128)(2,1)}, u32[]{:S(2)}) copy-start(bf16[3,3,256,256]{3,2,1,0:T(8,128)(2,1)} %param.11) | copy-start | bytes 3538948
  7.2 98.6 %all-gather.5.cloned.1.call-start = ((), (), s32[]{:S(2)}) async-start(), calls=%async_computation.2 | async-start | bytes 2359296 | tf_op jit(solution)/shard_map/all_gather | solution.py:92
  8.2 5.7 %collective-permute-start = (bf16[1,128,256]{2,1,0:T(8,128)(2,1)S(1)}, bf16[1,128,256]{2,1,0:T(8,128)(2,1)S(1)}, u32[]{:S(2)}, u32[]{:S(2)}) collective-permute-start(bf16[1,128,256]{2,1,0:T(8,128)(2,1)S(1)} %get-tuple-element.5), channel_id=1, source_target_pairs={{0,1},{1,2},{2,3},{3,4},{4,5},{5,6},{6,7},{8,9},{9,10},{10,11},{11... | collective-permute-start | bytes 196616 | tf_op jit(solution)/shard_map/ppermute | solution.py:17
  12.0 6.2 %collective-permute-start.1 = (bf16[1,128,256]{2,1,0:T(8,128)(2,1)S(1)}, bf16[1,128,256]{2,1,0:T(8,128)(2,1)S(1)}, u32[]{:S(2)}, u32[]{:S(2)}) collective-permute-start(bf16[1,128,256]{2,1,0:T(8,128)(2,1)S(1)} %get-tuple-element.6), channel_id=1, source_target_pairs={{1,0},{2,1},{3,2},{4,3},{5,4},{6,5},{7,6},{9,8},{10,9},{11,10},{12... | collective-permute-start | bytes 196616 | tf_op jit(solution)/shard_map/ppermute | solution.py:19
  19.5 0.7 copy-start.11
  22.3 7.1 %collective-permute-start.3 = (bf16[8,128,256]{2,0,1:T(8,128)(2,1)S(1)}, bf16[8,128,256]{2,0,1:T(8,128)(2,1)S(1)}, u32[]{:S(2)}, u32[]{:S(2)}) collective-permute-start(bf16[8,128,256]{2,0,1:T(8,128)(2,1)S(1)} %multiply_convert_fusion), channel_id=1, source_target_pairs={{0,8},{8,16},{16,24},{24,32},{32,40},{40,48},{48,56},{1,9},{9,17},... | collective-permute-start | bytes 1572872 | tf_op jit(solution)/shard_map/ppermute | solution.py:29
  23.6 18.1 %collective-permute-start.2 = (bf16[8,128,256]{2,0,1:T(8,128)(2,1)S(1)}, bf16[8,128,256]{2,0,1:T(8,128)(2,1)S(1)}, u32[]{:S(2)}, u32[]{:S(2)}) collective-permute-start(bf16[8,128,256]{2,0,1:T(8,128)(2,1)S(1)} %multiply_convert_fusion), channel_id=1, source_target_pairs={{0,16},{8,24},{16,32},{24,40},{32,48},{40,56},{1,17},{9,25},{17,33... | collective-permute-start | bytes 1572872 | tf_op jit(solution)/shard_map/ppermute | solution.py:29
  41.8 1.0 copy-start.1
  41.8 1.1 copy-start.8
  43.0 1.6 copy-start.6
  43.6 0.8 copy-start.4
  44.6 1.0 copy-start.2
  44.6 2.1 copy-start.3
  46.6 95.6 %all-gather.7.cloned.1.call-start = ((), (), s32[]{:S(2)}) async-start(), calls=%async_computation.3 | async-start | bytes 2359296 | tf_op jit(solution)/shard_map/all_gather | solution.py:93
  47.7 362.1 %reduce-scatter.4.cloned.1.call-start = ((), (), s32[]{:S(2)}) async-start(), calls=%async_computation.1 | async-start | bytes 1064960 | tf_op jit(solution)/shard_map/reduce_scatter | solution.py:116
  142.2 3.2 copy-start.7
  145.4 1.1 copy-start.9
  145.8 0.7 copy-start.10
  148.0 179.7 %copy-start.5 = (u32[256]{0:T(256)S(1)}, u32[256]{0:T(256)}, u32[]{:S(2)}) copy-start(u32[256]{0:T(256)} %constant.40) | copy-start | bytes 3076
  283.5 9.9 %collective-permute-start.19 = (f32[12,256]{1,0:T(8,128)S(1)}, f32[12,256]{1,0:T(8,128)S(1)}, u32[]{:S(2)}, u32[]{:S(2)}) collective-permute-start(f32[12,256]{1,0:T(8,128)S(1)} %slice.23), channel_id=1, source_target_pairs={{0,16},{1,17},{2,18},{3,19},{4,20},{5,21},{6,22},{7,23},{8,24},{9,... | collective-permute-start | bytes 36872
  284.8 11.8 %collective-permute-start.18 = (f32[16,256]{1,0:T(8,128)S(1)}, f32[16,256]{1,0:T(8,128)S(1)}, u32[]{:S(2)}, u32[]{:S(2)}) collective-permute-start(f32[16,256]{1,0:T(8,128)S(1)} %fusion), channel_id=1, source_target_pairs={{0,15},{1,16},{2,17},{3,18},{4,19},{5,20},{6,21},{7,22},{8,23},{9,... | collective-permute-start | bytes 49160
  287.1 15.5 %collective-permute-start.17 = (f32[16,256]{1,0:T(8,128)S(1)}, f32[16,256]{1,0:T(8,128)S(1)}, u32[]{:S(2)}, u32[]{:S(2)}) collective-permute-start(f32[16,256]{1,0:T(8,128)S(1)} %fusion), channel_id=1, source_target_pairs={{0,14},{1,15},{2,16},{3,17},{4,18},{5,19},{6,20},{7,21},{8,22},{9,... | collective-permute-start | bytes 49160
  288.4 16.1 %collective-permute-start.16 = (f32[16,256]{1,0:T(8,128)S(1)}, f32[16,256]{1,0:T(8,128)S(1)}, u32[]{:S(2)}, u32[]{:S(2)}) collective-permute-start(f32[16,256]{1,0:T(8,128)S(1)} %fusion), channel_id=1, source_target_pairs={{0,13},{1,14},{2,15},{3,16},{4,17},{5,18},{6,19},{7,20},{8,21},{9,... | collective-permute-start | bytes 49160
  289.7 16.1 %collective-permute-start.15 = (f32[16,256]{1,0:T(8,128)S(1)}, f32[16,256]{1,0:T(8,128)S(1)}, u32[]{:S(2)}, u32[]{:S(2)}) collective-permute-start(f32[16,256]{1,0:T(8,128)S(1)} %fusion), channel_id=1, source_target_pairs={{0,12},{1,13},{2,14},{3,15},{4,16},{5,17},{6,18},{7,19},{8,20},{9,... | collective-permute-start | bytes 49160
  293.4 17.5 %collective-permute-start.14 = (f32[16,256]{1,0:T(8,128)S(1)}, f32[16,256]{1,0:T(8,128)S(1)}, u32[]{:S(2)}, u32[]{:S(2)}) collective-permute-start(f32[16,256]{1,0:T(8,128)S(1)} %fusion), channel_id=1, source_target_pairs={{0,11},{1,12},{2,13},{3,14},{4,15},{5,16},{6,17},{7,18},{8,19},{9,... | collective-permute-start | bytes 49160
  296.6 16.1 %collective-permute-start.13 = (f32[16,256]{1,0:T(8,128)S(1)}, f32[16,256]{1,0:T(8,128)S(1)}, u32[]{:S(2)}, u32[]{:S(2)}) collective-permute-start(f32[16,256]{1,0:T(8,128)S(1)} %fusion), channel_id=1, source_target_pairs={{0,10},{1,11},{2,12},{3,13},{4,14},{5,15},{6,16},{7,17},{8,18},{9,... | collective-permute-start | bytes 49160
  302.6 12.9 %collective-permute-start.12 = (f32[16,256]{1,0:T(8,128)S(1)}, f32[16,256]{1,0:T(8,128)S(1)}, u32[]{:S(2)}, u32[]{:S(2)}) collective-permute-start(f32[16,256]{1,0:T(8,128)S(1)} %fusion), channel_id=1, source_target_pairs={{0,9},{1,10},{2,11},{3,12},{4,13},{5,14},{6,15},{7,16},{8,17},{9,1... | collective-permute-start | bytes 49160
  304.5 15.0 %collective-permute-start.11 = (f32[16,256]{1,0:T(8,128)S(1)}, f32[16,256]{1,0:T(8,128)S(1)}, u32[]{:S(2)}, u32[]{:S(2)}) collective-permute-start(f32[16,256]{1,0:T(8,128)S(1)} %fusion), channel_id=1, source_target_pairs={{0,8},{1,9},{2,10},{3,11},{4,12},{5,13},{6,14},{7,15},{8,16},{9,17... | collective-permute-start | bytes 49160
  305.9 15.5 %collective-permute-start.10 = (f32[16,256]{1,0:T(8,128)S(1)}, f32[16,256]{1,0:T(8,128)S(1)}, u32[]{:S(2)}, u32[]{:S(2)}) collective-permute-start(f32[16,256]{1,0:T(8,128)S(1)} %fusion), channel_id=1, source_target_pairs={{0,7},{1,8},{2,9},{3,10},{4,11},{5,12},{6,13},{7,14},{8,15},{9,16}... | collective-permute-start | bytes 49160
  310.9 12.7 %collective-permute-start.9 = (f32[16,256]{1,0:T(8,128)S(1)}, f32[16,256]{1,0:T(8,128)S(1)}, u32[]{:S(2)}, u32[]{:S(2)}) collective-permute-start(f32[16,256]{1,0:T(8,128)S(1)} %fusion), channel_id=1, source_target_pairs={{0,6},{1,7},{2,8},{3,9},{4,10},{5,11},{6,12},{7,13},{8,14},{9,15},... | collective-permute-start | bytes 49160
  312.7 16.2 %collective-permute-start.8 = (f32[16,256]{1,0:T(8,128)S(1)}, f32[16,256]{1,0:T(8,128)S(1)}, u32[]{:S(2)}, u32[]{:S(2)}) collective-permute-start(f32[16,256]{1,0:T(8,128)S(1)} %fusion), channel_id=1, source_target_pairs={{0,5},{1,6},{2,7},{3,8},{4,9},{5,10},{6,11},{7,12},{8,13},{9,14},{... | collective-permute-start | bytes 49160
  315.5 13.4 %collective-permute-start.7 = (f32[16,256]{1,0:T(8,128)S(1)}, f32[16,256]{1,0:T(8,128)S(1)}, u32[]{:S(2)}, u32[]{:S(2)}) collective-permute-start(f32[16,256]{1,0:T(8,128)S(1)} %fusion), channel_id=1, source_target_pairs={{0,4},{1,5},{2,6},{3,7},{4,8},{5,9},{6,10},{7,11},{8,12},{9,13},{1... | collective-permute-start | bytes 49160
  319.6 9.4 %collective-permute-start.6 = (f32[16,256]{1,0:T(8,128)S(1)}, f32[16,256]{1,0:T(8,128)S(1)}, u32[]{:S(2)}, u32[]{:S(2)}) collective-permute-start(f32[16,256]{1,0:T(8,128)S(1)} %fusion), channel_id=1, source_target_pairs={{0,3},{1,4},{2,5},{3,6},{4,7},{5,8},{6,9},{7,10},{8,11},{9,12},{10... | collective-permute-start | bytes 49160
  321.4 7.5 %collective-permute-start.5 = (f32[16,256]{1,0:T(8,128)S(1)}, f32[16,256]{1,0:T(8,128)S(1)}, u32[]{:S(2)}, u32[]{:S(2)}) collective-permute-start(f32[16,256]{1,0:T(8,128)S(1)} %fusion), channel_id=1, source_target_pairs={{0,2},{1,3},{2,4},{3,5},{4,6},{5,7},{6,8},{7,9},{8,10},{9,11},{10,... | collective-permute-start | bytes 49160
  323.6 5.4 %collective-permute-start.4 = (f32[16,256]{1,0:T(8,128)S(1)}, f32[16,256]{1,0:T(8,128)S(1)}, u32[]{:S(2)}, u32[]{:S(2)}) collective-permute-start(f32[16,256]{1,0:T(8,128)S(1)} %fusion), channel_id=1, source_target_pairs={{0,1},{1,2},{2,3},{3,4},{4,5},{5,6},{6,7},{7,8},{8,9},{9,10},{10,1... | collective-permute-start | bytes 49160
Sparse Core Ops, SparseCore 0:
  46.8 58.9 all-gather.4
  107.7 34.5 all-gather.6
  148.1 261.7 reduce-scatter.3
where the time goes:
time: 434 us; the launch traced here: 433 us
  waiting for transfers between devices  186 us (43%)
  blocking collectives  150 us (35%)
  starting transfers between devices  56.3 us (13%)
  matrix products  15.9 us (4%)
  between operations  15 us (3%)
  local copies, waits for them, and re-layouts  8.18 us (2%)
    unnamed x1, blocking collectives  134 us
    reduce_scatter x1, waiting for transfers between devices, local(): lax.psum_scatter(lax.dot_general(columns, diff_top, (((0,), (0,)), ((), (...  79 us
    all_gather x1, waiting for transfers between devices, local(): key_piece = lax.all_gather(key[None], 'tm', axis=0, tiled=True)  56.7 us
    unnamed x16, starting transfers between devices  43.9 us
    all_gather x1, waiting for transfers between devices, local(): value_piece = lax.all_gather(value[None], 'tm', axis=0, tiled=True)  32.6 us
    psum x1, blocking collectives, local(): grad_temporal, grad_out = lax.psum((share_temporal, share_out), 'dp')  16.7 us
    ppermute x2, waiting for transfers between devices, from_behind(): return lax.ppermute(block, axis, route)  12.3 us
  transfers between devices with their start and end apart: 23, of which 7 were waited for; matrix products, arithmetic and copies ran while one was open for 33% of the time, Pallas kernels for 0%

commit v1 on v0

v1 whole, which is shorter than its diff:
```python
import math

import jax
import jax.numpy as jnp
from jax import lax
from jax.sharding import PartitionSpec as P

F32 = jnp.float32
BF16 = jnp.bfloat16


def reduce_shares(grad):
    frames = lax.axis_size("tm")
    spaces = lax.axis_size("space")
    clips = lax.axis_size("dp")
    rows, cols = grad.shape
    piece = rows // (frames * spaces)
    halves = grad.reshape(frames // 2, 2, spaces, piece, cols)
    core = lax.axis_index("tm") % 2
    keep = lax.dynamic_index_in_dim(halves, core, 1, keepdims=False)
    give = lax.dynamic_index_in_dim(halves, 1 - core, 1, keepdims=False)
    got = lax.ppermute(give, "tm", [(i, i ^ 1) for i in range(frames)])
    part = (keep + got).transpose(1, 0, 2, 3).astype(BF16)
    part = lax.all_to_all(part, "space", 0, 0, tiled=True)
    part = jnp.sum(part.astype(F32), 0).astype(BF16)
    groups = [list(range(c, frames, 2)) for c in range(2)]
    part = lax.all_to_all(part, "tm", 0, 0, axis_index_groups=groups, tiled=True)
    part = jnp.sum(part.astype(F32), 0)
    others = [
        lax.ppermute(part, "dp", [(i, (i + k) % clips) for i in range(clips)])
        for k in range(1, clips)
    ]
    for other in others:
        part = part + other
    return part


def local(
    feats, w_spatial, w_temporal, teacher_mid, w_down, w_query, w_key, w_value, w_out, teacher_top
):
    numbers = ("NHWC", "HWIO", "NHWC")
    frames = lax.axis_size("tm")
    spaces = lax.axis_size("space")
    devices_all = lax.axis_size("dp") * frames * spaces
    frame_in = feats[0, 0]
    rows, cols, chan = frame_in.shape
    strip = cols // frames

    wide = jnp.pad(frame_in, ((0, 0), (1, 1), (0, 0)))
    windows = jnp.stack([wide[:, j * strip : j * strip + strip + 2] for j in range(frames)])
    windows = windows.reshape(frames, rows * (strip + 2), chan)
    cells = lax.all_to_all(windows, "tm", 0, 0, tiled=True)
    cells = cells.reshape(frames, rows, strip + 2, chan)

    half_rows, half_cols, width = teacher_top.shape[2:]
    half_strip = half_cols // frames
    t_mid = teacher_mid[0, 0].reshape(rows, frames, strip, chan).transpose(1, 0, 2, 3)
    t_mid = t_mid.reshape(frames, rows * strip, chan)
    t_top = teacher_top[0, 0].reshape(half_rows, frames, half_strip, width).transpose(1, 0, 2, 3)
    points = half_rows * half_strip
    t_top = t_top.reshape(frames, points, width)
    t_mid = lax.all_to_all(t_mid, "tm", 0, 0, tiled=True)
    t_top = lax.all_to_all(t_top, "tm", 0, 0, tiled=True)

    above = lax.ppermute(cells[:, rows - 1], "space", [(i, i + 1) for i in range(spaces - 1)])
    below = lax.ppermute(cells[:, 0], "space", [(i + 1, i) for i in range(spaces - 1)])
    padded = jnp.concatenate([above[:, None], cells, below[:, None]], 1)

    conv = lax.conv_general_dilated(
        padded, w_spatial, (1, 1), "VALID", dimension_numbers=numbers, preferred_element_type=F32
    )
    spatial = jax.nn.silu(conv).astype(BF16).reshape(frames, rows * strip, chan)
    back_one = jnp.pad(spatial[:-1], ((1, 0), (0, 0), (0, 0)))
    back_two = jnp.pad(spatial[:-2], ((2, 0), (0, 0), (0, 0)))
    stacked = jnp.concatenate([back_two, back_one, spatial], -1).reshape(-1, 3 * chan)
    temporal = jnp.dot(stacked, w_temporal, preferred_element_type=F32)
    centre = cells[:, :, 1 : strip + 1].reshape(-1, chan)
    mid = (centre.astype(F32) + temporal).astype(BF16)
    diff_mid = (mid.astype(F32) - t_mid.reshape(-1, chan).astype(F32)).astype(BF16)
    scale_mid = 1.0 / math.sqrt(rows * cols * devices_all)
    grad_temporal = (
        lax.dot_general(stacked, diff_mid, (((0,), (0,)), ((), ())), preferred_element_type=F32)
        * scale_mid
    )
    grad_temporal = reduce_shares(grad_temporal)

    coarse = lax.conv_general_dilated(
        mid.reshape(frames, rows, strip, chan),
        w_down,
        (2, 2),
        "VALID",
        dimension_numbers=numbers,
        preferred_element_type=F32,
    ).astype(BF16)
    coarse = coarse.reshape(frames * points, width)
    query = jnp.dot(coarse, w_query, preferred_element_type=F32).astype(BF16)
    key = jnp.dot(coarse, w_key, preferred_element_type=F32).astype(BF16)
    value = jnp.dot(coarse, w_value, preferred_element_type=F32).astype(BF16)
    query = query.astype(F32).reshape(frames, points, width)
    key = key.astype(F32).reshape(frames, points, width)
    value = value.astype(F32).reshape(frames, points, width)
    scores = jnp.sum(query[:, None] * key[None], -1) * (1.0 / math.sqrt(width))
    earlier = jnp.arange(frames)[:, None] >= jnp.arange(frames)[None, :]
    scores = jnp.where(earlier[:, :, None], scores, -1e30)
    best = jnp.max(scores, 1, keepdims=True)
    weights = jnp.where(earlier[:, :, None], jnp.exp(scores - best), 0.0)
    totals = jnp.sum(weights, 1)
    attended = jnp.sum(weights[..., None] * value[None], 1) / totals[..., None]
    attended = attended.astype(BF16).reshape(frames * points, width)
    out = jnp.dot(attended, w_out, preferred_element_type=F32)
    student = (coarse.astype(F32) + out).astype(BF16)
    home = lax.all_to_all(student.reshape(frames, points, width), "tm", 0, 0, tiled=True)
    home = home.reshape(frames, half_rows, half_strip, width).transpose(1, 0, 2, 3)
    diff_top = (student.astype(F32) - t_top.reshape(-1, width).astype(F32)).astype(BF16)
    scale_top = 1.0 / math.sqrt(points * frames * devices_all)
    grad_out = (
        lax.dot_general(attended, diff_top, (((0,), (0,)), ((), ())), preferred_element_type=F32)
        * scale_top
    )
    grad_out = reduce_shares(grad_out)
    return (home.reshape(1, 1, half_rows, half_cols, width), grad_temporal, grad_out)


def solution(mesh):
    return jax.shard_map(
        local,
        mesh=mesh,
        in_specs=(
            P("dp", "tm", "space", None, None),
            P(),
            P(),
            P("dp", "tm", "space", None, None),
            P(),
            P(),
            P(),
            P(),
            P(),
            P("dp", "tm", "space", None, None),
        ),
        out_specs=(
            P("dp", "tm", "space", None, None),
            P(("tm", "space"), None),
            P(("tm", "space"), None),
        ),
        check_vma=False,
    )
```

time: 434 us -> 152 us (0.35)
  blocking collectives: 150 us -> 0 us
  waiting for transfers between devices: 186 us -> 67.1 us
  between operations: 15 us -> 1.1 us
  local copies, waits for them, and re-layouts: 8.18 us -> 16.5 us
  matrix products: 15.9 us -> 8.82 us
  starting transfers between devices: 56.3 us -> 51.4 us
    unnamed x1 -> x0, blocking collectives: 134 us -> none
    all_gather x2 -> x0, waiting for transfers between devices: 89.3 us -> none  [the longest x1 56.7 us: local(): key_piece = lax.all_gather(key[None], 'tm', axis=0, tiled=True)]
    reduce_scatter x1 -> x0, waiting for transfers between devices: 79 us -> none  [local(): lax.psum_scatter(lax.dot_general(columns, diff_top, (((0,), (0,)), ((), (...]
    all_to_all x0 -> x8, waiting for transfers between devices: none -> 55 us  [the longest x1 17.8 us: local(): cells = lax.all_to_all(windows, 'tm', 0, 0, tiled=True)]
    unnamed x16 -> x0, starting transfers between devices: 43.9 us -> none
    all_to_all x0 -> x8, starting transfers between devices: none -> 37.9 us  [the longest x2 9.34 us: reduce_shares(): part = lax.all_to_all(part, 'space', 0, 0, tiled=True)]
    psum x1 -> x0, blocking collectives: 16.7 us -> none  [local(): grad_temporal, grad_out = lax.psum((share_temporal, share_out), 'dp')]
    dot_general x9 -> x7, matrix products: 14 us -> 6.69 us  [the longest x1 2.85 us: local(): lax.dot_general(stacked, diff_mid, (((0,), (0,)), ((), ())), preferred_el...]
  transfers between devices with their start and end apart: 23 -> 18, of which waited for: 7 -> 10; matrix products, arithmetic and copies ran while one was open for 33% -> 14% of each run, Pallas kernels for 0% -> 0%
where the time goes in v1:
time: 152 us; the launch traced here: 150 us
  waiting for transfers between devices  67.1 us (44%)
  starting transfers between devices  51.4 us (34%)
  local copies, waits for them, and re-layouts  16.5 us (11%)
  matrix products  8.82 us (6%)
  other arithmetic  5.61 us (4%)
    all_to_all x1, waiting for transfers between devices, local(): cells = lax.all_to_all(windows, 'tm', 0, 0, tiled=True)  17.8 us
    all_to_all x2, waiting for transfers between devices, reduce_shares(): part = lax.all_to_all(part, 'space', 0, 0, tiled=True)  12.7 us
    all_to_all x2, waiting for transfers between devices, reduce_shares(): lax.all_to_all(part, 'tm', 0, 0, axis_index_groups=groups, tiled=True)  10.9 us
    all_to_all x2, starting transfers between devices, reduce_shares(): part = lax.all_to_all(part, 'space', 0, 0, tiled=True)  9.34 us
    ppermute x1, waiting for transfers between devices, local(): lax.ppermute(cells[:, 0], 'space', [(i + 1, i) for i in range(spaces - 1)])  9.01 us
    all_to_all x1, starting transfers between devices, local(): cells = lax.all_to_all(windows, 'tm', 0, 0, tiled=True)  8.47 us
    all_to_all x1, waiting for transfers between devices, local(): lax.all_to_all(student.reshape(frames, points, width), 'tm', 0, 0, tiled=...  7.9 us
    ppermute x6, starting transfers between devices, reduce_shares(): lax.ppermute(part, 'dp', [(i, (i + k) % clips) for i in range(clips)])  6.69 us
  transfers between devices with their start and end apart: 18, of which 10 were waited for; matrix products, arithmetic and copies ran while one was open for 14% of the time, Pallas kernels for 0%

profile of v1, /device:TPU:4, one launch (start us, length us, event | category | flops | bytes accessed | tf_op | source)
XLA Modules:
  0.0 150.5 jit_solution(17601309548582035484)
XLA Ops:
  0.6 1.8 %pad_slice_fusion = (bf16[8,18,256]{2,1,0:T(8,128)(2,1)S(1)}, bf16[8,18,256]{2,1,0:T(8,128)(2,1)S(1)}, bf16[8,18,256]{2,1,0:T(8,128)(2,1)S(1)}, bf16[8,18,256]{2...) fusion(bf16[8,128,256]{2,1,0:T(8,128)(2,1)} %bitcast.99), kind=kLoop, calls=%fused_computation.35 | loop fusion | bytes 1703936 | tf_op jit(solution)/shard_map/slice | solution.py:50
  2.5 0.6 constant_dynamic-update-slice_fusion.7
  3.4 0.6 constant_dynamic-update-slice_fusion.6
  4.0 0.6 constant_dynamic-update-slice_fusion.5
  4.6 0.6 constant_dynamic-update-slice_fusion.4
  5.2 0.6 constant_dynamic-update-slice_fusion.3
  5.9 0.6 constant_dynamic-update-slice_fusion.2
  6.5 0.6 constant_dynamic-update-slice_fusion.1
  7.1 0.6 constant_dynamic-update-slice_fusion
  7.8 8.5 %all-to-all-start = ((bf16[8,144,256]{2,1,0:T(8,128)(2,1)}), bf16[8,144,256]{2,1,0:T(8,128)(2,1)S(1)}, u32[]{:S(2)}, u32[]{:S(2)}) async-start(bf16[8,144,256]{2,1,0:T(8,128)(2,1)} %constant_dynamic-update-slice_fusion), calls=%async_computation | async-start | bytes 1179648 | tf_op jit(solution)/shard_map/all_to_all | solution.py:52
  16.2 0.8 copy.101
  17.1 0.7 copy_bitcast_fusion.2
  17.8 17.8 %all-to-all-done = bf16[8,144,256]{2,1,0:T(8,128)(2,1)S(1)} async-done(((bf16[8,144,256]{2,1,0:T(8,128)(2,1)}), bf16[8,144,256]{2,1,0:T(8,128)(2,1)S(1)}, u32[]{:S(2)}, u32[]{:S(2)}) %all-to-all-start) | async-done | bytes 589856 | tf_op jit(solution)/shard_map/all_to_all | solution.py:52
  35.6 3.5 %all-to-all-start.2 = ((bf16[8,128,256]{2,1,0:T(8,128)(2,1)}), bf16[8,128,256]{2,1,0:T(8,128)(2,1)S(1)}, u32[]{:S(2)}, u32[]{:S(2)}) async-start(bf16[8,128,256]{2,1,0:T(8,128)(2,1)} %bitcast.24), calls=%async_computation.2 | async-start | bytes 1048576 | tf_op jit(solution)/shard_map/all_to_all | solution.py:62
  39.4 1.3 collective-permute-start.1
  40.7 4.5 %collective-permute-start = (bf16[8,18,256]{2,0,1:T(8,128)(2,1)S(1)}, bf16[8,18,256]{2,0,1:T(8,128)(2,1)S(1)}, u32[]{:S(2)}, u32[]{:S(2)}) collective-permute-start(bf16[8,18,256]{2,0,1:T(8,128)(2,1)S(1)} %get-tuple-element.7), channel_id=1, source_target_pairs={{0,1},{1,2},{2,3},{3,4},{4,5},{5,6},{6,7},{8,9},{9,10},{10,11},{11... | collective-permute-start | bytes 221192 | tf_op jit(solution)/shard_map/ppermute | solution.py:65
  45.3 0.3 copy.94
  45.7 9.0 %collective-permute-done.1 = bf16[8,18,256]{2,0,1:T(8,128)(2,1)S(1)} collective-permute-done((bf16[8,18,256]{2,0,1:T(8,128)(2,1)S(1)}, bf16[8,18,256]{2,0,1:T(8,128)(2,1)S(1)}, u32[]{:S(2)}, u32[]{:S(2)}) %collective-permute-start.1) | collective-permute-done | bytes 73760 | tf_op jit(solution)/shard_map/ppermute | solution.py:66
  54.7 1.4 multiply_convert_fusion
  56.5 0.9 copy-done.11
  57.4 0.6 fusion.1
  58.0 0.6 copy-done.10
  58.6 0.7 convolution_convert_fusion.3
  59.5 0.2 copy-done.2
  59.7 0.3 bitcast_convert_fusion.1
  60.0 0.5 copy-done.3
  60.4 0.3 bitcast_convert_fusion.2
  60.7 0.4 multiply_reduce_fusion.1
  61.1 0.7 fusion.33
  61.9 0.3 bitcast_convert_fusion
  62.2 6.6 %all-to-all-start.5 = ((bf16[8,32,512]{2,1,0:T(8,128)(2,1)}), bf16[8,32,512]{2,1,0:T(8,128)(2,1)}, u32[]{:S(2)}, u32[]{:S(2)}) async-start(bf16[8,32,512]{2,1,0:T(8,128)(2,1)} %copy_bitcast_fusion.2), calls=%async_computation.5 | async-start | bytes 524288 | tf_op jit(solution)/shard_map/all_to_all | solution.py:63
  68.8 2.9 %convolution_multiply_fusion.1 = f32[768,256]{1,0:T(8,128)} fusion(bf16[1024,256]{1,0:T(8,128)(2,1)} %bitcast.106, bf16[1024,256]{1,0:T(8,128)(2,1)S(1)} %bitcast.102, bf16[1024,256]{1,0:T(8,128)(2,1)} %bitcast.108, bf16[1024,256]{1,0:T(8,128)(2,1)S(1)} %bitcast.104, bf16[1024,256]{1,0:T(8,128)(2,1)} %copy-done.12), kind=kOutput, calls=%fused_computation.7 | convolution fusion | flops 408616960 | bytes 3407872 | tf_op jit(solution)/shard_map/dot_general | solution.py:82
  71.7 1.2 reshape.105
  73.0 1.0 copy.122
  74.0 0.5 collective-permute-start.2
  74.5 0.3 multiply_reduce_fusion
  75.0 1.0 fusion.2
  76.0 5.7 %all-to-all-done.5 = bf16[8,32,512]{2,1,0:T(8,128)(2,1)} async-done(((bf16[8,32,512]{2,1,0:T(8,128)(2,1)}), bf16[8,32,512]{2,1,0:T(8,128)(2,1)}, u32[]{:S(2)}, u32[]{:S(2)}) %all-to-all-start.5) | async-done | bytes 262176 | tf_op jit(solution)/shard_map/all_to_all | solution.py:63
  81.7 3.4 %all-to-all-start.1 = ((bf16[8,32,512]{2,1,0:T(8,128)(2,1)}), bf16[8,32,512]{2,1,0:T(8,128)(2,1)S(1)}, u32[]{:S(2)}, u32[]{:S(2)}) async-start(bf16[8,32,512]{2,1,0:T(8,128)(2,1)} %bitcast.18), calls=%async_computation.1 | async-start | bytes 524288 | tf_op jit(solution)/shard_map/all_to_all | solution.py:112
  85.1 1.4 convolution_multiply_fusion
  86.6 0.5 collective-permute-start.6
  87.1 1.2 fusion.23
  88.3 0.8 copy.104
  89.2 7.9 %all-to-all-done.1 = bf16[8,32,512]{2,1,0:T(8,128)(2,1)S(1)} async-done(((bf16[8,32,512]{2,1,0:T(8,128)(2,1)}), bf16[8,32,512]{2,1,0:T(8,128)(2,1)S(1)}, u32[]{:S(2)}, u32[]{:S(2)}) %all-to-all-start.1) | async-done | bytes 262176 | tf_op jit(solution)/shard_map/all_to_all | solution.py:112
  97.0 5.9 %all-to-all-start.3 = ((bf16[8,4,12,256]{3,1,2,0:T(4,128)(2,1)}), bf16[8,4,12,256]{3,1,2,0:T(4,128)(2,1)S(1)}, u32[]{:S(2)}, u32[]{:S(2)}) async-start(bf16[8,4,12,256]{3,1,2,0:T(4,128)(2,1)} %copy.104), calls=%async_computation.3 | async-start | bytes 393216 | tf_op jit(solution)/shard_map/all_to_all | solution.py:24
  103.0 0.8 fusion.21
  103.8 6.2 %all-to-all-done.3 = bf16[8,4,12,256]{3,1,2,0:T(4,128)(2,1)S(1)} async-done(((bf16[8,4,12,256]{3,1,2,0:T(4,128)(2,1)}), bf16[8,4,12,256]{3,1,2,0:T(4,128)(2,1)S(1)}, u32[]{:S(2)}, u32[]{:S(2)}) %all-to-all-start.3) | async-done | bytes 196640 | tf_op jit(solution)/shard_map/all_to_all | solution.py:24
  109.9 3.4 %all-to-all-start.6 = ((bf16[8,4,8,512]{3,2,1,0:T(8,128)(2,1)}), bf16[8,4,8,512]{3,2,1,0:T(8,128)(2,1)S(1)}, u32[]{:S(2)}, u32[]{:S(2)}) async-start(bf16[8,4,8,512]{3,2,1,0:T(8,128)(2,1)} %fusion.21), calls=%async_computation.6 | async-start | bytes 524288 | tf_op jit(solution)/shard_map/all_to_all | solution.py:24
  113.5 0.6 copy.105
  114.1 6.5 %all-to-all-done.6 = bf16[8,4,8,512]{3,2,1,0:T(8,128)(2,1)S(1)} async-done(((bf16[8,4,8,512]{3,2,1,0:T(8,128)(2,1)}), bf16[8,4,8,512]{3,2,1,0:T(8,128)(2,1)S(1)}, u32[]{:S(2)}, u32[]{:S(2)}) %all-to-all-start.6) | async-done | bytes 262176 | tf_op jit(solution)/shard_map/all_to_all | solution.py:24
  120.6 3.3 %all-to-all-start.4 = ((bf16[4,12,256]{2,1,0:T(8,128)(2,1)}), bf16[4,12,256]{2,1,0:T(8,128)(2,1)S(1)}, u32[]{:S(2)}, u32[]{:S(2)}) async-start(bf16[4,12,256]{2,1,0:T(8,128)(2,1)} %copy.105), calls=%async_computation.4 | async-start | bytes 65536 | tf_op jit(solution)/shard_map/all_to_all | solution.py:27
  123.9 0.7 copy_bitcast_fusion.3
  124.6 0.6 reduce_sum.77
  125.2 6.5 %all-to-all-done.4 = bf16[4,12,256]{2,1,0:T(8,128)(2,1)S(1)} async-done(((bf16[4,12,256]{2,1,0:T(8,128)(2,1)}), bf16[4,12,256]{2,1,0:T(8,128)(2,1)S(1)}, u32[]{:S(2)}, u32[]{:S(2)}) %all-to-all-start.4) | async-done | bytes 24608 | tf_op jit(solution)/shard_map/all_to_all | solution.py:27
  131.7 3.3 %all-to-all-start.7 = ((bf16[4,8,512]{2,1,0:T(8,128)(2,1)}), bf16[4,8,512]{2,1,0:T(8,128)(2,1)S(1)}, u32[]{:S(2)}, u32[]{:S(2)}) async-start(bf16[4,8,512]{2,1,0:T(8,128)(2,1)} %reduce_sum.77), calls=%async_computation.7 | async-start | bytes 65536 | tf_op jit(solution)/shard_map/all_to_all | solution.py:27
  135.0 0.6 collective-permute-start.5
  135.6 2.7 %collective-permute-start.4 = (f32[12,256]{1,0:T(8,128)S(1)}, f32[12,256]{1,0:T(8,128)S(1)}, u32[]{:S(2)}, u32[]{:S(2)}) collective-permute-start(f32[12,256]{1,0:T(8,128)S(1)} %convert_reduce_fusion.1), channel_id=1, source_target_pairs={{0,128},{64,192},{128,0},{192,64},{1,129},{65,193},{129,1},{193,65... | collective-permute-start | bytes 36872 | tf_op jit(solution)/shard_map/ppermute | solution.py:30
  138.3 4.5 %all-to-all-done.7 = bf16[4,8,512]{2,1,0:T(8,128)(2,1)S(1)} async-done(((bf16[4,8,512]{2,1,0:T(8,128)(2,1)}), bf16[4,8,512]{2,1,0:T(8,128)(2,1)S(1)}, u32[]{:S(2)}, u32[]{:S(2)}) %all-to-all-start.7) | async-done | bytes 32800 | tf_op jit(solution)/shard_map/all_to_all | solution.py:27
  142.8 0.6 collective-permute-start.9
  143.4 2.7 %collective-permute-start.8 = (f32[8,512]{1,0:T(8,128)S(1)}, f32[8,512]{1,0:T(8,128)S(1)}, u32[]{:S(2)}, u32[]{:S(2)}) collective-permute-start(f32[8,512]{1,0:T(8,128)S(1)} %convert_reduce_fusion), channel_id=1, source_target_pairs={{0,128},{64,192},{128,0},{192,64},{1,129},{65,193},{129,1},{193,65... | collective-permute-start | bytes 49160 | tf_op jit(solution)/shard_map/ppermute | solution.py:30
  146.2 0.6 add_add_fusion.1
  146.8 1.9 %collective-permute-done.8 = f32[8,512]{1,0:T(8,128)S(1)} collective-permute-done((f32[8,512]{1,0:T(8,128)S(1)}, f32[8,512]{1,0:T(8,128)S(1)}, u32[]{:S(2)}, u32[]{:S(2)}) %collective-permute-start.8) | collective-permute-done | bytes 16416 | tf_op jit(solution)/shard_map/ppermute | solution.py:30
  148.6 1.2 collective-permute-done.7
  149.9 0.6 add_add_fusion
  (58 shorter events, 1.6 us)
Async XLA Ops:
  0.6 54.0 %copy-start = (bf16[3,3,256,256]{3,2,1,0:T(8,128)(2,1)S(1)}, bf16[3,3,256,256]{3,2,1,0:T(8,128)(2,1)}, u32[]{:S(2)}) copy-start(bf16[3,3,256,256]{3,2,1,0:T(8,128)(2,1)} %param.11) | copy-start | bytes 3538948
  3.3 12.9 %copy-start.1 = (bf16[1,1,8,128,256]{4,3,2,1,0:T(8,128)(2,1)S(1)}, bf16[1,1,8,128,256]{4,3,2,1,0:T(8,128)(2,1)}, u32[]{:S(2)}) copy-start(bf16[1,1,8,128,256]{4,3,2,1,0:T(8,128)(2,1)} %param.13) | copy-start | bytes 1572868
  7.1 10.0 %copy-start.8 = (bf16[1,1,4,64,512]{4,3,2,1,0:T(8,128)(2,1)S(1)}, bf16[1,1,4,64,512]{4,3,2,1,0:T(8,128)(2,1)}, u32[]{:S(2)}) copy-start(bf16[1,1,4,64,512]{4,3,2,1,0:T(8,128)(2,1)} %param.19) | copy-start | bytes 786436
  7.8 27.9 %all-to-all-start = ((bf16[8,144,256]{2,1,0:T(8,128)(2,1)}), bf16[8,144,256]{2,1,0:T(8,128)(2,1)S(1)}, u32[]{:S(2)}, u32[]{:S(2)}) async-start(bf16[8,144,256]{2,1,0:T(8,128)(2,1)} %constant_dynamic-update-slice_fusion), calls=%async_computation | async-start | bytes 1179648 | tf_op jit(solution)/shard_map/all_to_all | solution.py:52
  35.6 26.6 %all-to-all-start.2 = ((bf16[8,128,256]{2,1,0:T(8,128)(2,1)}), bf16[8,128,256]{2,1,0:T(8,128)(2,1)S(1)}, u32[]{:S(2)}, u32[]{:S(2)}) async-start(bf16[8,128,256]{2,1,0:T(8,128)(2,1)} %bitcast.24), calls=%async_computation.2 | async-start | bytes 1048576 | tf_op jit(solution)/shard_map/all_to_all | solution.py:62
  39.4 15.3 %collective-permute-start.1 = (bf16[8,18,256]{2,0,1:T(8,128)(2,1)S(1)}, bf16[8,18,256]{2,0,1:T(8,128)(2,1)S(1)}, u32[]{:S(2)}, u32[]{:S(2)}) collective-permute-start(bf16[8,18,256]{2,0,1:T(8,128)(2,1)S(1)} %get-tuple-element.8), channel_id=1, source_target_pairs={{1,0},{2,1},{3,2},{4,3},{5,4},{6,5},{7,6},{9,8},{10,9},{11,10},{12... | collective-permute-start | bytes 221192 | tf_op jit(solution)/shard_map/ppermute | solution.py:66
  40.7 14.0 %collective-permute-start = (bf16[8,18,256]{2,0,1:T(8,128)(2,1)S(1)}, bf16[8,18,256]{2,0,1:T(8,128)(2,1)S(1)}, u32[]{:S(2)}, u32[]{:S(2)}) collective-permute-start(bf16[8,18,256]{2,0,1:T(8,128)(2,1)S(1)} %get-tuple-element.7), channel_id=1, source_target_pairs={{0,1},{1,2},{2,3},{3,4},{4,5},{5,6},{6,7},{8,9},{9,10},{10,11},{11... | collective-permute-start | bytes 221192 | tf_op jit(solution)/shard_map/ppermute | solution.py:65
  56.2 1.8 %copy-start.6 = (bf16[8,8,16,256]{3,2,1,0:T(8,128)(2,1)}, bf16[8,8,16,256]{3,2,1,0:T(8,128)(2,1)S(1)}, u32[]{:S(2)}) copy-start(bf16[8,8,16,256]{3,2,1,0:T(8,128)(2,1)S(1)} %copy.97) | copy-start | bytes 1572868
  56.4 1.0 copy-start.11
  56.5 2.9 %copy-start.7 = (bf16[8,128,256]{2,1,0:T(8,128)(2,1)}, bf16[8,128,256]{2,1,0:T(8,128)(2,1)S(1)}, u32[]{:S(2)}) copy-start(bf16[8,128,256]{2,1,0:T(8,128)(2,1)S(1)} %pad.13) | copy-start | bytes 1572868
  57.4 1.2 copy-start.10
  58.0 1.5 copy-start.12
  58.6 1.0 copy-start.2
  59.4 1.1 copy-start.3
  60.4 1.5 copy-start.4
  62.2 19.4 %all-to-all-start.5 = ((bf16[8,32,512]{2,1,0:T(8,128)(2,1)}), bf16[8,32,512]{2,1,0:T(8,128)(2,1)}, u32[]{:S(2)}, u32[]{:S(2)}) async-start(bf16[8,32,512]{2,1,0:T(8,128)(2,1)} %copy_bitcast_fusion.2), calls=%async_computation.5 | async-start | bytes 524288 | tf_op jit(solution)/shard_map/all_to_all | solution.py:63
  72.9 1.6 %copy-start.9 = (f32[8,8,32]{2,1,0:T(8,128)S(1)}, f32[8,8,32]{2,1,0:T(8,128)}, u32[]{:S(2)}) copy-start(f32[8,8,32]{2,1,0:T(8,128)} %get-tuple-element.18) | copy-start | bytes 24580
  73.0 2.0 %copy-start.5 = (bf16[512,512]{1,0:T(8,128)(2,1)S(1)}, bf16[512,512]{1,0:T(8,128)(2,1)}, u32[]{:S(2)}) copy-start(bf16[512,512]{1,0:T(8,128)(2,1)} %param.18) | copy-start | bytes 1572868
  74.0 13.1 %collective-permute-start.2 = (f32[4,8,12,256]{3,1,2,0:T(8,128)}, f32[4,8,12,256]{3,1,2,0:T(8,128)}, u32[]{:S(2)}, u32[]{:S(2)}) collective-permute-start(f32[4,8,12,256]{3,1,2,0:T(8,128)} %bitcast.86), channel_id=1, source_target_pairs={{0,8},{8,0},{16,24},{24,16},{32,40},{40,32},{48,56},{56,48},{1,9},... | collective-permute-start | bytes 1179656 | tf_op jit(solution)/shard_map/ppermute | solution.py:22
  81.7 15.4 %all-to-all-start.1 = ((bf16[8,32,512]{2,1,0:T(8,128)(2,1)}), bf16[8,32,512]{2,1,0:T(8,128)(2,1)S(1)}, u32[]{:S(2)}, u32[]{:S(2)}) async-start(bf16[8,32,512]{2,1,0:T(8,128)(2,1)} %bitcast.18), calls=%async_computation.1 | async-start | bytes 524288 | tf_op jit(solution)/shard_map/all_to_all | solution.py:112
  86.6 16.4 %collective-permute-start.6 = (f32[4,8,8,512]{3,2,0,1:T(8,128)S(1)}, f32[4,8,8,512]{3,2,0,1:T(8,128)S(1)}, u32[]{:S(2)}, u32[]{:S(2)}) collective-permute-start(f32[4,8,8,512]{3,2,0,1:T(8,128)S(1)} %bitcast.109), channel_id=1, source_target_pairs={{0,8},{8,0},{16,24},{24,16},{32,40},{40,32},{48,56},{56,48},{1,9},... | collective-permute-start | bytes 1572872 | tf_op jit(solution)/shard_map/ppermute | solution.py:22
  97.0 12.9 %all-to-all-start.3 = ((bf16[8,4,12,256]{3,1,2,0:T(4,128)(2,1)}), bf16[8,4,12,256]{3,1,2,0:T(4,128)(2,1)S(1)}, u32[]{:S(2)}, u32[]{:S(2)}) async-start(bf16[8,4,12,256]{3,1,2,0:T(4,128)(2,1)} %copy.104), calls=%async_computation.3 | async-start | bytes 393216 | tf_op jit(solution)/shard_map/all_to_all | solution.py:24
  109.9 10.6 %all-to-all-start.6 = ((bf16[8,4,8,512]{3,2,1,0:T(8,128)(2,1)}), bf16[8,4,8,512]{3,2,1,0:T(8,128)(2,1)S(1)}, u32[]{:S(2)}, u32[]{:S(2)}) async-start(bf16[8,4,8,512]{3,2,1,0:T(8,128)(2,1)} %fusion.21), calls=%async_computation.6 | async-start | bytes 524288 | tf_op jit(solution)/shard_map/all_to_all | solution.py:24
  120.6 11.1 %all-to-all-start.4 = ((bf16[4,12,256]{2,1,0:T(8,128)(2,1)}), bf16[4,12,256]{2,1,0:T(8,128)(2,1)S(1)}, u32[]{:S(2)}, u32[]{:S(2)}) async-start(bf16[4,12,256]{2,1,0:T(8,128)(2,1)} %copy.105), calls=%async_computation.4 | async-start | bytes 65536 | tf_op jit(solution)/shard_map/all_to_all | solution.py:27
  131.7 11.1 %all-to-all-start.7 = ((bf16[4,8,512]{2,1,0:T(8,128)(2,1)}), bf16[4,8,512]{2,1,0:T(8,128)(2,1)S(1)}, u32[]{:S(2)}, u32[]{:S(2)}) async-start(bf16[4,8,512]{2,1,0:T(8,128)(2,1)} %reduce_sum.77), calls=%async_computation.7 | async-start | bytes 65536 | tf_op jit(solution)/shard_map/all_to_all | solution.py:27
  135.0 11.2 %collective-permute-start.5 = (f32[12,256]{1,0:T(8,128)S(1)}, f32[12,256]{1,0:T(8,128)S(1)}, u32[]{:S(2)}, u32[]{:S(2)}) collective-permute-start(f32[12,256]{1,0:T(8,128)S(1)} %convert_reduce_fusion.1), channel_id=1, source_target_pairs={{0,192},{64,0},{128,64},{192,128},{1,193},{65,1},{129,65},{193,129... | collective-permute-start | bytes 36872 | tf_op jit(solution)/shard_map/ppermute | solution.py:30
  135.6 10.6 %collective-permute-start.4 = (f32[12,256]{1,0:T(8,128)S(1)}, f32[12,256]{1,0:T(8,128)S(1)}, u32[]{:S(2)}, u32[]{:S(2)}) collective-permute-start(f32[12,256]{1,0:T(8,128)S(1)} %convert_reduce_fusion.1), channel_id=1, source_target_pairs={{0,128},{64,192},{128,0},{192,64},{1,129},{65,193},{129,1},{193,65... | collective-permute-start | bytes 36872 | tf_op jit(solution)/shard_map/ppermute | solution.py:30
  138.3 7.8 %collective-permute-start.3 = (f32[12,256]{1,0:T(8,128)S(1)}, f32[12,256]{1,0:T(8,128)S(1)}, u32[]{:S(2)}, u32[]{:S(2)}) collective-permute-start(f32[12,256]{1,0:T(8,128)S(1)} %convert_reduce_fusion.1), channel_id=1, source_target_pairs={{0,64},{64,128},{128,192},{192,0},{1,65},{65,129},{129,193},{193,1... | collective-permute-start | bytes 36872 | tf_op jit(solution)/shard_map/ppermute | solution.py:30
  142.8 4.0 %collective-permute-start.9 = (f32[8,512]{1,0:T(8,128)S(1)}, f32[8,512]{1,0:T(8,128)S(1)}, u32[]{:S(2)}, u32[]{:S(2)}) collective-permute-start(f32[8,512]{1,0:T(8,128)S(1)} %convert_reduce_fusion), channel_id=1, source_target_pairs={{0,192},{64,0},{128,64},{192,128},{1,193},{65,1},{129,65},{193,129... | collective-permute-start | bytes 49160 | tf_op jit(solution)/shard_map/ppermute | solution.py:30
  143.4 5.2 %collective-permute-start.8 = (f32[8,512]{1,0:T(8,128)S(1)}, f32[8,512]{1,0:T(8,128)S(1)}, u32[]{:S(2)}, u32[]{:S(2)}) collective-permute-start(f32[8,512]{1,0:T(8,128)S(1)} %convert_reduce_fusion), channel_id=1, source_target_pairs={{0,128},{64,192},{128,0},{192,64},{1,129},{65,193},{129,1},{193,65... | collective-permute-start | bytes 49160 | tf_op jit(solution)/shard_map/ppermute | solution.py:30
  146.1 3.7 %collective-permute-start.7 = (f32[8,512]{1,0:T(8,128)S(1)}, f32[8,512]{1,0:T(8,128)S(1)}, u32[]{:S(2)}, u32[]{:S(2)}) collective-permute-start(f32[8,512]{1,0:T(8,128)S(1)} %convert_reduce_fusion), channel_id=1, source_target_pairs={{0,64},{64,128},{128,192},{192,0},{1,65},{65,129},{129,193},{193,1... | collective-permute-start | bytes 49160 | tf_op jit(solution)/shard_map/ppermute | solution.py:30

commit v2 on v1

v2 whole, which is shorter than its diff:
```python
import functools
import math

import jax
import jax.numpy as jnp
import numpy as np
from jax import lax
from jax.experimental import pallas as pl
from jax.experimental.pallas import tpu as pltpu
from jax.sharding import PartitionSpec as P

F32 = jnp.float32
BF16 = jnp.bfloat16
NEG = -1e30


def call(body, out_shape, args, any_args=(), scratch=(), name=None):
    specs = [
        pl.BlockSpec(memory_space=pl.ANY if i in any_args else pltpu.VMEM)
        for i in range(len(args))
    ]
    outs = [pl.BlockSpec(memory_space=pltpu.VMEM) for _ in out_shape]
    return pl.pallas_call(
        body,
        out_shape=out_shape,
        in_specs=specs,
        out_specs=outs,
        scratch_shapes=list(scratch),
        compiler_params=pltpu.CompilerParams(vmem_limit_bytes=48 << 20),
        name=name,
    )(*args)


def place():
    index = lax.axis_index("tm")
    return index // 2, index % 2


def edge_picker(count, cols, strip):
    strips = cols // strip
    pick = np.zeros((strips, 2 * 8, count * cols), np.float32)
    for j in range(strips):
        for r in range(count):
            if j > 0:
                pick[j, r, r * cols + j * strip - 1] = 1
            if j < strips - 1:
                pick[j, count + r, r * cols + (j + 1) * strip] = 1
    return jnp.asarray(pick.reshape(strips * 16, count * cols), BF16)


def pack_cells_body(own, partner, pick, *refs, links):
    outs, edges = refs[:links], refs[links]
    zhi, core = place()
    count, cols, chan = own.shape
    strip = cols // (2 * links)
    for s, source in enumerate((own, partner)):
        flat = source[...].reshape(count * cols, chan)
        found = jnp.dot(pick[...], flat, preferred_element_type=F32).astype(BF16)
        edges[...] = found.reshape(2 * links, 16, chan)
        for k in range(links):
            j = 2 * lax.rem(zhi + k, links) + core
            begin = pl.multiple_of(j * strip, strip)
            piece = source[:, pl.ds(begin, strip), :].reshape(count * strip, chan)
            outs[k][s, : count * strip] = piece
            outs[k][s, count * strip :] = edges[j]


def pack_cells(own, partner, links):
    count, cols, chan = own.shape
    strip = cols // (2 * links)
    pick = edge_picker(count, cols, strip)
    shape = jax.ShapeDtypeStruct((2, count * strip + 16, chan), BF16)
    return call(
        functools.partial(pack_cells_body, links=links),
        [shape] * links,
        (own, partner, pick),
        scratch=[pltpu.VMEM((2 * links, 16, chan), BF16)],
        name="pack_cells",
    )


def pack_teacher_body(own_mid, partner_mid, own_top, partner_top, *outs, links):
    zhi, core = place()
    rows, cols, chan = own_mid.shape
    half_rows, half_cols, width = own_top.shape
    strip = cols // (2 * links)
    half = half_cols // (2 * links)
    base = rows * strip
    points = half_rows * half
    for k in range(links):
        dest = lax.rem(zhi + k, links)
        j = 2 * dest + core
        for s, (mid, top) in enumerate(((own_mid, own_top), (partner_mid, partner_top))):
            begin = pl.multiple_of(j * strip, strip)
            outs[k][s, :base] = mid[:, pl.ds(begin, strip), :].reshape(base, chan)
            begin = pl.multiple_of(dest * 2 * half, 2 * half)
            both = top[:, pl.ds(begin, 2 * half), :].astype(F32)
            mine = jnp.where(core == 0, both[:, :half], both[:, half:])
            mine = mine.reshape(points, width)
            outs[k][s, base : base + points] = mine[:, :chan].astype(BF16)
            outs[k][s, base + points :] = mine[:, chan:].astype(BF16)


def pack_teacher(own_mid, partner_mid, own_top, partner_top, links):
    rows, cols, chan = own_mid.shape
    half_rows, half_cols, width = own_top.shape
    points = half_rows * (half_cols // (2 * links))
    height = rows * (cols // (2 * links)) + points * (width // chan)
    shape = jax.ShapeDtypeStruct((2, height, chan), BF16)
    return call(
        functools.partial(pack_teacher_body, links=links),
        [shape] * links,
        (own_mid, partner_mid, own_top, partner_top),
        name="pack_teacher",
    )


def shift_pickers(rows, strip):
    main = rows * strip
    left = np.zeros((rows + 2, strip, main + 16 + 2 * strip + 16), np.float32)
    right = np.zeros_like(left)
    halo = main + 16
    corner = halo + 2 * strip
    for q in range(rows + 2):
        if q == 0:
            cell, l_edge, r_edge = halo, corner, corner + 2
        elif q == rows + 1:
            cell, l_edge, r_edge = halo + strip, corner + 1, corner + 3
        else:
            cell, l_edge, r_edge = (q - 1) * strip, main + q - 1, main + rows + q - 1
        for c in range(strip):
            left[q, c, cell + c - 1 if c > 0 else l_edge] = 1
            right[q, c, cell + c + 1 if c < strip - 1 else r_edge] = 1
    both = np.concatenate([left, right], 0).reshape(2 * (rows + 2) * strip, -1)
    return jnp.asarray(both, BF16)


def parity_picker(frames, strip):
    half = strip // 2
    pick = np.zeros((2, frames, half, frames, strip), np.float32)
    for b in range(2):
        for t in range(frames):
            for c in range(half):
                pick[b, t, c, t, 2 * c + b] = 1
    return jnp.asarray(pick.reshape(frames * strip, frames * strip), BF16)


def encode_body(*refs, links, rows, strip):
    cells, refs = refs[:links], refs[links:]
    halos, refs = refs[:links], refs[links:]
    shifts, parity, w_spatial, w_temporal_h, w_down_h, w_proj_h, refs = (*refs[:6], refs[6:])
    spatial, mid_out, attended_out, student_out, refs = (*refs[:4], refs[4:])
    pieces, refs = refs[:links], refs[links:]
    grid, cat, patch, top, w_temporal, w_down, w_proj, sems = refs
    copies = [
        pltpu.make_async_copy(w_temporal_h, w_temporal, sems.at[0]),
        pltpu.make_async_copy(w_down_h, w_down, sems.at[1]),
        pltpu.make_async_copy(w_proj_h, w_proj, sems.at[2]),
    ]
    for copy in copies:
        copy.start()
    zhi, core = place()
    frames = 2 * links
    chan = spatial.shape[-1]
    width = attended_out.shape[-1]
    main = rows * strip
    tall = (rows + 2) * strip
    for k in range(links):
        origin = lax.rem(zhi - k + links, links)
        for s in range(2):
            t = 2 * origin + (core if s == 0 else 1 - core)
            cat[: main + 16] = cells[k][s]
            cat[main + 16 :] = halos[k][s]
            moved = jnp.dot(shifts[...], cat[...], preferred_element_type=F32).astype(BF16)
            grid[:, t, :, :chan] = moved[:tall].reshape(rows + 2, strip, chan)
            grid[:, t, :, 2 * chan :] = moved[tall:].reshape(rows + 2, strip, chan)
            grid[0, t, :, chan : 2 * chan] = halos[k][s, :strip]
            grid[1 : rows + 1, t, :, chan : 2 * chan] = cells[k][s, :main].reshape(
                rows, strip, chan
            )
            grid[rows + 1, t, :, chan : 2 * chan] = halos[k][s, strip : 2 * strip]
    cellcount = rows * frames * strip
    conv = jnp.dot(
        grid[:rows].reshape(cellcount, 3 * chan), w_spatial[0], preferred_element_type=F32
    )
    for d in range(1, 3):
        conv = conv + jnp.dot(
            grid[d : rows + d].reshape(cellcount, 3 * chan),
            w_spatial[d],
            preferred_element_type=F32,
        )
    conv = conv / (1.0 + jnp.exp(-conv))
    spatial[:, :2] = jnp.zeros((rows, 2, strip, chan), BF16)
    spatial[:, 2:] = conv.astype(BF16).reshape(rows, frames, strip, chan)
    copies[0].wait()
    acc = grid[1 : rows + 1, :, :, chan : 2 * chan].reshape(cellcount, chan).astype(F32)
    temporal = jnp.dot(
        spatial[:, :frames].reshape(cellcount, chan),
        w_temporal[:chan],
        preferred_element_type=F32,
    )
    for m in range(1, 3):
        temporal = temporal + jnp.dot(
            spatial[:, m : m + frames].reshape(cellcount, chan),
            w_temporal[m * chan : (m + 1) * chan],
            preferred_element_type=F32,
        )
    mid_out[...] = (acc + temporal).astype(BF16)
    line = frames * strip
    half = strip // 2
    for r in range(rows):
        both = jnp.dot(
            parity[...], mid_out[r * line : (r + 1) * line], preferred_element_type=F32
        ).astype(BF16)
        i, a = r // 2, r % 2
        span = slice(i * line // 2, (i + 1) * line // 2)
        patch[span, 2 * a * chan : (2 * a + 1) * chan] = both[: line // 2]
        patch[span, (2 * a + 1) * chan : (2 * a + 2) * chan] = both[line // 2 :]
    copies[1].wait()
    coarse = jnp.dot(patch[...], w_down[...], preferred_element_type=F32).astype(BF16)
    copies[2].wait()
    half_rows = rows // 2
    quads = (half_rows, frames, half, width)
    query = jnp.dot(coarse, w_proj[0], preferred_element_type=F32).astype(BF16)
    key = jnp.dot(coarse, w_proj[1], preferred_element_type=F32).astype(BF16)
    value = jnp.dot(coarse, w_proj[2], preferred_element_type=F32).astype(BF16)
    top[0] = query.astype(F32).reshape(quads)
    top[1] = key.astype(F32).reshape(quads)
    top[2] = value.astype(F32).reshape(quads)
    scale = 1.0 / math.sqrt(width)

    def attend(i, carry):
        for t in range(frames):
            q = top[0, i, t]
            scores = [
                jnp.sum(q * top[1, i, s], -1, keepdims=True) * scale for s in range(t + 1)
            ]
            best = functools.reduce(jnp.maximum, scores)
            weights = [jnp.exp(score - best) for score in scores]
            total = functools.reduce(jnp.add, weights)
            mix = functools.reduce(
                jnp.add, [weights[s] * top[2, i, s] for s in range(t + 1)]
            )
            top[3, i, t] = mix / total
        return carry

    lax.fori_loop(0, half_rows, attend, 0)
    attended = top[3].reshape(half_rows * frames * half, width).astype(BF16)
    attended_out[...] = attended
    out = jnp.dot(attended, w_proj[3], preferred_element_type=F32)
    student = (coarse.astype(F32) + out).astype(BF16)
    student_out[...] = student
    top[0] = student.astype(F32).reshape(quads)
    for k in range(links):
        dest = lax.rem(zhi + k, links)
        for s in range(2):
            t = 2 * dest + (core if s == 0 else 1 - core)
            pieces[k][s] = top[0, :, t].reshape(half_rows * half, width).astype(BF16)


def encode(cells, halos, w_spatial, w_temporal, w_down, w_proj, links, rows, strip):
    frames = 2 * links
    chan = w_temporal.shape[1]
    width = w_down.shape[-1]
    half = strip // 2
    points = (rows // 2) * half
    args = (
        *cells,
        *halos,
        shift_pickers(rows, strip),
        parity_picker(frames, strip),
        w_spatial.reshape(3, 3 * chan, chan),
        w_temporal,
        w_down.reshape(4 * chan, width),
        w_proj,
    )
    first = 2 * links + 3
    shapes = [
        jax.ShapeDtypeStruct((rows, frames + 2, strip, chan), BF16),
        jax.ShapeDtypeStruct((rows * frames * strip, chan), BF16),
        jax.ShapeDtypeStruct((frames * points, width), BF16),
        jax.ShapeDtypeStruct((frames * points, width), BF16),
    ] + [jax.ShapeDtypeStruct((2, points, width), BF16)] * links
    scratch = [
        pltpu.VMEM((rows + 2, frames, strip, 3 * chan), BF16),
        pltpu.VMEM((rows * strip + 16 + 2 * strip + 16, chan), BF16),
        pltpu.VMEM((frames * points, 4 * chan), BF16),
        pltpu.VMEM((4, rows // 2, frames, half, width), F32),
        pltpu.VMEM(w_temporal.shape, BF16),
        pltpu.VMEM((4 * chan, width), BF16),
        pltpu.VMEM((4, width, width), BF16),
        pltpu.SemaphoreType.DMA((3,)),
    ]
    outs = call(
        functools.partial(encode_body, links=links, rows=rows, strip=strip),
        shapes,
        args,
        any_args=(first, first + 1, first + 2),
        scratch=scratch,
        name="encode",
    )
    return outs[:4], outs[4:]


def gradients_body(*refs, links, scale_mid, scale_top):
    teachers, refs = refs[:links], refs[links:]
    spatial, mid, attended, student, keep, give, t_mid, t_top, g_mid, g_top = refs
    zhi, core = place()
    rows, padded, strip, chan = spatial.shape
    frames = padded - 2
    half_rows, _, half, width = t_top.shape
    base = rows * strip
    points = half_rows * half
    for k in range(links):
        origin = lax.rem(zhi - k + links, links)
        for s in range(2):
            t = 2 * origin + (core if s == 0 else 1 - core)
            t_mid[:, t] = teachers[k][s, :base].reshape(rows, strip, chan)
            low = teachers[k][s, base : base + points].astype(F32)
            high = teachers[k][s, base + points :].astype(F32)
            t_top[:, t, :, :chan] = low.reshape(half_rows, half, chan)
            t_top[:, t, :, chan:] = high.reshape(half_rows, half, chan)
    count = rows * frames * strip
    diff = (mid[...].astype(F32) - t_mid[...].reshape(count, chan).astype(F32)).astype(BF16)
    dims = (((0,), (0,)), ((), ()))
    for m in range(3):
        g_mid[m * chan : (m + 1) * chan] = (
            lax.dot_general(
                spatial[:, m : m + frames].reshape(count, chan),
                diff,
                dims,
                preferred_element_type=F32,
            )
            * scale_mid
        )
    diff = (
        student[...].astype(F32) - t_top[...].reshape(frames * points, width)
    ).astype(BF16)
    g_top[...] = lax.dot_general(attended[...], diff, dims, preferred_element_type=F32) * scale_top
    spaces = keep.shape[1]
    n_mid = g_mid.shape[0] // (frames * spaces)
    n_top = g_top.shape[0] // (frames * spaces)
    for c in range(2):

        @pl.when(core == c)
        def _():
            for side, ref in ((c, keep), (1 - c, give)):
                for z in range(links):
                    for p in range(spaces):
                        shard = (2 * z + side) * spaces + p
                        ref[z, p, :n_mid] = g_mid[shard * n_mid : (shard + 1) * n_mid].astype(
                            ref.dtype
                        )
                        ref[z, p, n_mid:16] = jnp.zeros((16 - n_mid, chan), ref.dtype)
                        block = g_top[shard * n_top : (shard + 1) * n_top].astype(ref.dtype)
                        ref[z, p, 16 : 16 + n_top] = block[:, :chan]
                        ref[z, p, 16 + n_top :] = block[:, chan:]


def gradients(teachers, spatial, mid, attended, student, links, spaces, scale_mid, scale_top):
    rows, padded, strip, chan = spatial.shape
    frames = padded - 2
    width = attended.shape[-1]
    height = 16 + (width // (frames * spaces)) * (width // chan)
    return call(
        functools.partial(
            gradients_body, links=links, scale_mid=scale_mid, scale_top=scale_top
        ),
        [
            jax.ShapeDtypeStruct((links, spaces, height, chan), F32),
            jax.ShapeDtypeStruct((links, spaces, height, chan), F32),
        ],
        (*teachers, spatial, mid, attended, student),
        scratch=[
            pltpu.VMEM((rows, frames, strip, chan), BF16),
            pltpu.VMEM((rows // 2, frames, strip // 2, width), F32),
            pltpu.VMEM((3 * chan, chan), F32),
            pltpu.VMEM((width, width), F32),
        ],
        name="gradients",
    )


def unpack_body(*refs, links):
    mine, swapped, out = refs[:links], refs[links], refs[links + 1]
    zhi, core = place()
    half_rows, cols, width = out.shape
    half = cols // (2 * links)
    for k in range(links):
        origin = lax.rem(zhi - k + links, links)
        own = mine[k][0].astype(F32).reshape(half_rows, half, width)
        other = swapped[k].astype(F32).reshape(half_rows, half, width)
        first = jnp.where(core == 0, own, other)
        second = jnp.where(core == 0, other, own)
        begin = pl.multiple_of(origin * 2 * half, 2 * half)
        out[:, pl.ds(begin, 2 * half), :] = jnp.concatenate([first, second], 1).astype(BF16)


def local(
    feats, w_spatial, w_temporal, teacher_mid, w_down, w_query, w_key, w_value, w_out, teacher_top
):
    frames = lax.axis_size("tm")
    spaces = lax.axis_size("space")
    clips = lax.axis_size("dp")
    links = frames // 2
    devices_all = clips * frames * spaces
    own = feats[0, 0]
    rows, cols, chan = own.shape
    strip = cols // frames
    half_rows, half_cols, width = teacher_top.shape[2:]
    points = half_rows * (half_cols // frames)

    def swap(block):
        return lax.ppermute(block, "tm", [(i, i ^ 1) for i in range(frames)])

    def spread(pieces):
        return [pieces[0]] + [
            lax.ppermute(pieces[k], "tm", [(i, (i + 2 * k) % frames) for i in range(frames)])
            for k in range(1, links)
        ]

    above = lax.ppermute(own[rows - 1], "space", [(i, i + 1) for i in range(spaces - 1)])
    below = lax.ppermute(own[0], "space", [(i + 1, i) for i in range(spaces - 1)])
    cells = spread(pack_cells(own, swap(own), links))
    halo = jnp.stack([above, below])
    halos = spread(pack_cells(halo, swap(halo), links))
    t_mid, t_top = teacher_mid[0, 0], teacher_top[0, 0]
    teachers = spread(pack_teacher(t_mid, swap(t_mid), t_top, swap(t_top), links))

    w_proj = jnp.stack([w_query, w_key, w_value, w_out])
    saved, pieces = encode(
        cells, halos, w_spatial, w_temporal, w_down, w_proj, links, rows, strip
    )
    returned = spread(pieces)
    swapped = swap(jnp.stack([piece[1] for piece in returned]))
    home = call(
        functools.partial(unpack_body, links=links),
        [jax.ShapeDtypeStruct((half_rows, half_cols, width), BF16)],
        (*returned, swapped),
        name="unpack",
    )[0]

    keep, give = gradients(
        teachers,
        *saved,
        links,
        spaces,
        1.0 / math.sqrt(rows * cols * devices_all),
        1.0 / math.sqrt(points * frames * devices_all),
    )
    part = (keep + swap(give)).astype(BF16)
    height = part.shape[2]
    part = part.reshape(links * spaces, height, chan)
    groups = [
        [(2 * z + c) * spaces + p for z in range(links) for p in range(spaces)] for c in range(2)
    ]
    part = lax.all_to_all(
        part, ("tm", "space"), 0, 0, axis_index_groups=groups, tiled=True
    )
    part = jnp.sum(part.astype(F32), 0)
    others = [
        lax.ppermute(part, "dp", [(i, (i + k) % clips) for i in range(clips)])
        for k in range(1, clips)
    ]
    for other in others:
        part = part + other
    n_top = width // (frames * spaces)
    grad_temporal = part[: 3 * chan // (frames * spaces)]
    grad_out = jnp.concatenate([part[16 : 16 + n_top], part[16 + n_top :]], 1)
    return (home[None, None], grad_temporal, grad_out)


def solution(mesh):
    return jax.shard_map(
        local,
        mesh=mesh,
        in_specs=(
            P("dp", "tm", "space", None, None),
            P(),
            P(),
            P("dp", "tm", "space", None, None),
            P(),
            P(),
            P(),
            P(),
            P(),
            P("dp", "tm", "space", None, None),
        ),
        out_specs=(
            P("dp", "tm", "space", None, None),
            P(("tm", "space"), None),
            P(("tm", "space"), None),
        ),
        check_vma=False,
    )
```

time: 152 us -> 118 us (0.78)
  waiting for transfers between devices: 67.1 us -> 42.2 us
  local copies, waits for them, and re-layouts: 16.5 us -> 5.32 us
  Pallas kernels: 0 us -> 9.69 us
  matrix products: 8.82 us -> 0 us
  starting transfers between devices: 51.4 us -> 53.3 us
    all_to_all x8 -> x1, waiting for transfers between devices: 55 us -> 0.01 us  [local(): lax.all_to_all(part, ('tm', 'space'), 0, 0, axis_index_groups=groups, til...]
    ppermute x10 -> x23, starting transfers between devices: 13.5 us -> 45.4 us  [the longest x12 35.2 us: spread(): lax.ppermute(pieces[k], 'tm', [(i, (i + 2 * k) % frames) for i in range(f...]
    ppermute x10 -> x23, waiting for transfers between devices: 12.1 us -> 42.2 us  [the longest x12 34.6 us: spread(): lax.ppermute(pieces[k], 'tm', [(i, (i + 2 * k) % frames) for i in range(f...]
    all_to_all x8 -> x1, starting transfers between devices: 37.9 us -> 7.89 us  [local(): lax.all_to_all(part, ('tm', 'space'), 0, 0, axis_index_groups=groups, til...]
    pallas_call x0 -> x6, Pallas kernels: none -> 9.69 us  [call(): pl.pallas_call(body, out_shape=out_shape, in_specs=specs, out_specs=outs,...]
    dot_general x7 -> x0, matrix products: 6.69 us -> none  [the longest x1 2.85 us: local(): lax.dot_general(stacked, diff_mid, (((0,), (0,)), ((), ())), preferred_el...]
    another operation x0 -> x3, other arithmetic: none -> 3 us  [the longest x1 2.97 us: local(): w_proj = jnp.stack([w_query, w_key, w_value, w_out])]
    unnamed x33 -> x24, local copies, waits for them, and re-layouts: 6.62 us -> 3.82 us
  transfers between devices with their start and end apart: 18 -> 24, of which waited for: 10 -> 9; matrix products, arithmetic and copies ran while one was open for 14% -> 3% of each run, Pallas kernels for 0% -> 8%
where the time goes in v2:
time: 118 us; the launch traced here: 116 us
  starting transfers between devices  53.3 us (45%)
  waiting for transfers between devices  42.2 us (36%)
  Pallas kernels  9.69 us (8%)
  local copies, waits for them, and re-layouts  5.32 us (5%)
  other arithmetic  4.65 us (4%)
    ppermute x12, starting transfers between devices, spread(): lax.ppermute(pieces[k], 'tm', [(i, (i + 2 * k) % frames) for i in range(f...  35.2 us
    ppermute x12, waiting for transfers between devices, spread(): lax.ppermute(pieces[k], 'tm', [(i, (i + 2 * k) % frames) for i in range(f...  34.6 us
    pallas_call x6, Pallas kernels, call(): pl.pallas_call(body, out_shape=out_shape, in_specs=specs, out_specs=outs,...  9.69 us
    all_to_all x1, starting transfers between devices, local(): lax.all_to_all(part, ('tm', 'space'), 0, 0, axis_index_groups=groups, til...  7.89 us
    ppermute x1, starting transfers between devices, local(): lax.ppermute(own[rows - 1], 'space', [(i, i + 1) for i in range(spaces -...  4.55 us
    unnamed x24, local copies, waits for them, and re-layouts  3.82 us
    ppermute x3, starting transfers between devices, local(): lax.ppermute(part, 'dp', [(i, (i + k) % clips) for i in range(clips)])  3.36 us
    ppermute x3, waiting for transfers between devices, local(): lax.ppermute(part, 'dp', [(i, (i + k) % clips) for i in range(clips)])  3.13 us
  transfers between devices with their start and end apart: 24, of which 9 were waited for; matrix products, arithmetic and copies ran while one was open for 3% of the time, Pallas kernels for 8%

profile of v2, /device:TPU:4, one launch (start us, length us, event | category | flops | bytes accessed | tf_op | source)
XLA Modules:
  0.0 116.0 jit_solution(479462765087913707)
XLA Ops:
  0.6 0.1 collective-permute-start
  0.7 0.5 collective-permute-start.14
  1.2 0.9 slice_bitcast_fusion.1
  2.1 1.3 %collective-permute-start.5 = (bf16[128,256]{1,0:T(8,128)(2,1)S(1)}, bf16[128,256]{1,0:T(8,128)(2,1)S(1)}, u32[]{:S(2)}, u32[]{:S(2)}) collective-permute-start(bf16[128,256]{1,0:T(8,128)(2,1)S(1)} %get-tuple-element.48), channel_id=1, source_target_pairs={{1,0},{2,1},{3,2},{4,3},{5,4},{6,5},{7,6},{9,8},{10,9},{11,10},{12... | collective-permute-start | bytes 196616 | tf_op jit(solution)/shard_map/ppermute | solution.py:423
  3.4 4.5 %collective-permute-start.4 = (bf16[128,256]{1,0:T(8,128)(2,1)S(1)}, bf16[128,256]{1,0:T(8,128)(2,1)S(1)}, u32[]{:S(2)}, u32[]{:S(2)}) collective-permute-start(bf16[128,256]{1,0:T(8,128)(2,1)S(1)} %get-tuple-element.47), channel_id=1, source_target_pairs={{0,1},{1,2},{2,3},{3,4},{4,5},{5,6},{6,7},{8,9},{9,10},{10,11},{11... | collective-permute-start | bytes 196616 | tf_op jit(solution)/shard_map/ppermute | solution.py:422
  8.0 0.1 collective-permute-start.15
  8.1 0.2 collective-permute-done.5
  8.3 1.6 %collective-permute-done.4 = bf16[128,256]{1,0:T(8,128)(2,1)S(1)} collective-permute-done((bf16[128,256]{1,0:T(8,128)(2,1)S(1)}, bf16[128,256]{1,0:T(8,128)(2,1)S(1)}, u32[]{:S(2)}, u32[]{:S(2)}) %collective-permute-start.4) | collective-permute-done | bytes 65568 | tf_op jit(solution)/shard_map/ppermute | solution.py:422
  9.9 0.1 collective-permute-start.6
  10.0 0.0 collective-permute-done.partner
  10.0 0.0 copy-start.2
  10.0 1.0 copy-done.2
  11.0 0.9 copy-done.5
  12.0 0.3 pack_cells.2
  12.3 3.3 %collective-permute-start.1 = (bf16[2,144,256]{2,1,0:T(8,128)(2,1)S(1)}, bf16[2,144,256]{2,1,0:T(8,128)(2,1)S(1)}, u32[]{:S(2)}, u32[]{:S(2)}) collective-permute-start(bf16[2,144,256]{2,1,0:T(8,128)(2,1)S(1)} %get-tuple-element.26), channel_id=1, source_target_pairs={{0,16},{8,24},{16,32},{24,40},{32,48},{40,56},{48,0},{56,8},{1,17}... | collective-permute-start | bytes 442376 | tf_op jit(solution)/shard_map/ppermute | solution.py:418
  15.7 0.0 collective-permute-done.6.partner
  15.7 0.8 copy-done.8
  16.5 0.2 pack_cells.3
  16.7 4.6 %collective-permute-start.7 = (bf16[2,48,256]{2,1,0:T(8,128)(2,1)S(1)}, bf16[2,48,256]{2,1,0:T(8,128)(2,1)S(1)}, u32[]{:S(2)}, u32[]{:S(2)}) collective-permute-start(bf16[2,48,256]{2,1,0:T(8,128)(2,1)S(1)} %get-tuple-element.30), channel_id=1, source_target_pairs={{0,16},{8,24},{16,32},{24,40},{32,48},{40,56},{48,0},{56,8},{1,17}... | collective-permute-start | bytes 147464 | tf_op jit(solution)/shard_map/ppermute | solution.py:418
  21.3 1.0 collective-permute-start.8
  22.3 0.0 collective-permute-done.15.partner_top
  22.3 4.0 %collective-permute-start.9 = (bf16[2,48,256]{2,1,0:T(8,128)(2,1)S(1)}, bf16[2,48,256]{2,1,0:T(8,128)(2,1)S(1)}, u32[]{:S(2)}, u32[]{:S(2)}) collective-permute-start(bf16[2,48,256]{2,1,0:T(8,128)(2,1)S(1)} %get-tuple-element.32), channel_id=1, source_target_pairs={{0,48},{8,56},{16,0},{24,8},{32,16},{40,24},{48,32},{56,40},{1,49}... | collective-permute-start | bytes 147464 | tf_op jit(solution)/shard_map/ppermute | solution.py:418
  26.3 0.0 collective-permute-done.14.partner_mid
  26.3 0.9 copy-done.6
  27.3 0.1 pack_teacher.1
  27.4 0.1 collective-permute-start.16
  27.5 0.0 collective-permute-done.7.refs_5_
  27.5 6.9 %collective-permute-start.17 = (bf16[2,192,256]{2,1,0:T(8,128)(2,1)S(1)}, bf16[2,192,256]{2,1,0:T(8,128)(2,1)S(1)}, u32[]{:S(2)}, u32[]{:S(2)}) collective-permute-start(bf16[2,192,256]{2,1,0:T(8,128)(2,1)S(1)} %get-tuple-element.39), channel_id=1, source_target_pairs={{0,32},{8,40},{16,48},{24,56},{32,0},{40,8},{48,16},{56,24},{1,33}... | collective-permute-start | bytes 589832 | tf_op jit(solution)/shard_map/ppermute | solution.py:418
  34.4 0.0 collective-permute-done.8.refs_6_
  34.4 2.0 %collective-permute-start.18 = (bf16[2,192,256]{2,1,0:T(8,128)(2,1)S(1)}, bf16[2,192,256]{2,1,0:T(8,128)(2,1)S(1)}, u32[]{:S(2)}, u32[]{:S(2)}) collective-permute-start(bf16[2,192,256]{2,1,0:T(8,128)(2,1)S(1)} %get-tuple-element.40), channel_id=1, source_target_pairs={{0,48},{8,56},{16,0},{24,8},{32,16},{40,24},{48,32},{56,40},{1,49}... | collective-permute-start | bytes 589832 | tf_op jit(solution)/shard_map/ppermute | solution.py:418
  36.4 0.0 collective-permute-done.9.refs_7_
  36.4 1.5 %collective-permute-start.2 = (bf16[2,144,256]{2,1,0:T(8,128)(2,1)S(1)}, bf16[2,144,256]{2,1,0:T(8,128)(2,1)S(1)}, u32[]{:S(2)}, u32[]{:S(2)}) collective-permute-start(bf16[2,144,256]{2,1,0:T(8,128)(2,1)S(1)} %get-tuple-element.27), channel_id=1, source_target_pairs={{0,32},{8,40},{16,48},{24,56},{32,0},{40,8},{48,16},{56,24},{1,33}... | collective-permute-start | bytes 442376 | tf_op jit(solution)/shard_map/ppermute | solution.py:418
  37.8 0.0 collective-permute-done.1.refs_1_
  37.8 3.1 %collective-permute-start.3 = (bf16[2,144,256]{2,1,0:T(8,128)(2,1)S(1)}, bf16[2,144,256]{2,1,0:T(8,128)(2,1)S(1)}, u32[]{:S(2)}, u32[]{:S(2)}) collective-permute-start(bf16[2,144,256]{2,1,0:T(8,128)(2,1)S(1)} %get-tuple-element.28), channel_id=1, source_target_pairs={{0,48},{8,56},{16,0},{24,8},{32,16},{40,24},{48,32},{56,40},{1,49}... | collective-permute-start | bytes 442376 | tf_op jit(solution)/shard_map/ppermute | solution.py:418
  40.9 0.0 copy-start.4
  40.9 0.0 copy-start.7
  40.9 0.0 copy-start.9
  41.0 3.0 %pad_maximum_fusion.refs_13_ = bf16[4,512,512]{2,1,0:T(8,128)(2,1)} fusion(bf16[1,512,512]{2,1,0:T(8,128)(2,1)S(1)} %bitcast.25, bf16[1,512,512]{2,1,0:T(8,128)(2,1)S(1)} %bitcast.26, bf16[1,512,512]{2,1,0:T(8,128)(2,1)} %bitcast.27, bf16[1,512,512]{2,1,0:T(8,128)(2,1)} %bitcast.28), kind=kLoop, calls=%fused_computation | loop fusion | flops 3145728 | bytes 4194304 | tf_op jit(solution)/shard_map/stack | solution.py:430
  43.9 2.9 %collective-permute-done.2.refs_2_ = bf16[2,144,256]{2,1,0:T(8,128)(2,1)S(1)} collective-permute-done((bf16[2,144,256]{2,1,0:T(8,128)(2,1)S(1)}, bf16[2,144,256]{2,1,0:T(8,128)(2,1)S(1)}, u32[]{:S(2)}, u32[]{:S(2)}) %collective-permute-start.2) | collective-permute-done | bytes 147488 | tf_op jit(solution)/shard_map/ppermute | solution.py:418
  46.9 18.3 %collective-permute-done.3.refs_3_ = bf16[2,144,256]{2,1,0:T(8,128)(2,1)S(1)} collective-permute-done((bf16[2,144,256]{2,1,0:T(8,128)(2,1)S(1)}, bf16[2,144,256]{2,1,0:T(8,128)(2,1)S(1)}, u32[]{:S(2)}, u32[]{:S(2)}) %collective-permute-start.3) | collective-permute-done | bytes 147488 | tf_op jit(solution)/shard_map/ppermute | solution.py:418
  65.2 7.4 %encode.1 = (bf16[8,10,16,256]{3,2,1,0:T(8,128)(2,1)S(1)}, bf16[1024,256]{1,0:T(8,128)(2,1)S(1)}, bf16[256,512]{1,0:T(8,128)(2,1)S(1)}, bf16[256,512]{1,0:T(8,12...) custom-call(bf16[2,144,256]{2,1,0:T(8,128)(2,1)S(1)} %get-tuple-elem, ...), custom_call_target="tpu_custom_call" | custom-call | tf_op jit(solution)/shard_map/encode/pallas_call | solution.py:23
  72.6 0.0 collective-permute-done.16.refs_1_
  72.6 0.0 collective-permute-done.17.refs_2_
  72.6 1.0 gradients.1
  73.6 0.1 collective-permute-start.19
  73.7 2.6 %collective-permute-done.19 = f32[4,8,32,256]{3,2,1,0:T(8,128)S(1)} collective-permute-done((f32[4,8,32,256]{3,2,1,0:T(8,128)S(1)}, f32[4,8,32,256]{3,2,1,0:T(8,128)S(1)}, u32[]{:S(2)}, u32[]{:S(2)}) %collective-permute-start.19) | collective-permute-done | bytes 1048608 | tf_op jit(solution)/shard_map/ppermute | solution.py:414
  76.3 0.9 add_convert_fusion
  77.3 7.9 %all-to-all-start = ((bf16[32,32,256]{2,1,0:T(8,128)(2,1)}), bf16[32,32,256]{2,1,0:T(8,128)(2,1)S(1)}, u32[]{:S(2)}, u32[]{:S(2)}) async-start(bf16[32,32,256]{2,1,0:T(8,128)(2,1)} %bitcast.14), calls=%async_computation | async-start | bytes 1048576 | tf_op jit(solution)/shard_map/all_to_all | solution.py:457
  85.2 4.0 %collective-permute-start.12 = (bf16[2,32,512]{2,1,0:T(8,128)(2,1)S(1)}, bf16[2,32,512]{2,1,0:T(8,128)(2,1)S(1)}, u32[]{:S(2)}, u32[]{:S(2)}) collective-permute-start(bf16[2,32,512]{2,1,0:T(8,128)(2,1)S(1)} %get-tuple-element.36), channel_id=1, source_target_pairs={{0,48},{8,56},{16,0},{24,8},{32,16},{40,24},{48,32},{56,40},{1,49}... | collective-permute-start | bytes 196616 | tf_op jit(solution)/shard_map/ppermute | solution.py:418
  89.2 2.3 %collective-permute-start.11 = (bf16[2,32,512]{2,1,0:T(8,128)(2,1)S(1)}, bf16[2,32,512]{2,1,0:T(8,128)(2,1)S(1)}, u32[]{:S(2)}, u32[]{:S(2)}) collective-permute-start(bf16[2,32,512]{2,1,0:T(8,128)(2,1)S(1)} %get-tuple-element.35), channel_id=1, source_target_pairs={{0,32},{8,40},{16,48},{24,56},{32,0},{40,8},{48,16},{56,24},{1,33}... | collective-permute-start | bytes 196616 | tf_op jit(solution)/shard_map/ppermute | solution.py:418
  91.5 2.4 %collective-permute-start.10 = (bf16[2,32,512]{2,1,0:T(8,128)(2,1)S(1)}, bf16[2,32,512]{2,1,0:T(8,128)(2,1)S(1)}, u32[]{:S(2)}, u32[]{:S(2)}) collective-permute-start(bf16[2,32,512]{2,1,0:T(8,128)(2,1)S(1)} %get-tuple-element.34), channel_id=1, source_target_pairs={{0,16},{8,24},{16,32},{24,40},{32,48},{40,56},{48,0},{56,8},{1,17}... | collective-permute-start | bytes 196616 | tf_op jit(solution)/shard_map/ppermute | solution.py:418
  93.9 8.7 %collective-permute-done.12.refs_3_ = bf16[2,32,512]{2,1,0:T(8,128)(2,1)S(1)} collective-permute-done((bf16[2,32,512]{2,1,0:T(8,128)(2,1)S(1)}, bf16[2,32,512]{2,1,0:T(8,128)(2,1)S(1)}, u32[]{:S(2)}, u32[]{:S(2)}) %collective-permute-start.12) | collective-permute-done | bytes 65568 | tf_op jit(solution)/shard_map/ppermute | solution.py:418
  102.6 4.7 %collective-permute-done.11.refs_2_ = bf16[2,32,512]{2,1,0:T(8,128)(2,1)S(1)} collective-permute-done((bf16[2,32,512]{2,1,0:T(8,128)(2,1)S(1)}, bf16[2,32,512]{2,1,0:T(8,128)(2,1)S(1)}, u32[]{:S(2)}, u32[]{:S(2)}) %collective-permute-start.11) | collective-permute-done | bytes 65568 | tf_op jit(solution)/shard_map/ppermute | solution.py:418
  107.3 0.0 collective-permute-done.10.refs_1_
  107.3 0.1 collective-permute-start.13
  107.4 0.1 convert_reduce_fusion
  107.5 0.6 collective-permute-start.22
  108.1 2.7 %collective-permute-start.21 = (f32[32,256]{1,0:T(8,128)S(1)}, f32[32,256]{1,0:T(8,128)S(1)}, u32[]{:S(2)}, u32[]{:S(2)}) collective-permute-start(f32[32,256]{1,0:T(8,128)S(1)} %convert_reduce_fusion), channel_id=1, source_target_pairs={{0,128},{64,192},{128,0},{192,64},{1,129},{65,193},{129,1},{193,65... | collective-permute-start | bytes 98312 | tf_op jit(solution)/shard_map/ppermute | solution.py:462
  110.9 0.0 collective-permute-start.20
  110.9 0.8 unpack.1
  111.6 2.2 %collective-permute-done.21 = f32[32,256]{1,0:T(8,128)S(1)} collective-permute-done((f32[32,256]{1,0:T(8,128)S(1)}, f32[32,256]{1,0:T(8,128)S(1)}, u32[]{:S(2)}, u32[]{:S(2)}) %collective-permute-start.21) | collective-permute-done | bytes 32800 | tf_op jit(solution)/shard_map/ppermute | solution.py:462
  113.8 0.9 collective-permute-done.20
  114.8 0.6 slice.41
  115.4 0.6 pad_maximum_fusion.3
  (28 shorter events, 0.1 us)
Async XLA Ops:
  0.6 25.7 %copy-start.3 = (bf16[1,1,8,128,256]{4,3,2,1,0:T(8,128)(2,1)S(1)}, bf16[1,1,8,128,256]{4,3,2,1,0:T(8,128)(2,1)}, u32[]{:S(2)}) copy-start(bf16[1,1,8,128,256]{4,3,2,1,0:T(8,128)(2,1)} %param.17) | copy-start | bytes 1572868
  0.6 9.3 %collective-permute-start = (bf16[8,128,256]{2,1,0:T(8,128)(2,1)}, bf16[8,128,256]{2,1,0:T(8,128)(2,1)S(1)}, u32[]{:S(2)}, u32[]{:S(2)}) collective-permute-start(bf16[8,128,256]{2,1,0:T(8,128)(2,1)} %bitcast.19), channel_id=1, source_target_pairs={{0,8},{8,0},{16,24},{24,16},{32,40},{40,32},{48,56},{56,48},{1,9},... | collective-permute-start | bytes 1572872 | tf_op jit(solution)/shard_map/ppermute | solution.py:414
  0.7 25.6 %collective-permute-start.14 = (bf16[8,128,256]{2,1,0:T(8,128)(2,1)}, bf16[8,128,256]{2,1,0:T(8,128)(2,1)S(1)}, u32[]{:S(2)}, u32[]{:S(2)}) collective-permute-start(bf16[8,128,256]{2,1,0:T(8,128)(2,1)} %bitcast.21), channel_id=1, source_target_pairs={{0,8},{8,0},{16,24},{24,16},{32,40},{40,32},{48,56},{56,48},{1,9},... | collective-permute-start | bytes 1572872 | tf_op jit(solution)/shard_map/ppermute | solution.py:414
  2.1 6.2 %collective-permute-start.5 = (bf16[128,256]{1,0:T(8,128)(2,1)S(1)}, bf16[128,256]{1,0:T(8,128)(2,1)S(1)}, u32[]{:S(2)}, u32[]{:S(2)}) collective-permute-start(bf16[128,256]{1,0:T(8,128)(2,1)S(1)} %get-tuple-element.48), channel_id=1, source_target_pairs={{1,0},{2,1},{3,2},{4,3},{5,4},{6,5},{7,6},{9,8},{10,9},{11,10},{12... | collective-permute-start | bytes 196616 | tf_op jit(solution)/shard_map/ppermute | solution.py:423
  3.4 6.4 %collective-permute-start.4 = (bf16[128,256]{1,0:T(8,128)(2,1)S(1)}, bf16[128,256]{1,0:T(8,128)(2,1)S(1)}, u32[]{:S(2)}, u32[]{:S(2)}) collective-permute-start(bf16[128,256]{1,0:T(8,128)(2,1)S(1)} %get-tuple-element.47), channel_id=1, source_target_pairs={{0,1},{1,2},{2,3},{3,4},{4,5},{5,6},{6,7},{8,9},{9,10},{10,11},{11... | collective-permute-start | bytes 196616 | tf_op jit(solution)/shard_map/ppermute | solution.py:422
  8.0 14.3 %collective-permute-start.15 = (bf16[4,64,512]{2,1,0:T(8,128)(2,1)}, bf16[4,64,512]{2,1,0:T(8,128)(2,1)S(1)}, u32[]{:S(2)}, u32[]{:S(2)}) collective-permute-start(bf16[4,64,512]{2,1,0:T(8,128)(2,1)} %bitcast.23), channel_id=1, source_target_pairs={{0,8},{8,0},{16,24},{24,16},{32,40},{40,32},{48,56},{56,48},{1,9},... | collective-permute-start | bytes 786440 | tf_op jit(solution)/shard_map/ppermute | solution.py:414
  9.9 5.8 %collective-permute-start.6 = (bf16[2,128,256]{2,1,0:T(8,128)(2,1)S(1)}, bf16[2,128,256]{2,1,0:T(8,128)(2,1)S(1)}, u32[]{:S(2)}, u32[]{:S(2)}) collective-permute-start(bf16[2,128,256]{2,1,0:T(8,128)(2,1)S(1)} %pad_maximum_fusion.1.own), channel_id=1, source_target_pairs={{0,8},{8,0},{16,24},{24,16},{32,40},{40,32},{48,56},{56,48},{1,9},... | collective-permute-start | bytes 393224 | tf_op jit(solution)/shard_map/ppermute | solution.py:414
  10.0 1.0 copy-start.2
  11.0 0.9 copy-start.5
  12.0 28.9 %copy-start.10 = (bf16[512,512]{1,0:T(8,128)(2,1)S(1)}, bf16[512,512]{1,0:T(8,128)(2,1)}, u32[]{:S(2)}) copy-start(bf16[512,512]{1,0:T(8,128)(2,1)} %param.22) | copy-start | bytes 1572868
  12.0 28.9 %copy-start.11 = (bf16[512,512]{1,0:T(8,128)(2,1)S(1)}, bf16[512,512]{1,0:T(8,128)(2,1)}, u32[]{:S(2)}) copy-start(bf16[512,512]{1,0:T(8,128)(2,1)} %param.21) | copy-start | bytes 1572868
  12.3 25.5 %collective-permute-start.1 = (bf16[2,144,256]{2,1,0:T(8,128)(2,1)S(1)}, bf16[2,144,256]{2,1,0:T(8,128)(2,1)S(1)}, u32[]{:S(2)}, u32[]{:S(2)}) collective-permute-start(bf16[2,144,256]{2,1,0:T(8,128)(2,1)S(1)} %get-tuple-element.26), channel_id=1, source_target_pairs={{0,16},{8,24},{16,32},{24,40},{32,48},{40,56},{48,0},{56,8},{1,17}... | collective-permute-start | bytes 442376 | tf_op jit(solution)/shard_map/ppermute | solution.py:418
  15.7 0.8 copy-start.8
  16.7 10.7 %collective-permute-start.7 = (bf16[2,48,256]{2,1,0:T(8,128)(2,1)S(1)}, bf16[2,48,256]{2,1,0:T(8,128)(2,1)S(1)}, u32[]{:S(2)}, u32[]{:S(2)}) collective-permute-start(bf16[2,48,256]{2,1,0:T(8,128)(2,1)S(1)} %get-tuple-element.30), channel_id=1, source_target_pairs={{0,16},{8,24},{16,32},{24,40},{32,48},{40,56},{48,0},{56,8},{1,17}... | collective-permute-start | bytes 147464 | tf_op jit(solution)/shard_map/ppermute | solution.py:418
  21.3 13.1 %collective-permute-start.8 = (bf16[2,48,256]{2,1,0:T(8,128)(2,1)S(1)}, bf16[2,48,256]{2,1,0:T(8,128)(2,1)S(1)}, u32[]{:S(2)}, u32[]{:S(2)}) collective-permute-start(bf16[2,48,256]{2,1,0:T(8,128)(2,1)S(1)} %get-tuple-element.31), channel_id=1, source_target_pairs={{0,32},{8,40},{16,48},{24,56},{32,0},{40,8},{48,16},{56,24},{1,33}... | collective-permute-start | bytes 147464 | tf_op jit(solution)/shard_map/ppermute | solution.py:418
  22.3 14.1 %collective-permute-start.9 = (bf16[2,48,256]{2,1,0:T(8,128)(2,1)S(1)}, bf16[2,48,256]{2,1,0:T(8,128)(2,1)S(1)}, u32[]{:S(2)}, u32[]{:S(2)}) collective-permute-start(bf16[2,48,256]{2,1,0:T(8,128)(2,1)S(1)} %get-tuple-element.32), channel_id=1, source_target_pairs={{0,48},{8,56},{16,0},{24,8},{32,16},{40,24},{48,32},{56,40},{1,49}... | collective-permute-start | bytes 147464 | tf_op jit(solution)/shard_map/ppermute | solution.py:418
  26.3 1.0 copy-start.6
  27.4 45.2 %collective-permute-start.16 = (bf16[2,192,256]{2,1,0:T(8,128)(2,1)S(1)}, bf16[2,192,256]{2,1,0:T(8,128)(2,1)S(1)}, u32[]{:S(2)}, u32[]{:S(2)}) collective-permute-start(bf16[2,192,256]{2,1,0:T(8,128)(2,1)S(1)} %get-tuple-element.38), channel_id=1, source_target_pairs={{0,16},{8,24},{16,32},{24,40},{32,48},{40,56},{48,0},{56,8},{1,17}... | collective-permute-start | bytes 589832 | tf_op jit(solution)/shard_map/ppermute | solution.py:418
  27.5 45.1 %collective-permute-start.17 = (bf16[2,192,256]{2,1,0:T(8,128)(2,1)S(1)}, bf16[2,192,256]{2,1,0:T(8,128)(2,1)S(1)}, u32[]{:S(2)}, u32[]{:S(2)}) collective-permute-start(bf16[2,192,256]{2,1,0:T(8,128)(2,1)S(1)} %get-tuple-element.39), channel_id=1, source_target_pairs={{0,32},{8,40},{16,48},{24,56},{32,0},{40,8},{48,16},{56,24},{1,33}... | collective-permute-start | bytes 589832 | tf_op jit(solution)/shard_map/ppermute | solution.py:418
  34.4 38.2 %collective-permute-start.18 = (bf16[2,192,256]{2,1,0:T(8,128)(2,1)S(1)}, bf16[2,192,256]{2,1,0:T(8,128)(2,1)S(1)}, u32[]{:S(2)}, u32[]{:S(2)}) collective-permute-start(bf16[2,192,256]{2,1,0:T(8,128)(2,1)S(1)} %get-tuple-element.40), channel_id=1, source_target_pairs={{0,48},{8,56},{16,0},{24,8},{32,16},{40,24},{48,32},{56,40},{1,49}... | collective-permute-start | bytes 589832 | tf_op jit(solution)/shard_map/ppermute | solution.py:418
  36.4 10.5 %collective-permute-start.2 = (bf16[2,144,256]{2,1,0:T(8,128)(2,1)S(1)}, bf16[2,144,256]{2,1,0:T(8,128)(2,1)S(1)}, u32[]{:S(2)}, u32[]{:S(2)}) collective-permute-start(bf16[2,144,256]{2,1,0:T(8,128)(2,1)S(1)} %get-tuple-element.27), channel_id=1, source_target_pairs={{0,32},{8,40},{16,48},{24,56},{32,0},{40,8},{48,16},{56,24},{1,33}... | collective-permute-start | bytes 442376 | tf_op jit(solution)/shard_map/ppermute | solution.py:418
  37.8 27.3 %collective-permute-start.3 = (bf16[2,144,256]{2,1,0:T(8,128)(2,1)S(1)}, bf16[2,144,256]{2,1,0:T(8,128)(2,1)S(1)}, u32[]{:S(2)}, u32[]{:S(2)}) collective-permute-start(bf16[2,144,256]{2,1,0:T(8,128)(2,1)S(1)} %get-tuple-element.28), channel_id=1, source_target_pairs={{0,48},{8,56},{16,0},{24,8},{32,16},{40,24},{48,32},{56,40},{1,49}... | collective-permute-start | bytes 442376 | tf_op jit(solution)/shard_map/ppermute | solution.py:418
  40.9 24.3 %copy-start = (bf16[3,3,256,256]{3,2,1,0:T(8,128)(2,1)S(1)}, bf16[3,3,256,256]{3,2,1,0:T(8,128)(2,1)}, u32[]{:S(2)}) copy-start(bf16[3,3,256,256]{3,2,1,0:T(8,128)(2,1)} %param.15) | copy-start | bytes 3538948
  40.9 24.3 %copy-start.1 = (bf16[2,2,256,512]{3,2,1,0:T(8,128)(2,1)S(1)}, bf16[2,2,256,512]{3,2,1,0:T(8,128)(2,1)}, u32[]{:S(2)}) copy-start(bf16[2,2,256,512]{3,2,1,0:T(8,128)(2,1)} %param.18) | copy-start | bytes 3145732
  40.9 24.3 %copy-start.4 = (bf16[768,256]{1,0:T(8,128)(2,1)S(1)}, bf16[768,256]{1,0:T(8,128)(2,1)}, u32[]{:S(2)}) copy-start(bf16[768,256]{1,0:T(8,128)(2,1)} %refs_11_.1) | copy-start | bytes 1179652
  40.9 24.3 %copy-start.7 = (bf16[320,192]{1,0:T(8,128)(2,1)S(1)}, bf16[320,192]{1,0:T(8,128)(2,1)}, u32[]{:S(2)}) copy-start(bf16[320,192]{1,0:T(8,128)(2,1)} %constant.12.clone.refs_8_) | copy-start | bytes 368644
  40.9 24.3 %copy-start.9 = (bf16[128,128]{1,0:T(8,128)(2,1)S(1)}, bf16[128,128]{1,0:T(8,128)(2,1)}, u32[]{:S(2)}) copy-start(bf16[128,128]{1,0:T(8,128)(2,1)} %constant.13.clone.refs_9_) | copy-start | bytes 98308
  73.6 2.7 %collective-permute-start.19 = (f32[4,8,32,256]{3,2,1,0:T(8,128)S(1)}, f32[4,8,32,256]{3,2,1,0:T(8,128)S(1)}, u32[]{:S(2)}, u32[]{:S(2)}) collective-permute-start(f32[4,8,32,256]{3,2,1,0:T(8,128)S(1)} %get-tuple-element.46), channel_id=1, source_target_pairs={{0,8},{8,0},{16,24},{24,16},{32,40},{40,32},{48,56},{56,48},{1,9},... | collective-permute-start | bytes 3145736 | tf_op jit(solution)/shard_map/ppermute | solution.py:414
  77.3 30.1 %all-to-all-start = ((bf16[32,32,256]{2,1,0:T(8,128)(2,1)}), bf16[32,32,256]{2,1,0:T(8,128)(2,1)S(1)}, u32[]{:S(2)}, u32[]{:S(2)}) async-start(bf16[32,32,256]{2,1,0:T(8,128)(2,1)} %bitcast.14), calls=%async_computation | async-start | bytes 1048576 | tf_op jit(solution)/shard_map/all_to_all | solution.py:457
  85.2 17.4 %collective-permute-start.12 = (bf16[2,32,512]{2,1,0:T(8,128)(2,1)S(1)}, bf16[2,32,512]{2,1,0:T(8,128)(2,1)S(1)}, u32[]{:S(2)}, u32[]{:S(2)}) collective-permute-start(bf16[2,32,512]{2,1,0:T(8,128)(2,1)S(1)} %get-tuple-element.36), channel_id=1, source_target_pairs={{0,48},{8,56},{16,0},{24,8},{32,16},{40,24},{48,32},{56,40},{1,49}... | collective-permute-start | bytes 196616 | tf_op jit(solution)/shard_map/ppermute | solution.py:418
  89.2 18.1 %collective-permute-start.11 = (bf16[2,32,512]{2,1,0:T(8,128)(2,1)S(1)}, bf16[2,32,512]{2,1,0:T(8,128)(2,1)S(1)}, u32[]{:S(2)}, u32[]{:S(2)}) collective-permute-start(bf16[2,32,512]{2,1,0:T(8,128)(2,1)S(1)} %get-tuple-element.35), channel_id=1, source_target_pairs={{0,32},{8,40},{16,48},{24,56},{32,0},{40,8},{48,16},{56,24},{1,33}... | collective-permute-start | bytes 196616 | tf_op jit(solution)/shard_map/ppermute | solution.py:418
  91.5 15.8 %collective-permute-start.10 = (bf16[2,32,512]{2,1,0:T(8,128)(2,1)S(1)}, bf16[2,32,512]{2,1,0:T(8,128)(2,1)S(1)}, u32[]{:S(2)}, u32[]{:S(2)}) collective-permute-start(bf16[2,32,512]{2,1,0:T(8,128)(2,1)S(1)} %get-tuple-element.34), channel_id=1, source_target_pairs={{0,16},{8,24},{16,32},{24,40},{32,48},{40,56},{48,0},{56,8},{1,17}... | collective-permute-start | bytes 196616 | tf_op jit(solution)/shard_map/ppermute | solution.py:418
  107.3 3.6 %collective-permute-start.13 = (bf16[4,32,512]{2,1,0:T(8,128)(2,1)S(1)}, bf16[4,32,512]{2,1,0:T(8,128)(2,1)S(1)}, u32[]{:S(2)}, u32[]{:S(2)}) collective-permute-start(bf16[4,32,512]{2,1,0:T(8,128)(2,1)S(1)} %pad_maximum_fusion.2), channel_id=1, source_target_pairs={{0,8},{8,0},{16,24},{24,16},{32,40},{40,32},{48,56},{56,48},{1,9},... | collective-permute-start | bytes 393224 | tf_op jit(solution)/shard_map/ppermute | solution.py:414
  107.5 4.1 %collective-permute-start.22 = (f32[32,256]{1,0:T(8,128)S(1)}, f32[32,256]{1,0:T(8,128)S(1)}, u32[]{:S(2)}, u32[]{:S(2)}) collective-permute-start(f32[32,256]{1,0:T(8,128)S(1)} %convert_reduce_fusion), channel_id=1, source_target_pairs={{0,192},{64,0},{128,64},{192,128},{1,193},{65,1},{129,65},{193,129... | collective-permute-start | bytes 98312 | tf_op jit(solution)/shard_map/ppermute | solution.py:462
  108.1 5.7 %collective-permute-start.21 = (f32[32,256]{1,0:T(8,128)S(1)}, f32[32,256]{1,0:T(8,128)S(1)}, u32[]{:S(2)}, u32[]{:S(2)}) collective-permute-start(f32[32,256]{1,0:T(8,128)S(1)} %convert_reduce_fusion), channel_id=1, source_target_pairs={{0,128},{64,192},{128,0},{192,64},{1,129},{65,193},{129,1},{193,65... | collective-permute-start | bytes 98312 | tf_op jit(solution)/shard_map/ppermute | solution.py:462
  110.9 3.9 %collective-permute-start.20 = (f32[32,256]{1,0:T(8,128)S(1)}, f32[32,256]{1,0:T(8,128)S(1)}, u32[]{:S(2)}, u32[]{:S(2)}) collective-permute-start(f32[32,256]{1,0:T(8,128)S(1)} %convert_reduce_fusion), channel_id=1, source_target_pairs={{0,64},{64,128},{128,192},{192,0},{1,65},{65,129},{129,193},{193,1... | collective-permute-start | bytes 98312 | tf_op jit(solution)/shard_map/ppermute | solution.py:462

commit v3 on v2

--- a/solution.py
+++ b/solution.py
@@ -9,26 +9,47 @@
 from jax.experimental.pallas import tpu as pltpu
 from jax.sharding import PartitionSpec as P
 
+
 F32 = jnp.float32
 BF16 = jnp.bfloat16
-NEG = -1e30
-
-
-def call(body, out_shape, args, any_args=(), scratch=(), name=None):
+
+
+def call(body, out_shape, args, scratch=(), room=8, manual=()):
     specs = [
-        pl.BlockSpec(memory_space=pl.ANY if i in any_args else pltpu.VMEM)
+        pl.BlockSpec(memory_space=pltpu.HBM if i in manual else pltpu.VMEM)
         for i in range(len(args))
     ]
     outs = [pl.BlockSpec(memory_space=pltpu.VMEM) for _ in out_shape]
+    held = [pltpu.VMEM(args[i].shape, args[i].dtype) for i in manual]
+
+    def run(*refs):
+        ins, rest = list(refs[: len(args)]), refs[len(args) :]
+        waits = []
+        if manual:
+            rest, local_refs, sems = rest[: -len(manual) - 1], rest[-len(manual) - 1 : -1], rest[-1]
+            for n, i in enumerate(manual):
+                copy = pltpu.make_async_copy(ins[i], local_refs[n], sems.at[n])
+                copy.start()
+                waits.append(copy.wait)
+                ins[i] = local_refs[n]
+            body(waits, *ins, *rest)
+        else:
+            body(*ins, *rest)
+
+    extra = held + [pltpu.SemaphoreType.DMA((len(manual),))] if manual else []
     return pl.pallas_call(
-        body,
+        run,
         out_shape=out_shape,
         in_specs=specs,
         out_specs=outs,
-        scratch_shapes=list(scratch),
-        compiler_params=pltpu.CompilerParams(vmem_limit_bytes=48 << 20),
-        name=name,
-    )(*args)
+        scratch_shapes=[*scratch, *extra],
+        compiler_params=pltpu.CompilerParams(vmem_limit_bytes=room << 20),
+    )(
+        *[
+            pltpu.with_memory_space_constraint(arg, pltpu.HBM) if i in manual else arg
+            for i, arg in enumerate(args)
+        ]
+    )
 
 
 def place():
@@ -36,51 +57,94 @@
     return index // 2, index % 2
 
 
+EDGES = 16
+
+
 def edge_picker(count, cols, strip):
     strips = cols // strip
-    pick = np.zeros((strips, 2 * 8, count * cols), np.float32)
+    pick = np.zeros((strips, EDGES, count * cols), np.float32)
     for j in range(strips):
         for r in range(count):
             if j > 0:
                 pick[j, r, r * cols + j * strip - 1] = 1
             if j < strips - 1:
                 pick[j, count + r, r * cols + (j + 1) * strip] = 1
-    return jnp.asarray(pick.reshape(strips * 16, count * cols), BF16)
-
-
-def pack_cells_body(own, partner, pick, *refs, links):
-    outs, edges = refs[:links], refs[links]
+    return jnp.asarray(pick.reshape(strips * EDGES, count * cols), BF16)
+
+
+def pack_piece(tall, edges, out, s, j):
+    count, cols, chan = tall.shape
+    strip = cols // edges.shape[0]
+    begin = pl.multiple_of(j * strip, strip)
+    out[s, : count * strip] = tall[:, pl.ds(begin, strip), :].reshape(count * strip, chan)
+    out[s, count * strip :] = edges[j]
+
+
+def find_edges(tall, pick, edges):
+    count, cols, chan = tall.shape
+    flat = tall[...].reshape(count * cols, chan)
+    found = jnp.dot(pick[...], flat, preferred_element_type=F32).astype(BF16)
+    edges[...] = found.reshape(edges.shape)
+
+
+def pack_main_body(waits, own, partner, pick, out, edges, *, links):
+    _, core = place()
+    for wait in waits:
+        wait()
+    for s, source in enumerate((own, partner)):
+        find_edges(source, pick, edges)
+        for k in range(links):
+            pack_piece(source, edges, out.at[k], s, 2 * k + core)
+
+
+def pack_main(own, partner, links):
+    rows, cols, chan = own.shape
+    strip = cols // (2 * links)
+    return call(
+        functools.partial(pack_main_body, links=links),
+        [jax.ShapeDtypeStruct((links, 2, rows * strip + EDGES, chan), BF16)],
+        (own, partner, edge_picker(rows, cols, strip)),
+        scratch=[pltpu.VMEM((2 * links, EDGES, chan), BF16)],
+        manual=(0, 2),
+    )[0]
+
+
+def pack_halo_body(waits, *refs, links):
+    sources, pick, outs = (refs[:2], refs[2:4]), refs[4], refs[5 : 5 + links]
+    tall, edges = refs[5 + links :]
     zhi, core = place()
-    count, cols, chan = own.shape
+    for wait in waits:
+        wait()
+    index = lax.axis_index("space")
+    first, last = index == 0, index == lax.axis_size("space") - 1
+    for s, (above, below) in enumerate(sources):
+        tall[0] = jnp.where(first, jnp.zeros_like(above), above[...])
+        tall[1] = jnp.where(last, jnp.zeros_like(below), below[...])
+        find_edges(tall, pick, edges)
+        for k in range(links):
+            pack_piece(tall, edges, outs[k], s, 2 * lax.rem(zhi + k, links) + core)
+
+
+def pack_halo(own, partner, links):
+    cols, chan = own[0].shape
     strip = cols // (2 * links)
-    for s, source in enumerate((own, partner)):
-        flat = source[...].reshape(count * cols, chan)
-        found = jnp.dot(pick[...], flat, preferred_element_type=F32).astype(BF16)
-        edges[...] = found.reshape(2 * links, 16, chan)
-        for k in range(links):
-            j = 2 * lax.rem(zhi + k, links) + core
-            begin = pl.multiple_of(j * strip, strip)
-            piece = source[:, pl.ds(begin, strip), :].reshape(count * strip, chan)
-            outs[k][s, : count * strip] = piece
-            outs[k][s, count * strip :] = edges[j]
-
-
-def pack_cells(own, partner, links):
-    count, cols, chan = own.shape
-    strip = cols // (2 * links)
-    pick = edge_picker(count, cols, strip)
-    shape = jax.ShapeDtypeStruct((2, count * strip + 16, chan), BF16)
+    shape = jax.ShapeDtypeStruct((2, 2 * strip + EDGES, chan), BF16)
     return call(
-        functools.partial(pack_cells_body, links=links),
+        functools.partial(pack_halo_body, links=links),
         [shape] * links,
-        (own, partner, pick),
-        scratch=[pltpu.VMEM((2 * links, 16, chan), BF16)],
-        name="pack_cells",
-    )
-
-
-def pack_teacher_body(own_mid, partner_mid, own_top, partner_top, *outs, links):
+        (*own, *partner, edge_picker(2, cols, strip)),
+        scratch=[
+            pltpu.VMEM((2, cols, chan), BF16),
+            pltpu.VMEM((2 * links, EDGES, chan), BF16),
+        ],
+        manual=(4,),
+    )
+
+
+def pack_teacher_body(waits, own_mid, partner_mid, own_top, partner_top, *outs, links):
     zhi, core = place()
+    for wait in waits:
+        wait()
     rows, cols, chan = own_mid.shape
     half_rows, half_cols, width = own_top.shape
     strip = cols // (2 * links)
@@ -106,21 +170,20 @@
     half_rows, half_cols, width = own_top.shape
     points = half_rows * (half_cols // (2 * links))
     height = rows * (cols // (2 * links)) + points * (width // chan)
-    shape = jax.ShapeDtypeStruct((2, height, chan), BF16)
     return call(
         functools.partial(pack_teacher_body, links=links),
-        [shape] * links,
+        [jax.ShapeDtypeStruct((2, height, chan), BF16)] * links,
         (own_mid, partner_mid, own_top, partner_top),
-        name="pack_teacher",
+        manual=(0, 2),
     )
 
 
 def shift_pickers(rows, strip):
     main = rows * strip
-    left = np.zeros((rows + 2, strip, main + 16 + 2 * strip + 16), np.float32)
+    halo = main + EDGES
+    corner = halo + 2 * strip
+    left = np.zeros((rows + 2, strip, corner + EDGES), np.float32)
     right = np.zeros_like(left)
-    halo = main + 16
-    corner = halo + 2 * strip
     for q in range(rows + 2):
         if q == 0:
             cell, l_edge, r_edge = halo, corner, corner + 2
@@ -145,40 +208,35 @@
     return jnp.asarray(pick.reshape(frames * strip, frames * strip), BF16)
 
 
-def encode_body(*refs, links, rows, strip):
-    cells, refs = refs[:links], refs[links:]
+def encode_body(waits, *refs, links, rows, strip):
+    cells, shifts, w_spatial, parity, w_temporal, w_down, refs = (*refs[:6], refs[6:])
     halos, refs = refs[:links], refs[links:]
-    shifts, parity, w_spatial, w_temporal_h, w_down_h, w_proj_h, refs = (*refs[:6], refs[6:])
+    w_proj, refs = refs[:4], refs[4:]
     spatial, mid_out, attended_out, student_out, refs = (*refs[:4], refs[4:])
     pieces, refs = refs[:links], refs[links:]
-    grid, cat, patch, top, w_temporal, w_down, w_proj, sems = refs
-    copies = [
-        pltpu.make_async_copy(w_temporal_h, w_temporal, sems.at[0]),
-        pltpu.make_async_copy(w_down_h, w_down, sems.at[1]),
-        pltpu.make_async_copy(w_proj_h, w_proj, sems.at[2]),
-    ]
-    for copy in copies:
-        copy.start()
+    grid, cat, patch, top = refs
     zhi, core = place()
     frames = 2 * links
     chan = spatial.shape[-1]
     width = attended_out.shape[-1]
+    tall = (rows + 2) * strip
+    waits[0]()
+    waits[1]()
     main = rows * strip
-    tall = (rows + 2) * strip
     for k in range(links):
         origin = lax.rem(zhi - k + links, links)
         for s in range(2):
             t = 2 * origin + (core if s == 0 else 1 - core)
-            cat[: main + 16] = cells[k][s]
-            cat[main + 16 :] = halos[k][s]
+            cat[: main + EDGES] = cells[origin, s]
+            cat[main + EDGES :] = halos[k][s]
             moved = jnp.dot(shifts[...], cat[...], preferred_element_type=F32).astype(BF16)
             grid[:, t, :, :chan] = moved[:tall].reshape(rows + 2, strip, chan)
             grid[:, t, :, 2 * chan :] = moved[tall:].reshape(rows + 2, strip, chan)
-            grid[0, t, :, chan : 2 * chan] = halos[k][s, :strip]
-            grid[1 : rows + 1, t, :, chan : 2 * chan] = cells[k][s, :main].reshape(
-                rows, strip, chan
-            )
-            grid[rows + 1, t, :, chan : 2 * chan] = halos[k][s, strip : 2 * strip]
+            centre = slice(chan, 2 * chan)
+            grid[0, t, :, centre] = halos[k][s, :strip]
+            grid[1 : rows + 1, t, :, centre] = cells[origin, s, :main].reshape(rows, strip, chan)
+            grid[rows + 1, t, :, centre] = halos[k][s, strip : 2 * strip]
+    waits[2]()
     cellcount = rows * frames * strip
     conv = jnp.dot(
         grid[:rows].reshape(cellcount, 3 * chan), w_spatial[0], preferred_element_type=F32
@@ -192,7 +250,8 @@
     conv = conv / (1.0 + jnp.exp(-conv))
     spatial[:, :2] = jnp.zeros((rows, 2, strip, chan), BF16)
     spatial[:, 2:] = conv.astype(BF16).reshape(rows, frames, strip, chan)
-    copies[0].wait()
+    for wait in waits[3:]:
+        wait()
     acc = grid[1 : rows + 1, :, :, chan : 2 * chan].reshape(cellcount, chan).astype(F32)
     temporal = jnp.dot(
         spatial[:, :frames].reshape(cellcount, chan),
@@ -216,14 +275,12 @@
         span = slice(i * line // 2, (i + 1) * line // 2)
         patch[span, 2 * a * chan : (2 * a + 1) * chan] = both[: line // 2]
         patch[span, (2 * a + 1) * chan : (2 * a + 2) * chan] = both[line // 2 :]
-    copies[1].wait()
     coarse = jnp.dot(patch[...], w_down[...], preferred_element_type=F32).astype(BF16)
-    copies[2].wait()
     half_rows = rows // 2
     quads = (half_rows, frames, half, width)
-    query = jnp.dot(coarse, w_proj[0], preferred_element_type=F32).astype(BF16)
-    key = jnp.dot(coarse, w_proj[1], preferred_element_type=F32).astype(BF16)
-    value = jnp.dot(coarse, w_proj[2], preferred_element_type=F32).astype(BF16)
+    query = jnp.dot(coarse, w_proj[0][...], preferred_element_type=F32).astype(BF16)
+    key = jnp.dot(coarse, w_proj[1][...], preferred_element_type=F32).astype(BF16)
+    value = jnp.dot(coarse, w_proj[2][...], preferred_element_type=F32).astype(BF16)
     top[0] = query.astype(F32).reshape(quads)
     top[1] = key.astype(F32).reshape(quads)
     top[2] = value.astype(F32).reshape(quads)
@@ -247,7 +304,7 @@
     lax.fori_loop(0, half_rows, attend, 0)
     attended = top[3].reshape(half_rows * frames * half, width).astype(BF16)
     attended_out[...] = attended
-    out = jnp.dot(attended, w_proj[3], preferred_element_type=F32)
+    out = jnp.dot(attended, w_proj[3][...], preferred_element_type=F32)
     student = (coarse.astype(F32) + out).astype(BF16)
     student_out[...] = student
     top[0] = student.astype(F32).reshape(quads)
@@ -265,16 +322,15 @@
     half = strip // 2
     points = (rows // 2) * half
     args = (
-        *cells,
-        *halos,
+        cells,
         shift_pickers(rows, strip),
+        w_spatial.reshape(3, 3 * chan, chan),
         parity_picker(frames, strip),
-        w_spatial.reshape(3, 3 * chan, chan),
         w_temporal,
         w_down.reshape(4 * chan, width),
-        w_proj,
-    )
-    first = 2 * links + 3
+        *halos,
+        *w_proj,
+    )
     shapes = [
         jax.ShapeDtypeStruct((rows, frames + 2, strip, chan), BF16),
         jax.ShapeDtypeStruct((rows * frames * strip, chan), BF16),
@@ -283,21 +339,17 @@
     ] + [jax.ShapeDtypeStruct((2, points, width), BF16)] * links
     scratch = [
         pltpu.VMEM((rows + 2, frames, strip, 3 * chan), BF16),
-        pltpu.VMEM((rows * strip + 16 + 2 * strip + 16, chan), BF16),
+        pltpu.VMEM((rows * strip + 2 * strip + 2 * EDGES, chan), BF16),
         pltpu.VMEM((frames * points, 4 * chan), BF16),
         pltpu.VMEM((4, rows // 2, frames, half, width), F32),
-        pltpu.VMEM(w_temporal.shape, BF16),
-        pltpu.VMEM((4 * chan, width), BF16),
-        pltpu.VMEM((4, width, width), BF16),
-        pltpu.SemaphoreType.DMA((3,)),
     ]
     outs = call(
         functools.partial(encode_body, links=links, rows=rows, strip=strip),
         shapes,
         args,
-        any_args=(first, first + 1, first + 2),
         scratch=scratch,
-        name="encode",
+        room=32,
+        manual=(0, 1, 2, 3, 4, 5, *range(6 + links, 10 + links)),
     )
     return outs[:4], outs[4:]
 
@@ -368,7 +420,7 @@
         ),
         [
             jax.ShapeDtypeStruct((links, spaces, height, chan), F32),
-            jax.ShapeDtypeStruct((links, spaces, height, chan), F32),
+            jax.ShapeDtypeStruct((links, spaces, height, chan), BF16),
         ],
         (*teachers, spatial, mid, attended, student),
         scratch=[
@@ -377,7 +429,7 @@
             pltpu.VMEM((3 * chan, chan), F32),
             pltpu.VMEM((width, width), F32),
         ],
-        name="gradients",
+        room=16,
     )
 
 
@@ -396,6 +448,16 @@
         out[:, pl.ds(begin, 2 * half), :] = jnp.concatenate([first, second], 1).astype(BF16)
 
 
+def finish_body(*refs):
+    parts, mid, top = refs[:-2], refs[-2], refs[-1]
+    total = functools.reduce(jnp.add, [part[...] for part in parts])
+    chan = total.shape[1]
+    n_top = top.shape[0]
+    mid[...] = total[: mid.shape[0]]
+    for h in range(top.shape[1] // chan):
+        top[:, h * chan : (h + 1) * chan] = total[16 + h * n_top : 16 + (h + 1) * n_top]
+
+
 def local(
     feats, w_spatial, w_temporal, teacher_mid, w_down, w_query, w_key, w_value, w_out, teacher_top
 ):
@@ -419,15 +481,24 @@
             for k in range(1, links)
         ]
 
-    above = lax.ppermute(own[rows - 1], "space", [(i, i + 1) for i in range(spaces - 1)])
-    below = lax.ppermute(own[0], "space", [(i + 1, i) for i in range(spaces - 1)])
-    cells = spread(pack_cells(own, swap(own), links))
-    halo = jnp.stack([above, below])
-    halos = spread(pack_cells(halo, swap(halo), links))
+    columns = [list(range(c, frames, 2)) for c in range(2)]
+
+    def gather(pieces):
+        return lax.all_to_all(pieces, "tm", 0, 0, axis_index_groups=columns, tiled=True)
+
+    ring = [(i, (i + 1) % spaces) for i in range(spaces)]
+    above = lax.ppermute(own[rows - 1], "space", ring)
+    below = lax.ppermute(own[0], "space", [(j, i) for i, j in ring])
+    cells = pack_main(own, swap(own), links)
+    cells = gather(cells)
+    other = (swap(above), swap(below))
+    halo = pack_halo((above, below), other, links)
+    halos = spread(halo)
     t_mid, t_top = teacher_mid[0, 0], teacher_top[0, 0]
-    teachers = spread(pack_teacher(t_mid, swap(t_mid), t_top, swap(t_top), links))
-
-    w_proj = jnp.stack([w_query, w_key, w_value, w_out])
+    teachers = pack_teacher(t_mid, swap(t_mid), t_top, swap(t_top), links)
+    teachers = spread(teachers)
+
+    w_proj = (w_query, w_key, w_value, w_out)
     saved, pieces = encode(
         cells, halos, w_spatial, w_temporal, w_down, w_proj, links, rows, strip
     )
@@ -437,7 +508,6 @@
         functools.partial(unpack_body, links=links),
         [jax.ShapeDtypeStruct((half_rows, half_cols, width), BF16)],
         (*returned, swapped),
-        name="unpack",
     )[0]
 
     keep, give = gradients(
@@ -448,25 +518,26 @@
         1.0 / math.sqrt(rows * cols * devices_all),
         1.0 / math.sqrt(points * frames * devices_all),
     )
-    part = (keep + swap(give)).astype(BF16)
-    height = part.shape[2]
-    part = part.reshape(links * spaces, height, chan)
+    part = (keep + swap(give).astype(F32)).astype(BF16)
+    part = part.reshape(links * spaces, *part.shape[2:])
     groups = [
         [(2 * z + c) * spaces + p for z in range(links) for p in range(spaces)] for c in range(2)
     ]
-    part = lax.all_to_all(
-        part, ("tm", "space"), 0, 0, axis_index_groups=groups, tiled=True
-    )
+    part = lax.all_to_all(part, ("tm", "space"), 0, 0, axis_index_groups=groups, tiled=True)
     part = jnp.sum(part.astype(F32), 0)
     others = [
         lax.ppermute(part, "dp", [(i, (i + k) % clips) for i in range(clips)])
         for k in range(1, clips)
     ]
-    for other in others:
-        part = part + other
     n_top = width // (frames * spaces)
-    grad_temporal = part[: 3 * chan // (frames * spaces)]
-    grad_out = jnp.concatenate([part[16 : 16 + n_top], part[16 + n_top :]], 1)
+    grad_temporal, grad_out = call(
+        finish_body,
+        [
+            jax.ShapeDtypeStruct((3 * chan // (frames * spaces), chan), F32),
+            jax.ShapeDtypeStruct((n_top, width), F32),
+        ],
+        (part, *others),
+    )
     return (home[None, None], grad_temporal, grad_out)
 
 

time: 118 us -> 113 us (0.958)
  the two profiles are of different devices: /device:TPU:4 before, /device:TPU:24 now
where the time goes in v3:
time: 113 us; the launch traced here: 112 us
  starting transfers between devices  53.4 us (47%)
  waiting for transfers between devices  40.7 us (36%)
  Pallas kernels  14.8 us (13%)
  local copies, waits for them, and re-layouts  1.72 us (2%)
    ppermute x9, starting transfers between devices, spread(): lax.ppermute(pieces[k], 'tm', [(i, (i + 2 * k) % frames) for i in range(f...  28.7 us
    ppermute x9, waiting for transfers between devices, spread(): lax.ppermute(pieces[k], 'tm', [(i, (i + 2 * k) % frames) for i in range(f...  23.8 us
    pallas_call x7, Pallas kernels, call(): pl.pallas_call(run, out_shape=out_shape, in_specs=specs, out_specs=outs,...  14.8 us
    all_to_all x1, starting transfers between devices, local(): lax.all_to_all(part, ('tm', 'space'), 0, 0, axis_index_groups=groups, til...  8.73 us
    all_to_all x1, starting transfers between devices, gather(): lax.all_to_all(pieces, 'tm', 0, 0, axis_index_groups=columns, tiled=True)  8.47 us
    ppermute x1, waiting for transfers between devices, local(): below = lax.ppermute(own[0], 'space', [(j, i) for i, j in ring])  6.56 us
    ppermute x7, waiting for transfers between devices, swap(): return lax.ppermute(block, 'tm', [(i, i ^ 1) for i in range(frames)])  5.26 us
    ppermute x3, starting transfers between devices, local(): lax.ppermute(part, 'dp', [(i, (i + k) % clips) for i in range(clips)])  4.53 us
  transfers between devices with their start and end apart: 23, of which 12 were waited for; matrix products, arithmetic and copies ran while one was open for 1% of the time, Pallas kernels for 10%

profile of v3, /device:TPU:24, one launch (start us, length us, event | category | flops | bytes accessed | tf_op | source)
XLA Modules:
  0.0 112.4 jit_solution(5398576152666810447)
XLA Ops:
  0.6 0.0 copy-start.1
  0.6 0.0 copy-start.2
  0.7 0.1 collective-permute-start
  0.8 2.1 %collective-permute-done.refs_1_ = bf16[8,128,256]{2,1,0:T(8,128)(2,1)S(1)} collective-permute-done((bf16[8,128,256]{2,1,0:T(8,128)(2,1)}, bf16[8,128,256]{2,1,0:T(8,128)(2,1)S(1)}, u32[]{:S(2)}, u32[]{:S(2)}) %collective-permute-start) | collective-permute-done | bytes 524320 | tf_op jit(solution)/shard_map/ppermute | solution.py:476
  2.9 2.3 %shard_map.157 = bf16[4,2,144,256]{3,2,1,0:T(8,128)(2,1)} custom-call(bf16[8,128,256]{2,1,0:T(8,128)(2,1)} %bitcast.14, bf16[8,128,256]{2,1,0:T(8,128)(2,1)S(1)} %collective-permute-done.refs_1_, bf16[128,1024]{1,0:T(8,128)(2,1)} %constant.10.clone.refs_2_), custom_call_target="tpu_custom_call" | custom-call | tf_op jit(solution)/shard_map/pallas_call | solution.py:40
  5.1 8.5 %all-to-all-start = ((bf16[4,2,144,256]{3,2,1,0:T(8,128)(2,1)}), bf16[4,2,144,256]{3,2,1,0:T(8,128)(2,1)S(1)}, u32[]{:S(2)}, u32[]{:S(2)}) async-start(bf16[4,2,144,256]{3,2,1,0:T(8,128)(2,1)} %shard_map.157), calls=%async_computation | async-start | bytes 1179648 | tf_op jit(solution)/shard_map/all_to_all | solution.py:487
  13.6 0.0 copy-done.1
  13.6 0.0 collective-permute-start.12
  13.6 0.0 copy-done.2
  13.6 0.5 collective-permute-start.13
  14.1 0.9 slice_bitcast_fusion
  15.0 1.3 %collective-permute-start.2 = (bf16[128,256]{1,0:T(8,128)(2,1)S(1)}, bf16[128,256]{1,0:T(8,128)(2,1)S(1)}, u32[]{:S(2)}, u32[]{:S(2)}) collective-permute-start(bf16[128,256]{1,0:T(8,128)(2,1)S(1)} %get-tuple-element.43), channel_id=1, source_target_pairs={{1,0},{2,1},{3,2},{4,3},{5,4},{6,5},{7,6},{0,7},{9,8},{10,9},{11,1... | collective-permute-start | bytes 196616 | tf_op jit(solution)/shard_map/ppermute | solution.py:491
  16.3 0.8 collective-permute-start.1
  17.1 0.0 collective-permute-done.13.refs_3_
  17.1 0.0 collective-permute-done.12.refs_1_
  17.1 1.2 %shard_map.161 = (bf16[2,192,256]{2,1,0:T(8,128)(2,1)S(1)}, bf16[2,192,256]{2,1,0:T(8,128)(2,1)S(1)}, bf16[2,192,256]{2,1,0:T(8,128)(2,1)S(1)}, bf16[2,192,256]{2,1,0:T(8,128)(2,1)S(1)}) custom-call(bf16[8,128,256]{2,1,0:T(8,128)(2,1)} %bitcast.15, bf16[8,128,256]{2,1,0:T(8,128)(2,1)S(1)} %collective-permute-done.12.refs_1_, bf16[4,64,512]{2,1,0:T(8,128)(2,1)} %bitcast.18, ...), custom_call_target="tpu_custom_call" | custom-call | tf_op jit(solution)/shard_map/pallas_call | solution.py:40
  18.3 3.0 %collective-permute-start.14 = (bf16[2,192,256]{2,1,0:T(8,128)(2,1)S(1)}, bf16[2,192,256]{2,1,0:T(8,128)(2,1)S(1)}, u32[]{:S(2)}, u32[]{:S(2)}) collective-permute-start(bf16[2,192,256]{2,1,0:T(8,128)(2,1)S(1)} %get-tuple-element.32), channel_id=1, source_target_pairs={{0,16},{8,24},{16,32},{24,40},{32,48},{40,56},{48,0},{56,8},{1,17}... | collective-permute-start | bytes 589832 | tf_op jit(solution)/shard_map/ppermute | solution.py:480
  21.3 3.6 %collective-permute-start.15 = (bf16[2,192,256]{2,1,0:T(8,128)(2,1)S(1)}, bf16[2,192,256]{2,1,0:T(8,128)(2,1)S(1)}, u32[]{:S(2)}, u32[]{:S(2)}) collective-permute-start(bf16[2,192,256]{2,1,0:T(8,128)(2,1)S(1)} %get-tuple-element.33), channel_id=1, source_target_pairs={{0,32},{8,40},{16,48},{24,56},{32,0},{40,8},{48,16},{56,24},{1,33}... | collective-permute-start | bytes 589832 | tf_op jit(solution)/shard_map/ppermute | solution.py:480
  24.9 3.6 %collective-permute-start.16 = (bf16[2,192,256]{2,1,0:T(8,128)(2,1)S(1)}, bf16[2,192,256]{2,1,0:T(8,128)(2,1)S(1)}, u32[]{:S(2)}, u32[]{:S(2)}) collective-permute-start(bf16[2,192,256]{2,1,0:T(8,128)(2,1)S(1)} %get-tuple-element.34), channel_id=1, source_target_pairs={{0,48},{8,56},{16,0},{24,8},{32,16},{40,24},{48,32},{56,40},{1,49}... | collective-permute-start | bytes 589832 | tf_op jit(solution)/shard_map/ppermute | solution.py:480
  28.5 6.6 %collective-permute-done.2.refs_1_ = bf16[128,256]{1,0:T(8,128)(2,1)S(1)} collective-permute-done((bf16[128,256]{1,0:T(8,128)(2,1)S(1)}, bf16[128,256]{1,0:T(8,128)(2,1)S(1)}, u32[]{:S(2)}, u32[]{:S(2)}) %collective-permute-start.2) | collective-permute-done | bytes 65568 | tf_op jit(solution)/shard_map/ppermute | solution.py:491
  35.0 0.0 collective-permute-start.4
  35.0 1.6 %collective-permute-done.1.refs_0_ = bf16[128,256]{1,0:T(8,128)(2,1)S(1)} collective-permute-done((bf16[128,256]{1,0:T(8,128)(2,1)S(1)}, bf16[128,256]{1,0:T(8,128)(2,1)S(1)}, u32[]{:S(2)}, u32[]{:S(2)}) %collective-permute-start.1) | collective-permute-done | bytes 65568 | tf_op jit(solution)/shard_map/ppermute | solution.py:490
  36.6 0.0 collective-permute-start.3
  36.6 0.0 collective-permute-done.4.refs_3_
  36.6 1.2 %collective-permute-done.3.refs_2_ = bf16[128,256]{1,0:T(8,128)(2,1)S(1)} collective-permute-done((bf16[128,256]{1,0:T(8,128)(2,1)S(1)}, bf16[128,256]{1,0:T(8,128)(2,1)S(1)}, u32[]{:S(2)}, u32[]{:S(2)}) %collective-permute-start.3) | collective-permute-done | bytes 65568 | tf_op jit(solution)/shard_map/ppermute | solution.py:476
  37.9 1.0 shard_map.158
  38.9 2.6 %collective-permute-start.5 = (bf16[2,48,256]{2,1,0:T(8,128)(2,1)S(1)}, bf16[2,48,256]{2,1,0:T(8,128)(2,1)S(1)}, u32[]{:S(2)}, u32[]{:S(2)}) collective-permute-start(bf16[2,48,256]{2,1,0:T(8,128)(2,1)S(1)} %get-tuple-element.24), channel_id=1, source_target_pairs={{0,16},{8,24},{16,32},{24,40},{32,48},{40,56},{48,0},{56,8},{1,17}... | collective-permute-start | bytes 147464 | tf_op jit(solution)/shard_map/ppermute | solution.py:480
  41.6 4.8 %collective-permute-start.6 = (bf16[2,48,256]{2,1,0:T(8,128)(2,1)S(1)}, bf16[2,48,256]{2,1,0:T(8,128)(2,1)S(1)}, u32[]{:S(2)}, u32[]{:S(2)}) collective-permute-start(bf16[2,48,256]{2,1,0:T(8,128)(2,1)S(1)} %get-tuple-element.25), channel_id=1, source_target_pairs={{0,32},{8,40},{16,48},{24,56},{32,0},{40,8},{48,16},{56,24},{1,33}... | collective-permute-start | bytes 147464 | tf_op jit(solution)/shard_map/ppermute | solution.py:480
  46.4 7.2 %collective-permute-done.5.refs_7_ = bf16[2,48,256]{2,1,0:T(8,128)(2,1)S(1)} collective-permute-done((bf16[2,48,256]{2,1,0:T(8,128)(2,1)S(1)}, bf16[2,48,256]{2,1,0:T(8,128)(2,1)S(1)}, u32[]{:S(2)}, u32[]{:S(2)}) %collective-permute-start.5) | collective-permute-done | bytes 49184 | tf_op jit(solution)/shard_map/ppermute | solution.py:480
  53.6 1.5 %collective-permute-start.7 = (bf16[2,48,256]{2,1,0:T(8,128)(2,1)S(1)}, bf16[2,48,256]{2,1,0:T(8,128)(2,1)S(1)}, u32[]{:S(2)}, u32[]{:S(2)}) collective-permute-start(bf16[2,48,256]{2,1,0:T(8,128)(2,1)S(1)} %get-tuple-element.26), channel_id=1, source_target_pairs={{0,48},{8,56},{16,0},{24,8},{32,16},{40,24},{48,32},{56,40},{1,49}... | collective-permute-start | bytes 147464 | tf_op jit(solution)/shard_map/ppermute | solution.py:480
  55.1 0.5 collective-permute-done.6.refs_8_
  55.6 3.0 %collective-permute-done.7.refs_9_ = bf16[2,48,256]{2,1,0:T(8,128)(2,1)S(1)} collective-permute-done((bf16[2,48,256]{2,1,0:T(8,128)(2,1)S(1)}, bf16[2,48,256]{2,1,0:T(8,128)(2,1)S(1)}, u32[]{:S(2)}, u32[]{:S(2)}) %collective-permute-start.7) | collective-permute-done | bytes 49184 | tf_op jit(solution)/shard_map/ppermute | solution.py:480
  58.6 0.0 all-to-all-done.refs_0_
  58.6 0.0 copy-start
  58.6 0.8 copy-done
  59.4 8.0 %shard_map.159 = (bf16[8,10,16,256]{3,2,1,0:T(8,128)(2,1)S(1)}, bf16[1024,256]{1,0:T(8,128)(2,1)S(1)}, bf16[256,512]{1,0:T(8,128)(2,1)S(1)}, bf16[256,512]{1,0:T...) custom-call(bf16[4,2,144,256]{3,2,1,0:T(8,128)(2,1)} %copy-done, ...), custom_call_target="tpu_custom_call" | custom-call | tf_op jit(solution)/shard_map/pallas_call | solution.py:40
  67.3 0.0 collective-permute-done.14.refs_1_
  67.4 0.0 collective-permute-done.15.refs_2_
  67.4 0.0 collective-permute-done.16.refs_3_
  67.4 0.9 shard_map.162
  68.3 0.1 collective-permute-start.17
  68.4 1.9 %collective-permute-done.17 = bf16[4,8,32,256]{3,2,1,0:T(8,128)(2,1)S(1)} collective-permute-done((bf16[4,8,32,256]{3,2,1,0:T(8,128)(2,1)S(1)}, bf16[4,8,32,256]{3,2,1,0:T(8,128)(2,1)S(1)}, u32[]{:S(2)}, u32[]{:S(2)}) %collective-permute-start.17) | collective-permute-done | bytes 524320 | tf_op jit(solution)/shard_map/ppermute | solution.py:476
  70.3 1.0 add_convert_fusion
  71.3 8.7 %all-to-all-start.1 = ((bf16[32,32,256]{2,1,0:T(8,128)(2,1)}), bf16[32,32,256]{2,1,0:T(8,128)(2,1)S(1)}, u32[]{:S(2)}, u32[]{:S(2)}) async-start(bf16[32,32,256]{2,1,0:T(8,128)(2,1)} %bitcast.8), calls=%async_computation.1 | async-start | bytes 1048576 | tf_op jit(solution)/shard_map/all_to_all | solution.py:526
  80.0 2.4 %collective-permute-start.8 = (bf16[2,32,512]{2,1,0:T(8,128)(2,1)S(1)}, bf16[2,32,512]{2,1,0:T(8,128)(2,1)S(1)}, u32[]{:S(2)}, u32[]{:S(2)}) collective-permute-start(bf16[2,32,512]{2,1,0:T(8,128)(2,1)S(1)} %get-tuple-element.28), channel_id=1, source_target_pairs={{0,16},{8,24},{16,32},{24,40},{32,48},{40,56},{48,0},{56,8},{1,17}... | collective-permute-start | bytes 196616 | tf_op jit(solution)/shard_map/ppermute | solution.py:480
  82.5 3.7 %collective-permute-start.9 = (bf16[2,32,512]{2,1,0:T(8,128)(2,1)S(1)}, bf16[2,32,512]{2,1,0:T(8,128)(2,1)S(1)}, u32[]{:S(2)}, u32[]{:S(2)}) collective-permute-start(bf16[2,32,512]{2,1,0:T(8,128)(2,1)S(1)} %get-tuple-element.29), channel_id=1, source_target_pairs={{0,32},{8,40},{16,48},{24,56},{32,0},{40,8},{48,16},{56,24},{1,33}... | collective-permute-start | bytes 196616 | tf_op jit(solution)/shard_map/ppermute | solution.py:480
  86.1 3.5 %collective-permute-start.10 = (bf16[2,32,512]{2,1,0:T(8,128)(2,1)S(1)}, bf16[2,32,512]{2,1,0:T(8,128)(2,1)S(1)}, u32[]{:S(2)}, u32[]{:S(2)}) collective-permute-start(bf16[2,32,512]{2,1,0:T(8,128)(2,1)S(1)} %get-tuple-element.30), channel_id=1, source_target_pairs={{0,48},{8,56},{16,0},{24,8},{32,16},{40,24},{48,32},{56,40},{1,49}... | collective-permute-start | bytes 196616 | tf_op jit(solution)/shard_map/ppermute | solution.py:480
  89.7 9.8 %collective-permute-done.8.refs_1_ = bf16[2,32,512]{2,1,0:T(8,128)(2,1)S(1)} collective-permute-done((bf16[2,32,512]{2,1,0:T(8,128)(2,1)S(1)}, bf16[2,32,512]{2,1,0:T(8,128)(2,1)S(1)}, u32[]{:S(2)}, u32[]{:S(2)}) %collective-permute-start.8) | collective-permute-done | bytes 65568 | tf_op jit(solution)/shard_map/ppermute | solution.py:480
  99.4 3.4 %collective-permute-done.9.refs_2_ = bf16[2,32,512]{2,1,0:T(8,128)(2,1)S(1)} collective-permute-done((bf16[2,32,512]{2,1,0:T(8,128)(2,1)S(1)}, bf16[2,32,512]{2,1,0:T(8,128)(2,1)S(1)}, u32[]{:S(2)}, u32[]{:S(2)}) %collective-permute-start.9) | collective-permute-done | bytes 65568 | tf_op jit(solution)/shard_map/ppermute | solution.py:480
  102.8 0.0 collective-permute-done.10.refs_3_
  102.9 0.1 collective-permute-start.11
  103.0 0.0 all-to-all-done.1
  103.0 0.1 convert_reduce_fusion.refs_0_
  103.1 2.8 %collective-permute-start.20 = (f32[32,256]{1,0:T(8,128)S(1)}, f32[32,256]{1,0:T(8,128)S(1)}, u32[]{:S(2)}, u32[]{:S(2)}) collective-permute-start(f32[32,256]{1,0:T(8,128)S(1)} %convert_reduce_fusion.refs_0_), channel_id=1, source_target_pairs={{0,192},{64,0},{128,64},{192,128},{1,193},{65,1},{129,65},{193,129... | collective-permute-start | bytes 98312 | tf_op jit(solution)/shard_map/ppermute | solution.py:529
  105.9 0.8 collective-permute-start.19
  106.7 0.9 collective-permute-start.18
  107.6 0.0 collective-permute-done.11.refs_4_
  107.6 0.8 shard_map.160
  108.4 0.0 collective-permute-done.20.refs_3_
  108.4 2.9 %collective-permute-done.19.refs_2_ = f32[32,256]{1,0:T(8,128)S(1)} collective-permute-done((f32[32,256]{1,0:T(8,128)S(1)}, f32[32,256]{1,0:T(8,128)S(1)}, u32[]{:S(2)}, u32[]{:S(2)}) %collective-permute-start.19) | collective-permute-done | bytes 32800 | tf_op jit(solution)/shard_map/ppermute | solution.py:529
  111.3 0.5 collective-permute-done.18.refs_1_
  111.8 0.6 shard_map.163
  (5 shorter events, 0.0 us)
Async XLA Ops:
  0.6 13.0 %copy-start.1 = (bf16[1,1,8,128,256]{4,3,2,1,0:T(8,128)(2,1)S(1)}, bf16[1,1,8,128,256]{4,3,2,1,0:T(8,128)(2,1)}, u32[]{:S(2)}) copy-start(bf16[1,1,8,128,256]{4,3,2,1,0:T(8,128)(2,1)} %param.17) | copy-start | bytes 1572868
  0.6 13.0 %copy-start.2 = (bf16[1,1,4,64,512]{4,3,2,1,0:T(8,128)(2,1)S(1)}, bf16[1,1,4,64,512]{4,3,2,1,0:T(8,128)(2,1)}, u32[]{:S(2)}) copy-start(bf16[1,1,4,64,512]{4,3,2,1,0:T(8,128)(2,1)} %param.23) | copy-start | bytes 786436
  0.7 2.2 %collective-permute-start = (bf16[8,128,256]{2,1,0:T(8,128)(2,1)}, bf16[8,128,256]{2,1,0:T(8,128)(2,1)S(1)}, u32[]{:S(2)}, u32[]{:S(2)}) collective-permute-start(bf16[8,128,256]{2,1,0:T(8,128)(2,1)} %bitcast.13), channel_id=1, source_target_pairs={{0,8},{8,0},{16,24},{24,16},{32,40},{40,32},{48,56},{56,48},{1,9},... | collective-permute-start | bytes 1572872 | tf_op jit(solution)/shard_map/ppermute | solution.py:476
  5.1 53.4 %all-to-all-start = ((bf16[4,2,144,256]{3,2,1,0:T(8,128)(2,1)}), bf16[4,2,144,256]{3,2,1,0:T(8,128)(2,1)S(1)}, u32[]{:S(2)}, u32[]{:S(2)}) async-start(bf16[4,2,144,256]{3,2,1,0:T(8,128)(2,1)} %shard_map.157), calls=%async_computation | async-start | bytes 1179648 | tf_op jit(solution)/shard_map/all_to_all | solution.py:487
  13.6 3.5 %collective-permute-start.12 = (bf16[8,128,256]{2,1,0:T(8,128)(2,1)S(1)}, bf16[8,128,256]{2,1,0:T(8,128)(2,1)S(1)}, u32[]{:S(2)}, u32[]{:S(2)}) collective-permute-start(bf16[8,128,256]{2,1,0:T(8,128)(2,1)S(1)} %bitcast.16), channel_id=1, source_target_pairs={{0,8},{8,0},{16,24},{24,16},{32,40},{40,32},{48,56},{56,48},{1,9},... | collective-permute-start | bytes 1572872 | tf_op jit(solution)/shard_map/ppermute | solution.py:476
  13.6 3.5 %collective-permute-start.13 = (bf16[4,64,512]{2,1,0:T(8,128)(2,1)S(1)}, bf16[4,64,512]{2,1,0:T(8,128)(2,1)S(1)}, u32[]{:S(2)}, u32[]{:S(2)}) collective-permute-start(bf16[4,64,512]{2,1,0:T(8,128)(2,1)S(1)} %bitcast.19), channel_id=1, source_target_pairs={{0,8},{8,0},{16,24},{24,16},{32,40},{40,32},{48,56},{56,48},{1,9},... | collective-permute-start | bytes 786440 | tf_op jit(solution)/shard_map/ppermute | solution.py:476
  15.0 20.0 %collective-permute-start.2 = (bf16[128,256]{1,0:T(8,128)(2,1)S(1)}, bf16[128,256]{1,0:T(8,128)(2,1)S(1)}, u32[]{:S(2)}, u32[]{:S(2)}) collective-permute-start(bf16[128,256]{1,0:T(8,128)(2,1)S(1)} %get-tuple-element.43), channel_id=1, source_target_pairs={{1,0},{2,1},{3,2},{4,3},{5,4},{6,5},{7,6},{0,7},{9,8},{10,9},{11,1... | collective-permute-start | bytes 196616 | tf_op jit(solution)/shard_map/ppermute | solution.py:491
  16.3 20.3 %collective-permute-start.1 = (bf16[128,256]{1,0:T(8,128)(2,1)S(1)}, bf16[128,256]{1,0:T(8,128)(2,1)S(1)}, u32[]{:S(2)}, u32[]{:S(2)}) collective-permute-start(bf16[128,256]{1,0:T(8,128)(2,1)S(1)} %get-tuple-element.44), channel_id=1, source_target_pairs={{0,1},{1,2},{2,3},{3,4},{4,5},{5,6},{6,7},{7,0},{8,9},{9,10},{10,1... | collective-permute-start | bytes 196616 | tf_op jit(solution)/shard_map/ppermute | solution.py:490
  18.3 49.0 %collective-permute-start.14 = (bf16[2,192,256]{2,1,0:T(8,128)(2,1)S(1)}, bf16[2,192,256]{2,1,0:T(8,128)(2,1)S(1)}, u32[]{:S(2)}, u32[]{:S(2)}) collective-permute-start(bf16[2,192,256]{2,1,0:T(8,128)(2,1)S(1)} %get-tuple-element.32), channel_id=1, source_target_pairs={{0,16},{8,24},{16,32},{24,40},{32,48},{40,56},{48,0},{56,8},{1,17}... | collective-permute-start | bytes 589832 | tf_op jit(solution)/shard_map/ppermute | solution.py:480
  21.3 46.0 %collective-permute-start.15 = (bf16[2,192,256]{2,1,0:T(8,128)(2,1)S(1)}, bf16[2,192,256]{2,1,0:T(8,128)(2,1)S(1)}, u32[]{:S(2)}, u32[]{:S(2)}) collective-permute-start(bf16[2,192,256]{2,1,0:T(8,128)(2,1)S(1)} %get-tuple-element.33), channel_id=1, source_target_pairs={{0,32},{8,40},{16,48},{24,56},{32,0},{40,8},{48,16},{56,24},{1,33}... | collective-permute-start | bytes 589832 | tf_op jit(solution)/shard_map/ppermute | solution.py:480
  24.9 42.5 %collective-permute-start.16 = (bf16[2,192,256]{2,1,0:T(8,128)(2,1)S(1)}, bf16[2,192,256]{2,1,0:T(8,128)(2,1)S(1)}, u32[]{:S(2)}, u32[]{:S(2)}) collective-permute-start(bf16[2,192,256]{2,1,0:T(8,128)(2,1)S(1)} %get-tuple-element.34), channel_id=1, source_target_pairs={{0,48},{8,56},{16,0},{24,8},{32,16},{40,24},{48,32},{56,40},{1,49}... | collective-permute-start | bytes 589832 | tf_op jit(solution)/shard_map/ppermute | solution.py:480
  35.0 1.6 %collective-permute-start.4 = (bf16[128,256]{1,0:T(8,128)(2,1)S(1)}, bf16[128,256]{1,0:T(8,128)(2,1)S(1)}, u32[]{:S(2)}, u32[]{:S(2)}) collective-permute-start(bf16[128,256]{1,0:T(8,128)(2,1)S(1)} %collective-permute-done.2.refs_1_), channel_id=1, source_target_pairs={{0,8},{8,0},{16,24},{24,16},{32,40},{40,32},{48,56},{56,48},{1,9},... | collective-permute-start | bytes 196616 | tf_op jit(solution)/shard_map/ppermute | solution.py:476
  36.6 1.3 %collective-permute-start.3 = (bf16[128,256]{1,0:T(8,128)(2,1)S(1)}, bf16[128,256]{1,0:T(8,128)(2,1)S(1)}, u32[]{:S(2)}, u32[]{:S(2)}) collective-permute-start(bf16[128,256]{1,0:T(8,128)(2,1)S(1)} %collective-permute-done.1.refs_0_), channel_id=1, source_target_pairs={{0,8},{8,0},{16,24},{24,16},{32,40},{40,32},{48,56},{56,48},{1,9},... | collective-permute-start | bytes 196616 | tf_op jit(solution)/shard_map/ppermute | solution.py:476
  38.9 14.6 %collective-permute-start.5 = (bf16[2,48,256]{2,1,0:T(8,128)(2,1)S(1)}, bf16[2,48,256]{2,1,0:T(8,128)(2,1)S(1)}, u32[]{:S(2)}, u32[]{:S(2)}) collective-permute-start(bf16[2,48,256]{2,1,0:T(8,128)(2,1)S(1)} %get-tuple-element.24), channel_id=1, source_target_pairs={{0,16},{8,24},{16,32},{24,40},{32,48},{40,56},{48,0},{56,8},{1,17}... | collective-permute-start | bytes 147464 | tf_op jit(solution)/shard_map/ppermute | solution.py:480
  41.6 14.1 %collective-permute-start.6 = (bf16[2,48,256]{2,1,0:T(8,128)(2,1)S(1)}, bf16[2,48,256]{2,1,0:T(8,128)(2,1)S(1)}, u32[]{:S(2)}, u32[]{:S(2)}) collective-permute-start(bf16[2,48,256]{2,1,0:T(8,128)(2,1)S(1)} %get-tuple-element.25), channel_id=1, source_target_pairs={{0,32},{8,40},{16,48},{24,56},{32,0},{40,8},{48,16},{56,24},{1,33}... | collective-permute-start | bytes 147464 | tf_op jit(solution)/shard_map/ppermute | solution.py:480
  53.6 5.0 %collective-permute-start.7 = (bf16[2,48,256]{2,1,0:T(8,128)(2,1)S(1)}, bf16[2,48,256]{2,1,0:T(8,128)(2,1)S(1)}, u32[]{:S(2)}, u32[]{:S(2)}) collective-permute-start(bf16[2,48,256]{2,1,0:T(8,128)(2,1)S(1)} %get-tuple-element.26), channel_id=1, source_target_pairs={{0,48},{8,56},{16,0},{24,8},{32,16},{40,24},{48,32},{56,40},{1,49}... | collective-permute-start | bytes 147464 | tf_op jit(solution)/shard_map/ppermute | solution.py:480
  58.6 0.8 copy-start
  68.3 2.0 %collective-permute-start.17 = (bf16[4,8,32,256]{3,2,1,0:T(8,128)(2,1)S(1)}, bf16[4,8,32,256]{3,2,1,0:T(8,128)(2,1)S(1)}, u32[]{:S(2)}, u32[]{:S(2)}) collective-permute-start(bf16[4,8,32,256]{3,2,1,0:T(8,128)(2,1)S(1)} %get-tuple-element.40), channel_id=1, source_target_pairs={{0,8},{8,0},{16,24},{24,16},{32,40},{40,32},{48,56},{56,48},{1,9},... | collective-permute-start | bytes 1572872 | tf_op jit(solution)/shard_map/ppermute | solution.py:476
  71.3 31.7 %all-to-all-start.1 = ((bf16[32,32,256]{2,1,0:T(8,128)(2,1)}), bf16[32,32,256]{2,1,0:T(8,128)(2,1)S(1)}, u32[]{:S(2)}, u32[]{:S(2)}) async-start(bf16[32,32,256]{2,1,0:T(8,128)(2,1)} %bitcast.8), calls=%async_computation.1 | async-start | bytes 1048576 | tf_op jit(solution)/shard_map/all_to_all | solution.py:526
  80.0 19.4 %collective-permute-start.8 = (bf16[2,32,512]{2,1,0:T(8,128)(2,1)S(1)}, bf16[2,32,512]{2,1,0:T(8,128)(2,1)S(1)}, u32[]{:S(2)}, u32[]{:S(2)}) collective-permute-start(bf16[2,32,512]{2,1,0:T(8,128)(2,1)S(1)} %get-tuple-element.28), channel_id=1, source_target_pairs={{0,16},{8,24},{16,32},{24,40},{32,48},{40,56},{48,0},{56,8},{1,17}... | collective-permute-start | bytes 196616 | tf_op jit(solution)/shard_map/ppermute | solution.py:480
  82.5 20.3 %collective-permute-start.9 = (bf16[2,32,512]{2,1,0:T(8,128)(2,1)S(1)}, bf16[2,32,512]{2,1,0:T(8,128)(2,1)S(1)}, u32[]{:S(2)}, u32[]{:S(2)}) collective-permute-start(bf16[2,32,512]{2,1,0:T(8,128)(2,1)S(1)} %get-tuple-element.29), channel_id=1, source_target_pairs={{0,32},{8,40},{16,48},{24,56},{32,0},{40,8},{48,16},{56,24},{1,33}... | collective-permute-start | bytes 196616 | tf_op jit(solution)/shard_map/ppermute | solution.py:480
  86.1 16.7 %collective-permute-start.10 = (bf16[2,32,512]{2,1,0:T(8,128)(2,1)S(1)}, bf16[2,32,512]{2,1,0:T(8,128)(2,1)S(1)}, u32[]{:S(2)}, u32[]{:S(2)}) collective-permute-start(bf16[2,32,512]{2,1,0:T(8,128)(2,1)S(1)} %get-tuple-element.30), channel_id=1, source_target_pairs={{0,48},{8,56},{16,0},{24,8},{32,16},{40,24},{48,32},{56,40},{1,49}... | collective-permute-start | bytes 196616 | tf_op jit(solution)/shard_map/ppermute | solution.py:480
  102.9 4.7 %collective-permute-start.11 = (bf16[4,32,512]{2,1,0:T(8,128)(2,1)S(1)}, bf16[4,32,512]{2,1,0:T(8,128)(2,1)S(1)}, u32[]{:S(2)}, u32[]{:S(2)}) collective-permute-start(bf16[4,32,512]{2,1,0:T(8,128)(2,1)S(1)} %pad_maximum_fusion), channel_id=1, source_target_pairs={{0,8},{8,0},{16,24},{24,16},{32,40},{40,32},{48,56},{56,48},{1,9},... | collective-permute-start | bytes 393224 | tf_op jit(solution)/shard_map/ppermute | solution.py:476
  103.1 5.3 %collective-permute-start.20 = (f32[32,256]{1,0:T(8,128)S(1)}, f32[32,256]{1,0:T(8,128)S(1)}, u32[]{:S(2)}, u32[]{:S(2)}) collective-permute-start(f32[32,256]{1,0:T(8,128)S(1)} %convert_reduce_fusion.refs_0_), channel_id=1, source_target_pairs={{0,192},{64,0},{128,64},{192,128},{1,193},{65,1},{129,65},{193,129... | collective-permute-start | bytes 98312 | tf_op jit(solution)/shard_map/ppermute | solution.py:529
  105.9 5.4 %collective-permute-start.19 = (f32[32,256]{1,0:T(8,128)S(1)}, f32[32,256]{1,0:T(8,128)S(1)}, u32[]{:S(2)}, u32[]{:S(2)}) collective-permute-start(f32[32,256]{1,0:T(8,128)S(1)} %convert_reduce_fusion.refs_0_), channel_id=1, source_target_pairs={{0,128},{64,192},{128,0},{192,64},{1,129},{65,193},{129,1},{193,65... | collective-permute-start | bytes 98312 | tf_op jit(solution)/shard_map/ppermute | solution.py:529
  106.7 5.1 %collective-permute-start.18 = (f32[32,256]{1,0:T(8,128)S(1)}, f32[32,256]{1,0:T(8,128)S(1)}, u32[]{:S(2)}, u32[]{:S(2)}) collective-permute-start(f32[32,256]{1,0:T(8,128)S(1)} %convert_reduce_fusion.refs_0_), channel_id=1, source_target_pairs={{0,64},{64,128},{128,192},{192,0},{1,65},{65,129},{129,193},{193,1... | collective-permute-start | bytes 98312 | tf_op jit(solution)/shard_map/ppermute | solution.py:529

commit v4 on v3

--- a/solution.py
+++ b/solution.py
@@ -87,14 +87,15 @@
     edges[...] = found.reshape(edges.shape)
 
 
-def pack_main_body(waits, own, partner, pick, out, edges, *, links):
-    _, core = place()
+def pack_main_body(waits, own, partner, pick, *refs, links):
+    outs, edges = refs[:links], refs[links]
+    zhi, core = place()
     for wait in waits:
         wait()
     for s, source in enumerate((own, partner)):
         find_edges(source, pick, edges)
         for k in range(links):
-            pack_piece(source, edges, out.at[k], s, 2 * k + core)
+            pack_piece(source, edges, outs[k], s, 2 * lax.rem(zhi + k, links) + core)
 
 
 def pack_main(own, partner, links):
@@ -102,17 +103,17 @@
     strip = cols // (2 * links)
     return call(
         functools.partial(pack_main_body, links=links),
-        [jax.ShapeDtypeStruct((links, 2, rows * strip + EDGES, chan), BF16)],
+        [jax.ShapeDtypeStruct((2, rows * strip + EDGES, chan), BF16)] * links,
         (own, partner, edge_picker(rows, cols, strip)),
         scratch=[pltpu.VMEM((2 * links, EDGES, chan), BF16)],
         manual=(0, 2),
-    )[0]
+    )
 
 
 def pack_halo_body(waits, *refs, links):
-    sources, pick, outs = (refs[:2], refs[2:4]), refs[4], refs[5 : 5 + links]
-    tall, edges = refs[5 + links :]
-    zhi, core = place()
+    sources, pick, out = (refs[:2], refs[2:4]), refs[4], refs[5]
+    tall, edges = refs[6:]
+    _, core = place()
     for wait in waits:
         wait()
     index = lax.axis_index("space")
@@ -122,23 +123,22 @@
         tall[1] = jnp.where(last, jnp.zeros_like(below), below[...])
         find_edges(tall, pick, edges)
         for k in range(links):
-            pack_piece(tall, edges, outs[k], s, 2 * lax.rem(zhi + k, links) + core)
+            pack_piece(tall, edges, out.at[k], s, 2 * k + core)
 
 
 def pack_halo(own, partner, links):
     cols, chan = own[0].shape
     strip = cols // (2 * links)
-    shape = jax.ShapeDtypeStruct((2, 2 * strip + EDGES, chan), BF16)
     return call(
         functools.partial(pack_halo_body, links=links),
-        [shape] * links,
+        [jax.ShapeDtypeStruct((links, 2, 2 * strip + EDGES, chan), BF16)],
         (*own, *partner, edge_picker(2, cols, strip)),
         scratch=[
             pltpu.VMEM((2, cols, chan), BF16),
             pltpu.VMEM((2 * links, EDGES, chan), BF16),
         ],
         manual=(4,),
-    )
+    )[0]
 
 
 def pack_teacher_body(waits, own_mid, partner_mid, own_top, partner_top, *outs, links):
@@ -209,8 +209,8 @@
 
 
 def encode_body(waits, *refs, links, rows, strip):
-    cells, shifts, w_spatial, parity, w_temporal, w_down, refs = (*refs[:6], refs[6:])
-    halos, refs = refs[:links], refs[links:]
+    halos, shifts, w_spatial, parity, w_temporal, w_down, refs = (*refs[:6], refs[6:])
+    cells, refs = refs[:links], refs[links:]
     w_proj, refs = refs[:4], refs[4:]
     spatial, mid_out, attended_out, student_out, refs = (*refs[:4], refs[4:])
     pieces, refs = refs[:links], refs[links:]
@@ -221,22 +221,21 @@
     width = attended_out.shape[-1]
     tall = (rows + 2) * strip
     waits[0]()
-    waits[1]()
     main = rows * strip
     for k in range(links):
         origin = lax.rem(zhi - k + links, links)
         for s in range(2):
             t = 2 * origin + (core if s == 0 else 1 - core)
-            cat[: main + EDGES] = cells[origin, s]
-            cat[main + EDGES :] = halos[k][s]
+            cat[: main + EDGES] = cells[k][s]
+            cat[main + EDGES :] = halos[origin, s]
             moved = jnp.dot(shifts[...], cat[...], preferred_element_type=F32).astype(BF16)
             grid[:, t, :, :chan] = moved[:tall].reshape(rows + 2, strip, chan)
             grid[:, t, :, 2 * chan :] = moved[tall:].reshape(rows + 2, strip, chan)
             centre = slice(chan, 2 * chan)
-            grid[0, t, :, centre] = halos[k][s, :strip]
-            grid[1 : rows + 1, t, :, centre] = cells[origin, s, :main].reshape(rows, strip, chan)
-            grid[rows + 1, t, :, centre] = halos[k][s, strip : 2 * strip]
-    waits[2]()
+            grid[0, t, :, centre] = halos[origin, s, :strip]
+            grid[1 : rows + 1, t, :, centre] = cells[k][s, :main].reshape(rows, strip, chan)
+            grid[rows + 1, t, :, centre] = halos[origin, s, strip : 2 * strip]
+    waits[1]()
     cellcount = rows * frames * strip
     conv = jnp.dot(
         grid[:rows].reshape(cellcount, 3 * chan), w_spatial[0], preferred_element_type=F32
@@ -250,7 +249,7 @@
     conv = conv / (1.0 + jnp.exp(-conv))
     spatial[:, :2] = jnp.zeros((rows, 2, strip, chan), BF16)
     spatial[:, 2:] = conv.astype(BF16).reshape(rows, frames, strip, chan)
-    for wait in waits[3:]:
+    for wait in waits[2:]:
         wait()
     acc = grid[1 : rows + 1, :, :, chan : 2 * chan].reshape(cellcount, chan).astype(F32)
     temporal = jnp.dot(
@@ -322,13 +321,13 @@
     half = strip // 2
     points = (rows // 2) * half
     args = (
-        cells,
+        halos,
         shift_pickers(rows, strip),
         w_spatial.reshape(3, 3 * chan, chan),
         parity_picker(frames, strip),
         w_temporal,
         w_down.reshape(4 * chan, width),
-        *halos,
+        *cells,
         *w_proj,
     )
     shapes = [
@@ -349,7 +348,7 @@
         args,
         scratch=scratch,
         room=32,
-        manual=(0, 1, 2, 3, 4, 5, *range(6 + links, 10 + links)),
+        manual=(1, 2, 3, 4, 5, *range(6 + links, 10 + links)),
     )
     return outs[:4], outs[4:]
 
@@ -389,7 +388,7 @@
         student[...].astype(F32) - t_top[...].reshape(frames * points, width)
     ).astype(BF16)
     g_top[...] = lax.dot_general(attended[...], diff, dims, preferred_element_type=F32) * scale_top
-    spaces = keep.shape[1]
+    spaces = 2 * keep.shape[0]
     n_mid = g_mid.shape[0] // (frames * spaces)
     n_top = g_top.shape[0] // (frames * spaces)
     for c in range(2):
@@ -400,13 +399,13 @@
                 for z in range(links):
                     for p in range(spaces):
                         shard = (2 * z + side) * spaces + p
-                        ref[z, p, :n_mid] = g_mid[shard * n_mid : (shard + 1) * n_mid].astype(
+                        ref[p // 2, z, p % 2, :n_mid] = g_mid[shard * n_mid : (shard + 1) * n_mid].astype(
                             ref.dtype
                         )
-                        ref[z, p, n_mid:16] = jnp.zeros((16 - n_mid, chan), ref.dtype)
+                        ref[p // 2, z, p % 2, n_mid:16] = jnp.zeros((16 - n_mid, chan), ref.dtype)
                         block = g_top[shard * n_top : (shard + 1) * n_top].astype(ref.dtype)
-                        ref[z, p, 16 : 16 + n_top] = block[:, :chan]
-                        ref[z, p, 16 + n_top :] = block[:, chan:]
+                        ref[p // 2, z, p % 2, 16 : 16 + n_top] = block[:, :chan]
+                        ref[p // 2, z, p % 2, 16 + n_top :] = block[:, chan:]
 
 
 def gradients(teachers, spatial, mid, attended, student, links, spaces, scale_mid, scale_top):
@@ -419,8 +418,8 @@
             gradients_body, links=links, scale_mid=scale_mid, scale_top=scale_top
         ),
         [
-            jax.ShapeDtypeStruct((links, spaces, height, chan), F32),
-            jax.ShapeDtypeStruct((links, spaces, height, chan), BF16),
+            jax.ShapeDtypeStruct((spaces // 2, links, 2, height, chan), F32),
+            jax.ShapeDtypeStruct((spaces // 2, links, 2, height, chan), BF16),
         ],
         (*teachers, spatial, mid, attended, student),
         scratch=[
@@ -490,10 +489,10 @@
     above = lax.ppermute(own[rows - 1], "space", ring)
     below = lax.ppermute(own[0], "space", [(j, i) for i, j in ring])
     cells = pack_main(own, swap(own), links)
-    cells = gather(cells)
+    cells = spread(cells)
     other = (swap(above), swap(below))
     halo = pack_halo((above, below), other, links)
-    halos = spread(halo)
+    halos = gather(halo)
     t_mid, t_top = teacher_mid[0, 0], teacher_top[0, 0]
     teachers = pack_teacher(t_mid, swap(t_mid), t_top, swap(t_top), links)
     teachers = spread(teachers)
@@ -519,9 +518,14 @@
         1.0 / math.sqrt(points * frames * devices_all),
     )
     part = (keep + swap(give).astype(F32)).astype(BF16)
-    part = part.reshape(links * spaces, *part.shape[2:])
+    lines = [list(range(a, spaces, 2)) for a in range(2)]
+    part = lax.all_to_all(part, "space", 0, 0, axis_index_groups=lines, tiled=True)
+    part = jnp.sum(part.astype(F32), 0).astype(BF16)
+    part = part.reshape(frames, *part.shape[2:])
     groups = [
-        [(2 * z + c) * spaces + p for z in range(links) for p in range(spaces)] for c in range(2)
+        [(2 * z + c) * spaces + p + a for z in range(links) for a in range(2)]
+        for c in range(2)
+        for p in range(0, spaces, 2)
     ]
     part = lax.all_to_all(part, ("tm", "space"), 0, 0, axis_index_groups=groups, tiled=True)
     part = jnp.sum(part.astype(F32), 0)

time: 113 us -> 118 us (1.044)
  the two profiles are of different devices: /device:TPU:24 before, /device:TPU:4 now
where the time goes in v4:
time: 118 us; the launch traced here: 116 us
  starting transfers between devices  46.3 us (39%)
  waiting for transfers between devices  39.7 us (34%)
  Pallas kernels  14.5 us (12%)
  blocking collectives  12.5 us (11%)
    ppermute x9, waiting for transfers between devices, spread(): lax.ppermute(pieces[k], 'tm', [(i, (i + 2 * k) % frames) for i in range(f...  27.1 us
    ppermute x9, starting transfers between devices, spread(): lax.ppermute(pieces[k], 'tm', [(i, (i + 2 * k) % frames) for i in range(f...  26.5 us
    pallas_call x7, Pallas kernels, call(): pl.pallas_call(run, out_shape=out_shape, in_specs=specs, out_specs=outs,...  14.5 us
    all_to_all x1, blocking collectives, local(): lax.all_to_all(part, 'space', 0, 0, axis_index_groups=lines, tiled=True)  12.5 us
    all_to_all x1, starting transfers between devices, gather(): lax.all_to_all(pieces, 'tm', 0, 0, axis_index_groups=columns, tiled=True)  5.76 us
    all_to_all x1, starting transfers between devices, local(): lax.all_to_all(part, ('tm', 'space'), 0, 0, axis_index_groups=groups, til...  5.33 us
    ppermute x1, starting transfers between devices, local(): below = lax.ppermute(own[0], 'space', [(j, i) for i, j in ring])  4.44 us
    ppermute x1, waiting for transfers between devices, local(): above = lax.ppermute(own[rows - 1], 'space', ring)  3.89 us
  transfers between devices with their start and end apart: 23, of which 9 were waited for; matrix products, arithmetic and copies ran while one was open for 1% of the time, Pallas kernels for 11%

profile of v4, /device:TPU:4, one launch (start us, length us, event | category | flops | bytes accessed | tf_op | source)
XLA Modules:
  0.0 115.6 jit_solution(16640223367865716761)
XLA Ops:
  0.6 0.1 collective-permute-start.4
  0.7 0.5 collective-permute-start.12
  1.2 0.1 collective-permute-start.13
  1.3 0.9 slice_bitcast_fusion
  2.2 4.4 %collective-permute-start.1 = (bf16[128,256]{1,0:T(8,128)(2,1)S(1)}, bf16[128,256]{1,0:T(8,128)(2,1)S(1)}, u32[]{:S(2)}, u32[]{:S(2)}) collective-permute-start(bf16[128,256]{1,0:T(8,128)(2,1)S(1)} %get-tuple-element.43), channel_id=1, source_target_pairs={{1,0},{2,1},{3,2},{4,3},{5,4},{6,5},{7,6},{0,7},{9,8},{10,9},{11,1... | collective-permute-start | bytes 196616 | tf_op jit(solution)/shard_map/ppermute | solution.py:490
  6.7 0.0 collective-permute-start
  6.7 2.5 %collective-permute-done.1.refs_1_ = bf16[128,256]{1,0:T(8,128)(2,1)S(1)} collective-permute-done((bf16[128,256]{1,0:T(8,128)(2,1)S(1)}, bf16[128,256]{1,0:T(8,128)(2,1)S(1)}, u32[]{:S(2)}, u32[]{:S(2)}) %collective-permute-start.1) | collective-permute-done | bytes 65568 | tf_op jit(solution)/shard_map/ppermute | solution.py:490
  9.1 0.0 collective-permute-start.3
  9.1 3.9 %collective-permute-done.refs_0_ = bf16[128,256]{1,0:T(8,128)(2,1)S(1)} collective-permute-done((bf16[128,256]{1,0:T(8,128)(2,1)S(1)}, bf16[128,256]{1,0:T(8,128)(2,1)S(1)}, u32[]{:S(2)}, u32[]{:S(2)}) %collective-permute-start) | collective-permute-done | bytes 65568 | tf_op jit(solution)/shard_map/ppermute | solution.py:489
  13.0 0.0 collective-permute-start.2
  13.0 0.0 collective-permute-done.3.refs_3_
  13.0 1.2 %collective-permute-done.2.refs_2_ = bf16[128,256]{1,0:T(8,128)(2,1)S(1)} collective-permute-done((bf16[128,256]{1,0:T(8,128)(2,1)S(1)}, bf16[128,256]{1,0:T(8,128)(2,1)S(1)}, u32[]{:S(2)}, u32[]{:S(2)}) %collective-permute-start.2) | collective-permute-done | bytes 65568 | tf_op jit(solution)/shard_map/ppermute | solution.py:475
  14.3 1.7 %shard_map.157 = bf16[4,2,48,256]{3,2,1,0:T(8,128)(2,1)} custom-call(bf16[128,256]{1,0:T(8,128)(2,1)S(1)} %collective-permute-done.refs_0_, bf16[128,256]{1,0:T(8,128)(2,1)S(1)} %collective-permute-done.1.refs_1_, bf16[128,256]{1,0:T(8,128)(2,1)S(1)} %collective-permute-done.2.refs_2_, bf16[128,256]{1,0:T(8,128)(2,1)S(1)} %collective-permute-done.3.refs_3_, ...), custom_call_target="tpu_custom_call" | custom-call | tf_op jit(solution)/shard_map/pallas_call | solution.py:40
  16.0 0.0 collective-permute-done.4.refs_1_
  16.0 1.5 %shard_map.158 = (bf16[2,144,256]{2,1,0:T(8,128)(2,1)S(1)}, bf16[2,144,256]{2,1,0:T(8,128)(2,1)S(1)}, bf16[2,144,256]{2,1,0:T(8,128)(2,1)S(1)}, bf16[2,144,256]{2,1,0:T(8,128)(2,1)S(1)}) custom-call(bf16[8,128,256]{2,1,0:T(8,128)(2,1)} %bitcast.14, bf16[8,128,256]{2,1,0:T(8,128)(2,1)S(1)} %collective-permute-done.4.refs_1_, ...), custom_call_target="tpu_custom_call" | custom-call | tf_op jit(solution)/shard_map/pallas_call | solution.py:40
  17.5 3.3 %collective-permute-start.5 = (bf16[2,144,256]{2,1,0:T(8,128)(2,1)S(1)}, bf16[2,144,256]{2,1,0:T(8,128)(2,1)S(1)}, u32[]{:S(2)}, u32[]{:S(2)}) collective-permute-start(bf16[2,144,256]{2,1,0:T(8,128)(2,1)S(1)} %get-tuple-element.24), channel_id=1, source_target_pairs={{0,16},{8,24},{16,32},{24,40},{32,48},{40,56},{48,0},{56,8},{1,17}... | collective-permute-start | bytes 442376 | tf_op jit(solution)/shard_map/ppermute | solution.py:479
  20.9 5.8 %all-to-all-start = ((bf16[4,2,48,256]{3,2,1,0:T(8,128)(2,1)}), bf16[4,2,48,256]{3,2,1,0:T(8,128)(2,1)S(1)}, u32[]{:S(2)}, u32[]{:S(2)}) async-start(bf16[4,2,48,256]{3,2,1,0:T(8,128)(2,1)} %shard_map.157), calls=%async_computation | async-start | bytes 393216 | tf_op jit(solution)/shard_map/all_to_all | solution.py:486
  26.6 0.0 collective-permute-done.13.refs_3_
  26.6 0.0 collective-permute-done.12.refs_1_
  26.6 1.2 %shard_map.161 = (bf16[2,192,256]{2,1,0:T(8,128)(2,1)S(1)}, bf16[2,192,256]{2,1,0:T(8,128)(2,1)S(1)}, bf16[2,192,256]{2,1,0:T(8,128)(2,1)S(1)}, bf16[2,192,256]{2,1,0:T(8,128)(2,1)S(1)}) custom-call(bf16[8,128,256]{2,1,0:T(8,128)(2,1)} %bitcast.16, bf16[8,128,256]{2,1,0:T(8,128)(2,1)S(1)} %collective-permute-done.12.refs_1_, bf16[4,64,512]{2,1,0:T(8,128)(2,1)} %bitcast.19, ...), custom_call_target="tpu_custom_call" | custom-call | tf_op jit(solution)/shard_map/pallas_call | solution.py:40
  27.9 3.0 %collective-permute-start.14 = (bf16[2,192,256]{2,1,0:T(8,128)(2,1)S(1)}, bf16[2,192,256]{2,1,0:T(8,128)(2,1)S(1)}, u32[]{:S(2)}, u32[]{:S(2)}) collective-permute-start(bf16[2,192,256]{2,1,0:T(8,128)(2,1)S(1)} %get-tuple-element.32), channel_id=1, source_target_pairs={{0,16},{8,24},{16,32},{24,40},{32,48},{40,56},{48,0},{56,8},{1,17}... | collective-permute-start | bytes 589832 | tf_op jit(solution)/shard_map/ppermute | solution.py:479
  30.8 3.6 %collective-permute-start.15 = (bf16[2,192,256]{2,1,0:T(8,128)(2,1)S(1)}, bf16[2,192,256]{2,1,0:T(8,128)(2,1)S(1)}, u32[]{:S(2)}, u32[]{:S(2)}) collective-permute-start(bf16[2,192,256]{2,1,0:T(8,128)(2,1)S(1)} %get-tuple-element.33), channel_id=1, source_target_pairs={{0,32},{8,40},{16,48},{24,56},{32,0},{40,8},{48,16},{56,24},{1,33}... | collective-permute-start | bytes 589832 | tf_op jit(solution)/shard_map/ppermute | solution.py:479
  34.4 3.6 %collective-permute-start.16 = (bf16[2,192,256]{2,1,0:T(8,128)(2,1)S(1)}, bf16[2,192,256]{2,1,0:T(8,128)(2,1)S(1)}, u32[]{:S(2)}, u32[]{:S(2)}) collective-permute-start(bf16[2,192,256]{2,1,0:T(8,128)(2,1)S(1)} %get-tuple-element.34), channel_id=1, source_target_pairs={{0,48},{8,56},{16,0},{24,8},{32,16},{40,24},{48,32},{56,40},{1,49}... | collective-permute-start | bytes 589832 | tf_op jit(solution)/shard_map/ppermute | solution.py:479
  38.0 0.1 collective-permute-start.6
  38.1 0.0 collective-permute-done.5.refs_7_
  38.1 2.8 %collective-permute-start.7 = (bf16[2,144,256]{2,1,0:T(8,128)(2,1)S(1)}, bf16[2,144,256]{2,1,0:T(8,128)(2,1)S(1)}, u32[]{:S(2)}, u32[]{:S(2)}) collective-permute-start(bf16[2,144,256]{2,1,0:T(8,128)(2,1)S(1)} %get-tuple-element.26), channel_id=1, source_target_pairs={{0,48},{8,56},{16,0},{24,8},{32,16},{40,24},{48,32},{56,40},{1,49}... | collective-permute-start | bytes 442376 | tf_op jit(solution)/shard_map/ppermute | solution.py:479
  40.9 0.0 all-to-all-done.refs_0_
  40.9 15.6 %collective-permute-done.6.refs_8_ = bf16[2,144,256]{2,1,0:T(8,128)(2,1)S(1)} collective-permute-done((bf16[2,144,256]{2,1,0:T(8,128)(2,1)S(1)}, bf16[2,144,256]{2,1,0:T(8,128)(2,1)S(1)}, u32[]{:S(2)}, u32[]{:S(2)}) %collective-permute-start.6) | collective-permute-done | bytes 147488 | tf_op jit(solution)/shard_map/ppermute | solution.py:479
  56.5 7.7 %collective-permute-done.7.refs_9_ = bf16[2,144,256]{2,1,0:T(8,128)(2,1)S(1)} collective-permute-done((bf16[2,144,256]{2,1,0:T(8,128)(2,1)S(1)}, bf16[2,144,256]{2,1,0:T(8,128)(2,1)S(1)}, u32[]{:S(2)}, u32[]{:S(2)}) %collective-permute-start.7) | collective-permute-done | bytes 147488 | tf_op jit(solution)/shard_map/ppermute | solution.py:479
  64.3 7.8 %shard_map.159 = (bf16[8,10,16,256]{3,2,1,0:T(8,128)(2,1)S(1)}, bf16[1024,256]{1,0:T(8,128)(2,1)S(1)}, bf16[256,512]{1,0:T(8,128)(2,1)S(1)}, bf16[256,512]{1,0:T...) custom-call(bf16[4,2,48,256]{3,2,1,0:T(8,128)(2,1)S(1)} %all-to-all-, ...), custom_call_target="tpu_custom_call" | custom-call | tf_op jit(solution)/shard_map/pallas_call | solution.py:40
  72.1 0.0 collective-permute-done.14.refs_1_
  72.1 0.0 collective-permute-done.15.refs_2_
  72.1 0.0 collective-permute-done.16.refs_3_
  72.1 0.9 shard_map.162
  73.0 0.1 collective-permute-start.17
  73.1 1.9 %collective-permute-done.17 = bf16[4,4,2,32,256]{4,3,2,1,0:T(8,128)(2,1)S(1)} collective-permute-done((bf16[4,4,2,32,256]{4,3,2,1,0:T(8,128)(2,1)S(1)}, bf16[4,4,2,32,256]{4,3,2,1,0:T(8,128)(2,1)S(1)}, u32[]{:S(2)}, u32[]{:S(2)}) %collective-permute-start.17) | collective-permute-done | bytes 524320 | tf_op jit(solution)/shard_map/ppermute | solution.py:475
  75.0 0.2 add_convert_fusion
  75.2 12.5 %all_to_all.15 = bf16[4,4,2,32,256]{4,3,2,1,0:T(8,128)(2,1)S(1)} all-to-all(bf16[4,4,2,32,256]{4,3,2,1,0:T(8,128)(2,1)S(1)} %add_convert_fusion), channel_id=1, replica_groups={{0,2,4,6},{1,3,5,7},{8,10,12,14},{9,11,13,15},{16,18,20,22},{17,19,21,2..., dimensions={0} | all-to-all | bytes 1048576 | tf_op jit(solution)/shard_map/all_to_all | solution.py:522
  87.7 0.7 reduce_sum.21
  88.4 5.3 %all-to-all-start.2 = ((bf16[8,32,256]{2,1,0:T(8,128)(2,1)}), bf16[8,32,256]{2,1,0:T(8,128)(2,1)S(1)}, u32[]{:S(2)}, u32[]{:S(2)}) async-start(bf16[8,32,256]{2,1,0:T(8,128)(2,1)} %bitcast.8), calls=%async_computation.2 | async-start | bytes 262144 | tf_op jit(solution)/shard_map/all_to_all | solution.py:530
  93.8 2.9 %collective-permute-start.8 = (bf16[2,32,512]{2,1,0:T(8,128)(2,1)S(1)}, bf16[2,32,512]{2,1,0:T(8,128)(2,1)S(1)}, u32[]{:S(2)}, u32[]{:S(2)}) collective-permute-start(bf16[2,32,512]{2,1,0:T(8,128)(2,1)S(1)} %get-tuple-element.28), channel_id=1, source_target_pairs={{0,16},{8,24},{16,32},{24,40},{32,48},{40,56},{48,0},{56,8},{1,17}... | collective-permute-start | bytes 196616 | tf_op jit(solution)/shard_map/ppermute | solution.py:479
  96.7 3.6 %collective-permute-start.9 = (bf16[2,32,512]{2,1,0:T(8,128)(2,1)S(1)}, bf16[2,32,512]{2,1,0:T(8,128)(2,1)S(1)}, u32[]{:S(2)}, u32[]{:S(2)}) collective-permute-start(bf16[2,32,512]{2,1,0:T(8,128)(2,1)S(1)} %get-tuple-element.29), channel_id=1, source_target_pairs={{0,32},{8,40},{16,48},{24,56},{32,0},{40,8},{48,16},{56,24},{1,33}... | collective-permute-start | bytes 196616 | tf_op jit(solution)/shard_map/ppermute | solution.py:479
  100.3 3.6 %collective-permute-start.10 = (bf16[2,32,512]{2,1,0:T(8,128)(2,1)S(1)}, bf16[2,32,512]{2,1,0:T(8,128)(2,1)S(1)}, u32[]{:S(2)}, u32[]{:S(2)}) collective-permute-start(bf16[2,32,512]{2,1,0:T(8,128)(2,1)S(1)} %get-tuple-element.30), channel_id=1, source_target_pairs={{0,48},{8,56},{16,0},{24,8},{32,16},{40,24},{48,32},{56,40},{1,49}... | collective-permute-start | bytes 196616 | tf_op jit(solution)/shard_map/ppermute | solution.py:479
  103.8 0.0 collective-permute-done.8.refs_1_
  103.8 3.7 %collective-permute-done.9.refs_2_ = bf16[2,32,512]{2,1,0:T(8,128)(2,1)S(1)} collective-permute-done((bf16[2,32,512]{2,1,0:T(8,128)(2,1)S(1)}, bf16[2,32,512]{2,1,0:T(8,128)(2,1)S(1)}, u32[]{:S(2)}, u32[]{:S(2)}) %collective-permute-start.9) | collective-permute-done | bytes 65568 | tf_op jit(solution)/shard_map/ppermute | solution.py:479
  107.5 0.0 collective-permute-done.10.refs_3_
  107.6 0.1 collective-permute-start.11
  107.7 0.0 all-to-all-done.2
  107.7 0.6 collective-permute-start.20
  108.3 2.7 %collective-permute-start.19 = (f32[32,256]{1,0:T(8,128)S(1)}, f32[32,256]{1,0:T(8,128)S(1)}, u32[]{:S(2)}, u32[]{:S(2)}) collective-permute-start(f32[32,256]{1,0:T(8,128)S(1)} %convert_reduce_fusion.refs_0_), channel_id=1, source_target_pairs={{0,128},{64,192},{128,0},{192,64},{1,129},{65,193},{129,1},{193,65... | collective-permute-start | bytes 98312 | tf_op jit(solution)/shard_map/ppermute | solution.py:533
  111.1 0.0 collective-permute-start.18
  111.1 0.0 collective-permute-done.11.refs_4_
  111.1 0.8 shard_map.160
  111.9 0.0 collective-permute-done.20.refs_3_
  111.9 2.2 %collective-permute-done.19.refs_2_ = f32[32,256]{1,0:T(8,128)S(1)} collective-permute-done((f32[32,256]{1,0:T(8,128)S(1)}, f32[32,256]{1,0:T(8,128)S(1)}, u32[]{:S(2)}, u32[]{:S(2)}) %collective-permute-start.19) | collective-permute-done | bytes 32800 | tf_op jit(solution)/shard_map/ppermute | solution.py:533
  114.1 0.9 collective-permute-done.18.refs_1_
  115.0 0.6 shard_map.163
  (6 shorter events, 0.1 us)
Async XLA Ops:
  0.6 15.4 %collective-permute-start.4 = (bf16[8,128,256]{2,1,0:T(8,128)(2,1)}, bf16[8,128,256]{2,1,0:T(8,128)(2,1)S(1)}, u32[]{:S(2)}, u32[]{:S(2)}) collective-permute-start(bf16[8,128,256]{2,1,0:T(8,128)(2,1)} %bitcast.13), channel_id=1, source_target_pairs={{0,8},{8,0},{16,24},{24,16},{32,40},{40,32},{48,56},{56,48},{1,9},... | collective-permute-start | bytes 1572872 | tf_op jit(solution)/shard_map/ppermute | solution.py:475
  0.7 25.9 %collective-permute-start.12 = (bf16[8,128,256]{2,1,0:T(8,128)(2,1)}, bf16[8,128,256]{2,1,0:T(8,128)(2,1)S(1)}, u32[]{:S(2)}, u32[]{:S(2)}) collective-permute-start(bf16[8,128,256]{2,1,0:T(8,128)(2,1)} %bitcast.15), channel_id=1, source_target_pairs={{0,8},{8,0},{16,24},{24,16},{32,40},{40,32},{48,56},{56,48},{1,9},... | collective-permute-start | bytes 1572872 | tf_op jit(solution)/shard_map/ppermute | solution.py:475
  1.2 25.4 %collective-permute-start.13 = (bf16[4,64,512]{2,1,0:T(8,128)(2,1)}, bf16[4,64,512]{2,1,0:T(8,128)(2,1)S(1)}, u32[]{:S(2)}, u32[]{:S(2)}) collective-permute-start(bf16[4,64,512]{2,1,0:T(8,128)(2,1)} %bitcast.18), channel_id=1, source_target_pairs={{0,8},{8,0},{16,24},{24,16},{32,40},{40,32},{48,56},{56,48},{1,9},... | collective-permute-start | bytes 786440 | tf_op jit(solution)/shard_map/ppermute | solution.py:475
  2.2 6.9 %collective-permute-start.1 = (bf16[128,256]{1,0:T(8,128)(2,1)S(1)}, bf16[128,256]{1,0:T(8,128)(2,1)S(1)}, u32[]{:S(2)}, u32[]{:S(2)}) collective-permute-start(bf16[128,256]{1,0:T(8,128)(2,1)S(1)} %get-tuple-element.43), channel_id=1, source_target_pairs={{1,0},{2,1},{3,2},{4,3},{5,4},{6,5},{7,6},{0,7},{9,8},{10,9},{11,1... | collective-permute-start | bytes 196616 | tf_op jit(solution)/shard_map/ppermute | solution.py:490
  6.7 6.4 %collective-permute-start = (bf16[128,256]{1,0:T(8,128)(2,1)S(1)}, bf16[128,256]{1,0:T(8,128)(2,1)S(1)}, u32[]{:S(2)}, u32[]{:S(2)}) collective-permute-start(bf16[128,256]{1,0:T(8,128)(2,1)S(1)} %get-tuple-element.44), channel_id=1, source_target_pairs={{0,1},{1,2},{2,3},{3,4},{4,5},{5,6},{6,7},{7,0},{8,9},{9,10},{10,1... | collective-permute-start | bytes 196616 | tf_op jit(solution)/shard_map/ppermute | solution.py:489
  9.1 3.9 %collective-permute-start.3 = (bf16[128,256]{1,0:T(8,128)(2,1)S(1)}, bf16[128,256]{1,0:T(8,128)(2,1)S(1)}, u32[]{:S(2)}, u32[]{:S(2)}) collective-permute-start(bf16[128,256]{1,0:T(8,128)(2,1)S(1)} %collective-permute-done.1.refs_1_), channel_id=1, source_target_pairs={{0,8},{8,0},{16,24},{24,16},{32,40},{40,32},{48,56},{56,48},{1,9},... | collective-permute-start | bytes 196616 | tf_op jit(solution)/shard_map/ppermute | solution.py:475
  13.0 1.3 %collective-permute-start.2 = (bf16[128,256]{1,0:T(8,128)(2,1)S(1)}, bf16[128,256]{1,0:T(8,128)(2,1)S(1)}, u32[]{:S(2)}, u32[]{:S(2)}) collective-permute-start(bf16[128,256]{1,0:T(8,128)(2,1)S(1)} %collective-permute-done.refs_0_), channel_id=1, source_target_pairs={{0,8},{8,0},{16,24},{24,16},{32,40},{40,32},{48,56},{56,48},{1,9},... | collective-permute-start | bytes 196616 | tf_op jit(solution)/shard_map/ppermute | solution.py:475
  17.5 20.6 %collective-permute-start.5 = (bf16[2,144,256]{2,1,0:T(8,128)(2,1)S(1)}, bf16[2,144,256]{2,1,0:T(8,128)(2,1)S(1)}, u32[]{:S(2)}, u32[]{:S(2)}) collective-permute-start(bf16[2,144,256]{2,1,0:T(8,128)(2,1)S(1)} %get-tuple-element.24), channel_id=1, source_target_pairs={{0,16},{8,24},{16,32},{24,40},{32,48},{40,56},{48,0},{56,8},{1,17}... | collective-permute-start | bytes 442376 | tf_op jit(solution)/shard_map/ppermute | solution.py:479
  20.9 20.1 %all-to-all-start = ((bf16[4,2,48,256]{3,2,1,0:T(8,128)(2,1)}), bf16[4,2,48,256]{3,2,1,0:T(8,128)(2,1)S(1)}, u32[]{:S(2)}, u32[]{:S(2)}) async-start(bf16[4,2,48,256]{3,2,1,0:T(8,128)(2,1)} %shard_map.157), calls=%async_computation | async-start | bytes 393216 | tf_op jit(solution)/shard_map/all_to_all | solution.py:486
  27.9 44.2 %collective-permute-start.14 = (bf16[2,192,256]{2,1,0:T(8,128)(2,1)S(1)}, bf16[2,192,256]{2,1,0:T(8,128)(2,1)S(1)}, u32[]{:S(2)}, u32[]{:S(2)}) collective-permute-start(bf16[2,192,256]{2,1,0:T(8,128)(2,1)S(1)} %get-tuple-element.32), channel_id=1, source_target_pairs={{0,16},{8,24},{16,32},{24,40},{32,48},{40,56},{48,0},{56,8},{1,17}... | collective-permute-start | bytes 589832 | tf_op jit(solution)/shard_map/ppermute | solution.py:479
  30.8 41.2 %collective-permute-start.15 = (bf16[2,192,256]{2,1,0:T(8,128)(2,1)S(1)}, bf16[2,192,256]{2,1,0:T(8,128)(2,1)S(1)}, u32[]{:S(2)}, u32[]{:S(2)}) collective-permute-start(bf16[2,192,256]{2,1,0:T(8,128)(2,1)S(1)} %get-tuple-element.33), channel_id=1, source_target_pairs={{0,32},{8,40},{16,48},{24,56},{32,0},{40,8},{48,16},{56,24},{1,33}... | collective-permute-start | bytes 589832 | tf_op jit(solution)/shard_map/ppermute | solution.py:479
  34.4 37.7 %collective-permute-start.16 = (bf16[2,192,256]{2,1,0:T(8,128)(2,1)S(1)}, bf16[2,192,256]{2,1,0:T(8,128)(2,1)S(1)}, u32[]{:S(2)}, u32[]{:S(2)}) collective-permute-start(bf16[2,192,256]{2,1,0:T(8,128)(2,1)S(1)} %get-tuple-element.34), channel_id=1, source_target_pairs={{0,48},{8,56},{16,0},{24,8},{32,16},{40,24},{48,32},{56,40},{1,49}... | collective-permute-start | bytes 589832 | tf_op jit(solution)/shard_map/ppermute | solution.py:479
  38.0 18.6 %collective-permute-start.6 = (bf16[2,144,256]{2,1,0:T(8,128)(2,1)S(1)}, bf16[2,144,256]{2,1,0:T(8,128)(2,1)S(1)}, u32[]{:S(2)}, u32[]{:S(2)}) collective-permute-start(bf16[2,144,256]{2,1,0:T(8,128)(2,1)S(1)} %get-tuple-element.25), channel_id=1, source_target_pairs={{0,32},{8,40},{16,48},{24,56},{32,0},{40,8},{48,16},{56,24},{1,33}... | collective-permute-start | bytes 442376 | tf_op jit(solution)/shard_map/ppermute | solution.py:479
  38.1 26.2 %collective-permute-start.7 = (bf16[2,144,256]{2,1,0:T(8,128)(2,1)S(1)}, bf16[2,144,256]{2,1,0:T(8,128)(2,1)S(1)}, u32[]{:S(2)}, u32[]{:S(2)}) collective-permute-start(bf16[2,144,256]{2,1,0:T(8,128)(2,1)S(1)} %get-tuple-element.26), channel_id=1, source_target_pairs={{0,48},{8,56},{16,0},{24,8},{32,16},{40,24},{48,32},{56,40},{1,49}... | collective-permute-start | bytes 442376 | tf_op jit(solution)/shard_map/ppermute | solution.py:479
  73.0 2.0 %collective-permute-start.17 = (bf16[4,4,2,32,256]{4,3,2,1,0:T(8,128)(2,1)S(1)}, bf16[4,4,2,32,256]{4,3,2,1,0:T(8,128)(2,1)S(1)}, u32[]{:S(2)}, u32[]{:S(2)}) collective-permute-start(bf16[4,4,2,32,256]{4,3,2,1,0:T(8,128)(2,1)S(1)} %get-tuple-element.40), channel_id=1, source_target_pairs={{0,8},{8,0},{16,24},{24,16},{32,40},{40,32},{48,56},{56,48},{1,9},... | collective-permute-start | bytes 1572872 | tf_op jit(solution)/shard_map/ppermute | solution.py:475
  88.4 19.3 %all-to-all-start.2 = ((bf16[8,32,256]{2,1,0:T(8,128)(2,1)}), bf16[8,32,256]{2,1,0:T(8,128)(2,1)S(1)}, u32[]{:S(2)}, u32[]{:S(2)}) async-start(bf16[8,32,256]{2,1,0:T(8,128)(2,1)} %bitcast.8), calls=%async_computation.2 | async-start | bytes 262144 | tf_op jit(solution)/shard_map/all_to_all | solution.py:530
  93.8 10.1 %collective-permute-start.8 = (bf16[2,32,512]{2,1,0:T(8,128)(2,1)S(1)}, bf16[2,32,512]{2,1,0:T(8,128)(2,1)S(1)}, u32[]{:S(2)}, u32[]{:S(2)}) collective-permute-start(bf16[2,32,512]{2,1,0:T(8,128)(2,1)S(1)} %get-tuple-element.28), channel_id=1, source_target_pairs={{0,16},{8,24},{16,32},{24,40},{32,48},{40,56},{48,0},{56,8},{1,17}... | collective-permute-start | bytes 196616 | tf_op jit(solution)/shard_map/ppermute | solution.py:479
  96.7 10.9 %collective-permute-start.9 = (bf16[2,32,512]{2,1,0:T(8,128)(2,1)S(1)}, bf16[2,32,512]{2,1,0:T(8,128)(2,1)S(1)}, u32[]{:S(2)}, u32[]{:S(2)}) collective-permute-start(bf16[2,32,512]{2,1,0:T(8,128)(2,1)S(1)} %get-tuple-element.29), channel_id=1, source_target_pairs={{0,32},{8,40},{16,48},{24,56},{32,0},{40,8},{48,16},{56,24},{1,33}... | collective-permute-start | bytes 196616 | tf_op jit(solution)/shard_map/ppermute | solution.py:479
  100.3 7.3 %collective-permute-start.10 = (bf16[2,32,512]{2,1,0:T(8,128)(2,1)S(1)}, bf16[2,32,512]{2,1,0:T(8,128)(2,1)S(1)}, u32[]{:S(2)}, u32[]{:S(2)}) collective-permute-start(bf16[2,32,512]{2,1,0:T(8,128)(2,1)S(1)} %get-tuple-element.30), channel_id=1, source_target_pairs={{0,48},{8,56},{16,0},{24,8},{32,16},{40,24},{48,32},{56,40},{1,49}... | collective-permute-start | bytes 196616 | tf_op jit(solution)/shard_map/ppermute | solution.py:479
  107.6 3.5 %collective-permute-start.11 = (bf16[4,32,512]{2,1,0:T(8,128)(2,1)S(1)}, bf16[4,32,512]{2,1,0:T(8,128)(2,1)S(1)}, u32[]{:S(2)}, u32[]{:S(2)}) collective-permute-start(bf16[4,32,512]{2,1,0:T(8,128)(2,1)S(1)} %pad_maximum_fusion), channel_id=1, source_target_pairs={{0,8},{8,0},{16,24},{24,16},{32,40},{40,32},{48,56},{56,48},{1,9},... | collective-permute-start | bytes 393224 | tf_op jit(solution)/shard_map/ppermute | solution.py:475
  107.7 4.1 %collective-permute-start.20 = (f32[32,256]{1,0:T(8,128)S(1)}, f32[32,256]{1,0:T(8,128)S(1)}, u32[]{:S(2)}, u32[]{:S(2)}) collective-permute-start(f32[32,256]{1,0:T(8,128)S(1)} %convert_reduce_fusion.refs_0_), channel_id=1, source_target_pairs={{0,192},{64,0},{128,64},{192,128},{1,193},{65,1},{129,65},{193,129... | collective-permute-start | bytes 98312 | tf_op jit(solution)/shard_map/ppermute | solution.py:533
  108.3 5.7 %collective-permute-start.19 = (f32[32,256]{1,0:T(8,128)S(1)}, f32[32,256]{1,0:T(8,128)S(1)}, u32[]{:S(2)}, u32[]{:S(2)}) collective-permute-start(f32[32,256]{1,0:T(8,128)S(1)} %convert_reduce_fusion.refs_0_), channel_id=1, source_target_pairs={{0,128},{64,192},{128,0},{192,64},{1,129},{65,193},{129,1},{193,65... | collective-permute-start | bytes 98312 | tf_op jit(solution)/shard_map/ppermute | solution.py:533
  111.1 3.9 %collective-permute-start.18 = (f32[32,256]{1,0:T(8,128)S(1)}, f32[32,256]{1,0:T(8,128)S(1)}, u32[]{:S(2)}, u32[]{:S(2)}) collective-permute-start(f32[32,256]{1,0:T(8,128)S(1)} %convert_reduce_fusion.refs_0_), channel_id=1, source_target_pairs={{0,64},{64,128},{128,192},{192,0},{1,65},{65,129},{129,193},{193,1... | collective-permute-start | bytes 98312 | tf_op jit(solution)/shard_map/ppermute | solution.py:533

commit v5 on v4

--- a/solution.py
+++ b/solution.py
@@ -12,6 +12,7 @@
 
 F32 = jnp.float32
 BF16 = jnp.bfloat16
+LANES = 128
 
 
 def call(body, out_shape, args, scratch=(), room=8, manual=()):
@@ -399,27 +400,29 @@
                 for z in range(links):
                     for p in range(spaces):
                         shard = (2 * z + side) * spaces + p
-                        ref[p // 2, z, p % 2, :n_mid] = g_mid[shard * n_mid : (shard + 1) * n_mid].astype(
-                            ref.dtype
-                        )
-                        ref[p // 2, z, p % 2, n_mid:16] = jnp.zeros((16 - n_mid, chan), ref.dtype)
-                        block = g_top[shard * n_top : (shard + 1) * n_top].astype(ref.dtype)
-                        ref[p // 2, z, p % 2, 16 : 16 + n_top] = block[:, :chan]
-                        ref[p // 2, z, p % 2, 16 + n_top :] = block[:, chan:]
+                        piece = ref.at[p // 2, z, p % 2]
+                        rows_mid = g_mid[shard * n_mid : (shard + 1) * n_mid]
+                        rows_top = g_top[shard * n_top : (shard + 1) * n_top]
+                        row = 0
+                        for block in (rows_mid, rows_top):
+                            for h in range(block.shape[1] // LANES):
+                                part = block[:, h * LANES : (h + 1) * LANES]
+                                piece[row : row + block.shape[0]] = part.astype(ref.dtype)
+                                row += block.shape[0]
 
 
 def gradients(teachers, spatial, mid, attended, student, links, spaces, scale_mid, scale_top):
     rows, padded, strip, chan = spatial.shape
     frames = padded - 2
     width = attended.shape[-1]
-    height = 16 + (width // (frames * spaces)) * (width // chan)
+    height = (3 * chan * chan + width * width) // (frames * spaces * LANES)
     return call(
         functools.partial(
             gradients_body, links=links, scale_mid=scale_mid, scale_top=scale_top
         ),
         [
-            jax.ShapeDtypeStruct((spaces // 2, links, 2, height, chan), F32),
-            jax.ShapeDtypeStruct((spaces // 2, links, 2, height, chan), BF16),
+            jax.ShapeDtypeStruct((spaces // 2, links, 2, height, LANES), F32),
+            jax.ShapeDtypeStruct((spaces // 2, links, 2, height, LANES), BF16),
         ],
         (*teachers, spatial, mid, attended, student),
         scratch=[
@@ -450,11 +453,12 @@
 def finish_body(*refs):
     parts, mid, top = refs[:-2], refs[-2], refs[-1]
     total = functools.reduce(jnp.add, [part[...] for part in parts])
-    chan = total.shape[1]
-    n_top = top.shape[0]
-    mid[...] = total[: mid.shape[0]]
-    for h in range(top.shape[1] // chan):
-        top[:, h * chan : (h + 1) * chan] = total[16 + h * n_top : 16 + (h + 1) * n_top]
+    row = 0
+    for out in (mid, top):
+        count, cols = out.shape
+        for h in range(cols // LANES):
+            out[:, h * LANES : (h + 1) * LANES] = total[row : row + count]
+            row += count
 
 
 def local(

time: 118 us -> 116 us (0.983)
    ppermute x9, starting transfers between devices: 26.5 us -> 24.4 us  [spread(): lax.ppermute(pieces[k], 'tm', [(i, (i + 2 * k) % frames) for i in range(f...]
    all_to_all x1, starting transfers between devices: 5.76 us -> 7.57 us  [gather(): lax.all_to_all(pieces, 'tm', 0, 0, axis_index_groups=columns, tiled=True)]
  transfers between devices with their start and end apart: 23 -> 23, of which waited for: 9 -> 11; matrix products, arithmetic and copies ran while one was open for 1% -> 1% of each run, Pallas kernels for 11% -> 11%
where the time goes in v5:
time: 116 us; the launch traced here: 114 us
  starting transfers between devices  46.1 us (40%)
  waiting for transfers between devices  38.9 us (34%)
  Pallas kernels  14.5 us (12%)
  blocking collectives  11.7 us (10%)
    ppermute x9, waiting for transfers between devices, spread(): lax.ppermute(pieces[k], 'tm', [(i, (i + 2 * k) % frames) for i in range(f...  26.4 us
    ppermute x9, starting transfers between devices, spread(): lax.ppermute(pieces[k], 'tm', [(i, (i + 2 * k) % frames) for i in range(f...  24.4 us
    pallas_call x7, Pallas kernels, call(): pl.pallas_call(run, out_shape=out_shape, in_specs=specs, out_specs=outs,...  14.5 us
    all_to_all x1, blocking collectives, local(): lax.all_to_all(part, 'space', 0, 0, axis_index_groups=lines, tiled=True)  11.7 us
    all_to_all x1, starting transfers between devices, gather(): lax.all_to_all(pieces, 'tm', 0, 0, axis_index_groups=columns, tiled=True)  7.57 us
    all_to_all x1, starting transfers between devices, local(): lax.all_to_all(part, ('tm', 'space'), 0, 0, axis_index_groups=groups, til...  5.45 us
    ppermute x1, starting transfers between devices, local(): below = lax.ppermute(own[0], 'space', [(j, i) for i, j in ring])  4.44 us
    ppermute x1, waiting for transfers between devices, local(): above = lax.ppermute(own[rows - 1], 'space', ring)  3.89 us
  transfers between devices with their start and end apart: 23, of which 11 were waited for; matrix products, arithmetic and copies ran while one was open for 1% of the time, Pallas kernels for 11%

profile of v5, /device:TPU:4, one launch (start us, length us, event | category | flops | bytes accessed | tf_op | source)
XLA Modules:
  0.0 113.8 jit_solution(4752595942063293100)
XLA Ops:
  0.6 0.1 collective-permute-start.4
  0.7 0.5 collective-permute-start.12
  1.2 0.1 collective-permute-start.13
  1.3 0.9 slice_bitcast_fusion
  2.2 4.4 %collective-permute-start.1 = (bf16[128,256]{1,0:T(8,128)(2,1)S(1)}, bf16[128,256]{1,0:T(8,128)(2,1)S(1)}, u32[]{:S(2)}, u32[]{:S(2)}) collective-permute-start(bf16[128,256]{1,0:T(8,128)(2,1)S(1)} %get-tuple-element.43), channel_id=1, source_target_pairs={{1,0},{2,1},{3,2},{4,3},{5,4},{6,5},{7,6},{0,7},{9,8},{10,9},{11,1... | collective-permute-start | bytes 196616 | tf_op jit(solution)/shard_map/ppermute | solution.py:494
  6.7 0.0 collective-permute-start
  6.7 2.5 %collective-permute-done.1.refs_1_ = bf16[128,256]{1,0:T(8,128)(2,1)S(1)} collective-permute-done((bf16[128,256]{1,0:T(8,128)(2,1)S(1)}, bf16[128,256]{1,0:T(8,128)(2,1)S(1)}, u32[]{:S(2)}, u32[]{:S(2)}) %collective-permute-start.1) | collective-permute-done | bytes 65568 | tf_op jit(solution)/shard_map/ppermute | solution.py:494
  9.1 0.0 collective-permute-start.3
  9.1 3.9 %collective-permute-done.refs_0_ = bf16[128,256]{1,0:T(8,128)(2,1)S(1)} collective-permute-done((bf16[128,256]{1,0:T(8,128)(2,1)S(1)}, bf16[128,256]{1,0:T(8,128)(2,1)S(1)}, u32[]{:S(2)}, u32[]{:S(2)}) %collective-permute-start) | collective-permute-done | bytes 65568 | tf_op jit(solution)/shard_map/ppermute | solution.py:493
  13.0 0.0 collective-permute-start.2
  13.0 0.0 collective-permute-done.3.refs_3_
  13.0 1.2 %collective-permute-done.2.refs_2_ = bf16[128,256]{1,0:T(8,128)(2,1)S(1)} collective-permute-done((bf16[128,256]{1,0:T(8,128)(2,1)S(1)}, bf16[128,256]{1,0:T(8,128)(2,1)S(1)}, u32[]{:S(2)}, u32[]{:S(2)}) %collective-permute-start.2) | collective-permute-done | bytes 65568 | tf_op jit(solution)/shard_map/ppermute | solution.py:479
  14.3 1.7 %shard_map.157 = bf16[4,2,48,256]{3,2,1,0:T(8,128)(2,1)} custom-call(bf16[128,256]{1,0:T(8,128)(2,1)S(1)} %collective-permute-done.refs_0_, bf16[128,256]{1,0:T(8,128)(2,1)S(1)} %collective-permute-done.1.refs_1_, bf16[128,256]{1,0:T(8,128)(2,1)S(1)} %collective-permute-done.2.refs_2_, bf16[128,256]{1,0:T(8,128)(2,1)S(1)} %collective-permute-done.3.refs_3_, ...), custom_call_target="tpu_custom_call" | custom-call | tf_op jit(solution)/shard_map/pallas_call | solution.py:41
  16.0 7.6 %all-to-all-start = ((bf16[4,2,48,256]{3,2,1,0:T(8,128)(2,1)}), bf16[4,2,48,256]{3,2,1,0:T(8,128)(2,1)S(1)}, u32[]{:S(2)}, u32[]{:S(2)}) async-start(bf16[4,2,48,256]{3,2,1,0:T(8,128)(2,1)} %shard_map.157), calls=%async_computation | async-start | bytes 393216 | tf_op jit(solution)/shard_map/all_to_all | solution.py:490
  23.6 0.0 collective-permute-done.4.refs_1_
  23.6 1.4 %shard_map.158 = (bf16[2,144,256]{2,1,0:T(8,128)(2,1)S(1)}, bf16[2,144,256]{2,1,0:T(8,128)(2,1)S(1)}, bf16[2,144,256]{2,1,0:T(8,128)(2,1)S(1)}, bf16[2,144,256]{2,1,0:T(8,128)(2,1)S(1)}) custom-call(bf16[8,128,256]{2,1,0:T(8,128)(2,1)} %bitcast.14, bf16[8,128,256]{2,1,0:T(8,128)(2,1)S(1)} %collective-permute-done.4.refs_1_, ...), custom_call_target="tpu_custom_call" | custom-call | tf_op jit(solution)/shard_map/pallas_call | solution.py:41
  25.1 3.0 %collective-permute-start.5 = (bf16[2,144,256]{2,1,0:T(8,128)(2,1)S(1)}, bf16[2,144,256]{2,1,0:T(8,128)(2,1)S(1)}, u32[]{:S(2)}, u32[]{:S(2)}) collective-permute-start(bf16[2,144,256]{2,1,0:T(8,128)(2,1)S(1)} %get-tuple-element.24), channel_id=1, source_target_pairs={{0,16},{8,24},{16,32},{24,40},{32,48},{40,56},{48,0},{56,8},{1,17}... | collective-permute-start | bytes 442376 | tf_op jit(solution)/shard_map/ppermute | solution.py:483
  28.1 0.0 collective-permute-done.13.refs_3_
  28.1 0.0 collective-permute-done.12.refs_1_
  28.1 1.2 %shard_map.161 = (bf16[2,192,256]{2,1,0:T(8,128)(2,1)S(1)}, bf16[2,192,256]{2,1,0:T(8,128)(2,1)S(1)}, bf16[2,192,256]{2,1,0:T(8,128)(2,1)S(1)}, bf16[2,192,256]{2,1,0:T(8,128)(2,1)S(1)}) custom-call(bf16[8,128,256]{2,1,0:T(8,128)(2,1)} %bitcast.16, bf16[8,128,256]{2,1,0:T(8,128)(2,1)S(1)} %collective-permute-done.12.refs_1_, bf16[4,64,512]{2,1,0:T(8,128)(2,1)} %bitcast.19, ...), custom_call_target="tpu_custom_call" | custom-call | tf_op jit(solution)/shard_map/pallas_call | solution.py:41
  29.3 3.7 %collective-permute-start.14 = (bf16[2,192,256]{2,1,0:T(8,128)(2,1)S(1)}, bf16[2,192,256]{2,1,0:T(8,128)(2,1)S(1)}, u32[]{:S(2)}, u32[]{:S(2)}) collective-permute-start(bf16[2,192,256]{2,1,0:T(8,128)(2,1)S(1)} %get-tuple-element.32), channel_id=1, source_target_pairs={{0,16},{8,24},{16,32},{24,40},{32,48},{40,56},{48,0},{56,8},{1,17}... | collective-permute-start | bytes 589832 | tf_op jit(solution)/shard_map/ppermute | solution.py:483
  32.9 0.1 collective-permute-start.15
  33.0 4.0 %collective-permute-start.16 = (bf16[2,192,256]{2,1,0:T(8,128)(2,1)S(1)}, bf16[2,192,256]{2,1,0:T(8,128)(2,1)S(1)}, u32[]{:S(2)}, u32[]{:S(2)}) collective-permute-start(bf16[2,192,256]{2,1,0:T(8,128)(2,1)S(1)} %get-tuple-element.34), channel_id=1, source_target_pairs={{0,48},{8,56},{16,0},{24,8},{32,16},{40,24},{48,32},{56,40},{1,49}... | collective-permute-start | bytes 589832 | tf_op jit(solution)/shard_map/ppermute | solution.py:483
  37.1 2.4 %collective-permute-start.6 = (bf16[2,144,256]{2,1,0:T(8,128)(2,1)S(1)}, bf16[2,144,256]{2,1,0:T(8,128)(2,1)S(1)}, u32[]{:S(2)}, u32[]{:S(2)}) collective-permute-start(bf16[2,144,256]{2,1,0:T(8,128)(2,1)S(1)} %get-tuple-element.25), channel_id=1, source_target_pairs={{0,32},{8,40},{16,48},{24,56},{32,0},{40,8},{48,16},{56,24},{1,33}... | collective-permute-start | bytes 442376 | tf_op jit(solution)/shard_map/ppermute | solution.py:483
  39.4 1.0 collective-permute-done.5.refs_7_
  40.4 1.2 %collective-permute-start.7 = (bf16[2,144,256]{2,1,0:T(8,128)(2,1)S(1)}, bf16[2,144,256]{2,1,0:T(8,128)(2,1)S(1)}, u32[]{:S(2)}, u32[]{:S(2)}) collective-permute-start(bf16[2,144,256]{2,1,0:T(8,128)(2,1)S(1)} %get-tuple-element.26), channel_id=1, source_target_pairs={{0,48},{8,56},{16,0},{24,8},{32,16},{40,24},{48,32},{56,40},{1,49}... | collective-permute-start | bytes 442376 | tf_op jit(solution)/shard_map/ppermute | solution.py:483
  41.6 0.0 all-to-all-done.refs_0_
  41.6 16.6 %collective-permute-done.6.refs_8_ = bf16[2,144,256]{2,1,0:T(8,128)(2,1)S(1)} collective-permute-done((bf16[2,144,256]{2,1,0:T(8,128)(2,1)S(1)}, bf16[2,144,256]{2,1,0:T(8,128)(2,1)S(1)}, u32[]{:S(2)}, u32[]{:S(2)}) %collective-permute-start.6) | collective-permute-done | bytes 147488 | tf_op jit(solution)/shard_map/ppermute | solution.py:483
  58.2 5.7 %collective-permute-done.7.refs_9_ = bf16[2,144,256]{2,1,0:T(8,128)(2,1)S(1)} collective-permute-done((bf16[2,144,256]{2,1,0:T(8,128)(2,1)S(1)}, bf16[2,144,256]{2,1,0:T(8,128)(2,1)S(1)}, u32[]{:S(2)}, u32[]{:S(2)}) %collective-permute-start.7) | collective-permute-done | bytes 147488 | tf_op jit(solution)/shard_map/ppermute | solution.py:483
  63.9 7.8 %shard_map.159 = (bf16[8,10,16,256]{3,2,1,0:T(8,128)(2,1)S(1)}, bf16[1024,256]{1,0:T(8,128)(2,1)S(1)}, bf16[256,512]{1,0:T(8,128)(2,1)S(1)}, bf16[256,512]{1,0:T...) custom-call(bf16[4,2,48,256]{3,2,1,0:T(8,128)(2,1)S(1)} %all-to-all-, ...), custom_call_target="tpu_custom_call" | custom-call | tf_op jit(solution)/shard_map/pallas_call | solution.py:41
  71.7 0.0 collective-permute-done.14.refs_1_
  71.7 0.0 collective-permute-done.15.refs_2_
  71.7 0.0 collective-permute-done.16.refs_3_
  71.7 0.9 shard_map.162
  72.7 0.1 collective-permute-start.17
  72.8 1.8 %collective-permute-done.17 = bf16[4,4,2,56,128]{4,3,2,1,0:T(8,128)(2,1)S(1)} collective-permute-done((bf16[4,4,2,56,128]{4,3,2,1,0:T(8,128)(2,1)S(1)}, bf16[4,4,2,56,128]{4,3,2,1,0:T(8,128)(2,1)S(1)}, u32[]{:S(2)}, u32[]{:S(2)}) %collective-permute-start.17) | collective-permute-done | bytes 458784 | tf_op jit(solution)/shard_map/ppermute | solution.py:479
  74.6 0.1 add_convert_fusion
  74.7 11.7 %all_to_all.15 = bf16[4,4,2,56,128]{4,3,2,1,0:T(8,128)(2,1)S(1)} all-to-all(bf16[4,4,2,56,128]{4,3,2,1,0:T(8,128)(2,1)S(1)} %add_convert_fusion), channel_id=1, replica_groups={{0,2,4,6},{1,3,5,7},{8,10,12,14},{9,11,13,15},{16,18,20,22},{17,19,21,2..., dimensions={0} | all-to-all | bytes 917504 | tf_op jit(solution)/shard_map/all_to_all | solution.py:526
  86.4 0.7 reduce_sum.21
  87.1 5.5 %all-to-all-start.2 = ((bf16[8,56,128]{2,1,0:T(8,128)(2,1)}), bf16[8,56,128]{2,1,0:T(8,128)(2,1)S(1)}, u32[]{:S(2)}, u32[]{:S(2)}) async-start(bf16[8,56,128]{2,1,0:T(8,128)(2,1)} %bitcast.8), calls=%async_computation.2 | async-start | bytes 229376 | tf_op jit(solution)/shard_map/all_to_all | solution.py:534
  92.6 2.9 %collective-permute-start.8 = (bf16[2,32,512]{2,1,0:T(8,128)(2,1)S(1)}, bf16[2,32,512]{2,1,0:T(8,128)(2,1)S(1)}, u32[]{:S(2)}, u32[]{:S(2)}) collective-permute-start(bf16[2,32,512]{2,1,0:T(8,128)(2,1)S(1)} %get-tuple-element.28), channel_id=1, source_target_pairs={{0,16},{8,24},{16,32},{24,40},{32,48},{40,56},{48,0},{56,8},{1,17}... | collective-permute-start | bytes 196616 | tf_op jit(solution)/shard_map/ppermute | solution.py:483
  95.5 3.6 %collective-permute-start.9 = (bf16[2,32,512]{2,1,0:T(8,128)(2,1)S(1)}, bf16[2,32,512]{2,1,0:T(8,128)(2,1)S(1)}, u32[]{:S(2)}, u32[]{:S(2)}) collective-permute-start(bf16[2,32,512]{2,1,0:T(8,128)(2,1)S(1)} %get-tuple-element.29), channel_id=1, source_target_pairs={{0,32},{8,40},{16,48},{24,56},{32,0},{40,8},{48,16},{56,24},{1,33}... | collective-permute-start | bytes 196616 | tf_op jit(solution)/shard_map/ppermute | solution.py:483
  99.1 3.6 %collective-permute-start.10 = (bf16[2,32,512]{2,1,0:T(8,128)(2,1)S(1)}, bf16[2,32,512]{2,1,0:T(8,128)(2,1)S(1)}, u32[]{:S(2)}, u32[]{:S(2)}) collective-permute-start(bf16[2,32,512]{2,1,0:T(8,128)(2,1)S(1)} %get-tuple-element.30), channel_id=1, source_target_pairs={{0,48},{8,56},{16,0},{24,8},{32,16},{40,24},{48,32},{56,40},{1,49}... | collective-permute-start | bytes 196616 | tf_op jit(solution)/shard_map/ppermute | solution.py:483
  102.6 0.0 collective-permute-done.8.refs_1_
  102.6 2.8 %collective-permute-done.9.refs_2_ = bf16[2,32,512]{2,1,0:T(8,128)(2,1)S(1)} collective-permute-done((bf16[2,32,512]{2,1,0:T(8,128)(2,1)S(1)}, bf16[2,32,512]{2,1,0:T(8,128)(2,1)S(1)}, u32[]{:S(2)}, u32[]{:S(2)}) %collective-permute-start.9) | collective-permute-done | bytes 65568 | tf_op jit(solution)/shard_map/ppermute | solution.py:483
  105.4 0.3 collective-permute-done.10.refs_3_
  105.8 0.1 collective-permute-start.11
  105.9 0.0 all-to-all-done.2
  105.9 0.6 collective-permute-start.20
  106.5 2.7 %collective-permute-start.19 = (f32[56,128]{1,0:T(8,128)S(1)}, f32[56,128]{1,0:T(8,128)S(1)}, u32[]{:S(2)}, u32[]{:S(2)}) collective-permute-start(f32[56,128]{1,0:T(8,128)S(1)} %convert_reduce_fusion.refs_0_), channel_id=1, source_target_pairs={{0,128},{64,192},{128,0},{192,64},{1,129},{65,193},{129,1},{193,65... | collective-permute-start | bytes 86024 | tf_op jit(solution)/shard_map/ppermute | solution.py:537
  109.3 0.0 collective-permute-start.18
  109.3 0.0 collective-permute-done.11.refs_4_
  109.3 0.8 shard_map.160
  110.1 0.0 collective-permute-done.20.refs_3_
  110.1 2.1 %collective-permute-done.19.refs_2_ = f32[56,128]{1,0:T(8,128)S(1)} collective-permute-done((f32[56,128]{1,0:T(8,128)S(1)}, f32[56,128]{1,0:T(8,128)S(1)}, u32[]{:S(2)}, u32[]{:S(2)}) %collective-permute-start.19) | collective-permute-done | bytes 28704 | tf_op jit(solution)/shard_map/ppermute | solution.py:537
  112.2 1.0 collective-permute-done.18.refs_1_
  113.2 0.6 shard_map.163
  (6 shorter events, 0.1 us)
Async XLA Ops:
  0.6 23.0 %collective-permute-start.4 = (bf16[8,128,256]{2,1,0:T(8,128)(2,1)}, bf16[8,128,256]{2,1,0:T(8,128)(2,1)S(1)}, u32[]{:S(2)}, u32[]{:S(2)}) collective-permute-start(bf16[8,128,256]{2,1,0:T(8,128)(2,1)} %bitcast.13), channel_id=1, source_target_pairs={{0,8},{8,0},{16,24},{24,16},{32,40},{40,32},{48,56},{56,48},{1,9},... | collective-permute-start | bytes 1572872 | tf_op jit(solution)/shard_map/ppermute | solution.py:479
  0.7 27.3 %collective-permute-start.12 = (bf16[8,128,256]{2,1,0:T(8,128)(2,1)}, bf16[8,128,256]{2,1,0:T(8,128)(2,1)S(1)}, u32[]{:S(2)}, u32[]{:S(2)}) collective-permute-start(bf16[8,128,256]{2,1,0:T(8,128)(2,1)} %bitcast.15), channel_id=1, source_target_pairs={{0,8},{8,0},{16,24},{24,16},{32,40},{40,32},{48,56},{56,48},{1,9},... | collective-permute-start | bytes 1572872 | tf_op jit(solution)/shard_map/ppermute | solution.py:479
  1.2 26.8 %collective-permute-start.13 = (bf16[4,64,512]{2,1,0:T(8,128)(2,1)}, bf16[4,64,512]{2,1,0:T(8,128)(2,1)S(1)}, u32[]{:S(2)}, u32[]{:S(2)}) collective-permute-start(bf16[4,64,512]{2,1,0:T(8,128)(2,1)} %bitcast.18), channel_id=1, source_target_pairs={{0,8},{8,0},{16,24},{24,16},{32,40},{40,32},{48,56},{56,48},{1,9},... | collective-permute-start | bytes 786440 | tf_op jit(solution)/shard_map/ppermute | solution.py:479
  2.2 6.9 %collective-permute-start.1 = (bf16[128,256]{1,0:T(8,128)(2,1)S(1)}, bf16[128,256]{1,0:T(8,128)(2,1)S(1)}, u32[]{:S(2)}, u32[]{:S(2)}) collective-permute-start(bf16[128,256]{1,0:T(8,128)(2,1)S(1)} %get-tuple-element.43), channel_id=1, source_target_pairs={{1,0},{2,1},{3,2},{4,3},{5,4},{6,5},{7,6},{0,7},{9,8},{10,9},{11,1... | collective-permute-start | bytes 196616 | tf_op jit(solution)/shard_map/ppermute | solution.py:494
  6.7 6.4 %collective-permute-start = (bf16[128,256]{1,0:T(8,128)(2,1)S(1)}, bf16[128,256]{1,0:T(8,128)(2,1)S(1)}, u32[]{:S(2)}, u32[]{:S(2)}) collective-permute-start(bf16[128,256]{1,0:T(8,128)(2,1)S(1)} %get-tuple-element.44), channel_id=1, source_target_pairs={{0,1},{1,2},{2,3},{3,4},{4,5},{5,6},{6,7},{7,0},{8,9},{9,10},{10,1... | collective-permute-start | bytes 196616 | tf_op jit(solution)/shard_map/ppermute | solution.py:493
  9.1 3.9 %collective-permute-start.3 = (bf16[128,256]{1,0:T(8,128)(2,1)S(1)}, bf16[128,256]{1,0:T(8,128)(2,1)S(1)}, u32[]{:S(2)}, u32[]{:S(2)}) collective-permute-start(bf16[128,256]{1,0:T(8,128)(2,1)S(1)} %collective-permute-done.1.refs_1_), channel_id=1, source_target_pairs={{0,8},{8,0},{16,24},{24,16},{32,40},{40,32},{48,56},{56,48},{1,9},... | collective-permute-start | bytes 196616 | tf_op jit(solution)/shard_map/ppermute | solution.py:479
  13.0 1.3 %collective-permute-start.2 = (bf16[128,256]{1,0:T(8,128)(2,1)S(1)}, bf16[128,256]{1,0:T(8,128)(2,1)S(1)}, u32[]{:S(2)}, u32[]{:S(2)}) collective-permute-start(bf16[128,256]{1,0:T(8,128)(2,1)S(1)} %collective-permute-done.refs_0_), channel_id=1, source_target_pairs={{0,8},{8,0},{16,24},{24,16},{32,40},{40,32},{48,56},{56,48},{1,9},... | collective-permute-start | bytes 196616 | tf_op jit(solution)/shard_map/ppermute | solution.py:479
  16.0 25.6 %all-to-all-start = ((bf16[4,2,48,256]{3,2,1,0:T(8,128)(2,1)}), bf16[4,2,48,256]{3,2,1,0:T(8,128)(2,1)S(1)}, u32[]{:S(2)}, u32[]{:S(2)}) async-start(bf16[4,2,48,256]{3,2,1,0:T(8,128)(2,1)} %shard_map.157), calls=%async_computation | async-start | bytes 393216 | tf_op jit(solution)/shard_map/all_to_all | solution.py:490
  25.1 15.3 %collective-permute-start.5 = (bf16[2,144,256]{2,1,0:T(8,128)(2,1)S(1)}, bf16[2,144,256]{2,1,0:T(8,128)(2,1)S(1)}, u32[]{:S(2)}, u32[]{:S(2)}) collective-permute-start(bf16[2,144,256]{2,1,0:T(8,128)(2,1)S(1)} %get-tuple-element.24), channel_id=1, source_target_pairs={{0,16},{8,24},{16,32},{24,40},{32,48},{40,56},{48,0},{56,8},{1,17}... | collective-permute-start | bytes 442376 | tf_op jit(solution)/shard_map/ppermute | solution.py:483
  29.3 42.4 %collective-permute-start.14 = (bf16[2,192,256]{2,1,0:T(8,128)(2,1)S(1)}, bf16[2,192,256]{2,1,0:T(8,128)(2,1)S(1)}, u32[]{:S(2)}, u32[]{:S(2)}) collective-permute-start(bf16[2,192,256]{2,1,0:T(8,128)(2,1)S(1)} %get-tuple-element.32), channel_id=1, source_target_pairs={{0,16},{8,24},{16,32},{24,40},{32,48},{40,56},{48,0},{56,8},{1,17}... | collective-permute-start | bytes 589832 | tf_op jit(solution)/shard_map/ppermute | solution.py:483
  32.9 38.8 %collective-permute-start.15 = (bf16[2,192,256]{2,1,0:T(8,128)(2,1)S(1)}, bf16[2,192,256]{2,1,0:T(8,128)(2,1)S(1)}, u32[]{:S(2)}, u32[]{:S(2)}) collective-permute-start(bf16[2,192,256]{2,1,0:T(8,128)(2,1)S(1)} %get-tuple-element.33), channel_id=1, source_target_pairs={{0,32},{8,40},{16,48},{24,56},{32,0},{40,8},{48,16},{56,24},{1,33}... | collective-permute-start | bytes 589832 | tf_op jit(solution)/shard_map/ppermute | solution.py:483
  33.0 38.7 %collective-permute-start.16 = (bf16[2,192,256]{2,1,0:T(8,128)(2,1)S(1)}, bf16[2,192,256]{2,1,0:T(8,128)(2,1)S(1)}, u32[]{:S(2)}, u32[]{:S(2)}) collective-permute-start(bf16[2,192,256]{2,1,0:T(8,128)(2,1)S(1)} %get-tuple-element.34), channel_id=1, source_target_pairs={{0,48},{8,56},{16,0},{24,8},{32,16},{40,24},{48,32},{56,40},{1,49}... | collective-permute-start | bytes 589832 | tf_op jit(solution)/shard_map/ppermute | solution.py:483
  37.1 21.1 %collective-permute-start.6 = (bf16[2,144,256]{2,1,0:T(8,128)(2,1)S(1)}, bf16[2,144,256]{2,1,0:T(8,128)(2,1)S(1)}, u32[]{:S(2)}, u32[]{:S(2)}) collective-permute-start(bf16[2,144,256]{2,1,0:T(8,128)(2,1)S(1)} %get-tuple-element.25), channel_id=1, source_target_pairs={{0,32},{8,40},{16,48},{24,56},{32,0},{40,8},{48,16},{56,24},{1,33}... | collective-permute-start | bytes 442376 | tf_op jit(solution)/shard_map/ppermute | solution.py:483
  40.4 23.5 %collective-permute-start.7 = (bf16[2,144,256]{2,1,0:T(8,128)(2,1)S(1)}, bf16[2,144,256]{2,1,0:T(8,128)(2,1)S(1)}, u32[]{:S(2)}, u32[]{:S(2)}) collective-permute-start(bf16[2,144,256]{2,1,0:T(8,128)(2,1)S(1)} %get-tuple-element.26), channel_id=1, source_target_pairs={{0,48},{8,56},{16,0},{24,8},{32,16},{40,24},{48,32},{56,40},{1,49}... | collective-permute-start | bytes 442376 | tf_op jit(solution)/shard_map/ppermute | solution.py:483
  72.7 1.9 %collective-permute-start.17 = (bf16[4,4,2,56,128]{4,3,2,1,0:T(8,128)(2,1)S(1)}, bf16[4,4,2,56,128]{4,3,2,1,0:T(8,128)(2,1)S(1)}, u32[]{:S(2)}, u32[]{:S(2)}) collective-permute-start(bf16[4,4,2,56,128]{4,3,2,1,0:T(8,128)(2,1)S(1)} %get-tuple-element.40), channel_id=1, source_target_pairs={{0,8},{8,0},{16,24},{24,16},{32,40},{40,32},{48,56},{56,48},{1,9},... | collective-permute-start | bytes 1376264 | tf_op jit(solution)/shard_map/ppermute | solution.py:479
  87.1 18.8 %all-to-all-start.2 = ((bf16[8,56,128]{2,1,0:T(8,128)(2,1)}), bf16[8,56,128]{2,1,0:T(8,128)(2,1)S(1)}, u32[]{:S(2)}, u32[]{:S(2)}) async-start(bf16[8,56,128]{2,1,0:T(8,128)(2,1)} %bitcast.8), calls=%async_computation.2 | async-start | bytes 229376 | tf_op jit(solution)/shard_map/all_to_all | solution.py:534
  92.6 10.1 %collective-permute-start.8 = (bf16[2,32,512]{2,1,0:T(8,128)(2,1)S(1)}, bf16[2,32,512]{2,1,0:T(8,128)(2,1)S(1)}, u32[]{:S(2)}, u32[]{:S(2)}) collective-permute-start(bf16[2,32,512]{2,1,0:T(8,128)(2,1)S(1)} %get-tuple-element.28), channel_id=1, source_target_pairs={{0,16},{8,24},{16,32},{24,40},{32,48},{40,56},{48,0},{56,8},{1,17}... | collective-permute-start | bytes 196616 | tf_op jit(solution)/shard_map/ppermute | solution.py:483
  95.5 10.0 %collective-permute-start.9 = (bf16[2,32,512]{2,1,0:T(8,128)(2,1)S(1)}, bf16[2,32,512]{2,1,0:T(8,128)(2,1)S(1)}, u32[]{:S(2)}, u32[]{:S(2)}) collective-permute-start(bf16[2,32,512]{2,1,0:T(8,128)(2,1)S(1)} %get-tuple-element.29), channel_id=1, source_target_pairs={{0,32},{8,40},{16,48},{24,56},{32,0},{40,8},{48,16},{56,24},{1,33}... | collective-permute-start | bytes 196616 | tf_op jit(solution)/shard_map/ppermute | solution.py:483
  99.1 6.7 %collective-permute-start.10 = (bf16[2,32,512]{2,1,0:T(8,128)(2,1)S(1)}, bf16[2,32,512]{2,1,0:T(8,128)(2,1)S(1)}, u32[]{:S(2)}, u32[]{:S(2)}) collective-permute-start(bf16[2,32,512]{2,1,0:T(8,128)(2,1)S(1)} %get-tuple-element.30), channel_id=1, source_target_pairs={{0,48},{8,56},{16,0},{24,8},{32,16},{40,24},{48,32},{56,40},{1,49}... | collective-permute-start | bytes 196616 | tf_op jit(solution)/shard_map/ppermute | solution.py:483
  105.8 3.5 %collective-permute-start.11 = (bf16[4,32,512]{2,1,0:T(8,128)(2,1)S(1)}, bf16[4,32,512]{2,1,0:T(8,128)(2,1)S(1)}, u32[]{:S(2)}, u32[]{:S(2)}) collective-permute-start(bf16[4,32,512]{2,1,0:T(8,128)(2,1)S(1)} %pad_maximum_fusion), channel_id=1, source_target_pairs={{0,8},{8,0},{16,24},{24,16},{32,40},{40,32},{48,56},{56,48},{1,9},... | collective-permute-start | bytes 393224 | tf_op jit(solution)/shard_map/ppermute | solution.py:479
  105.9 4.1 %collective-permute-start.20 = (f32[56,128]{1,0:T(8,128)S(1)}, f32[56,128]{1,0:T(8,128)S(1)}, u32[]{:S(2)}, u32[]{:S(2)}) collective-permute-start(f32[56,128]{1,0:T(8,128)S(1)} %convert_reduce_fusion.refs_0_), channel_id=1, source_target_pairs={{0,192},{64,0},{128,64},{192,128},{1,193},{65,1},{129,65},{193,129... | collective-permute-start | bytes 86024 | tf_op jit(solution)/shard_map/ppermute | solution.py:537
  106.5 5.6 %collective-permute-start.19 = (f32[56,128]{1,0:T(8,128)S(1)}, f32[56,128]{1,0:T(8,128)S(1)}, u32[]{:S(2)}, u32[]{:S(2)}) collective-permute-start(f32[56,128]{1,0:T(8,128)S(1)} %convert_reduce_fusion.refs_0_), channel_id=1, source_target_pairs={{0,128},{64,192},{128,0},{192,64},{1,129},{65,193},{129,1},{193,65... | collective-permute-start | bytes 86024 | tf_op jit(solution)/shard_map/ppermute | solution.py:537
  109.3 3.9 %collective-permute-start.18 = (f32[56,128]{1,0:T(8,128)S(1)}, f32[56,128]{1,0:T(8,128)S(1)}, u32[]{:S(2)}, u32[]{:S(2)}) collective-permute-start(f32[56,128]{1,0:T(8,128)S(1)} %convert_reduce_fusion.refs_0_), channel_id=1, source_target_pairs={{0,64},{64,128},{128,192},{192,0},{1,65},{65,129},{129,193},{193,1... | collective-permute-start | bytes 86024 | tf_op jit(solution)/shard_map/ppermute | solution.py:537

commit v6 on v5

--- a/solution.py
+++ b/solution.py
@@ -59,18 +59,19 @@
 
 
 EDGES = 16
-
-
-def edge_picker(count, cols, strip):
+CORNERS = 8
+
+
+def edge_picker(count, cols, strip, height):
     strips = cols // strip
-    pick = np.zeros((strips, EDGES, count * cols), np.float32)
+    pick = np.zeros((strips, height, count * cols), np.float32)
     for j in range(strips):
         for r in range(count):
             if j > 0:
                 pick[j, r, r * cols + j * strip - 1] = 1
             if j < strips - 1:
                 pick[j, count + r, r * cols + (j + 1) * strip] = 1
-    return jnp.asarray(pick.reshape(strips * EDGES, count * cols), BF16)
+    return jnp.asarray(pick.reshape(strips * height, count * cols), BF16)
 
 
 def pack_piece(tall, edges, out, s, j):
@@ -84,7 +85,7 @@
 def find_edges(tall, pick, edges):
     count, cols, chan = tall.shape
     flat = tall[...].reshape(count * cols, chan)
-    found = jnp.dot(pick[...], flat, preferred_element_type=F32).astype(BF16)
+    found = jnp.dot(pick, flat, preferred_element_type=F32).astype(BF16)
     edges[...] = found.reshape(edges.shape)
 
 
@@ -94,7 +95,7 @@
     for wait in waits:
         wait()
     for s, source in enumerate((own, partner)):
-        find_edges(source, pick, edges)
+        find_edges(source, pick[...], edges)
         for k in range(links):
             pack_piece(source, edges, outs[k], s, 2 * lax.rem(zhi + k, links) + core)
 
@@ -105,18 +106,26 @@
     return call(
         functools.partial(pack_main_body, links=links),
         [jax.ShapeDtypeStruct((2, rows * strip + EDGES, chan), BF16)] * links,
-        (own, partner, edge_picker(rows, cols, strip)),
+        (own, partner, edge_picker(rows, cols, strip, EDGES)),
         scratch=[pltpu.VMEM((2 * links, EDGES, chan), BF16)],
         manual=(0, 2),
     )
 
 
-def pack_halo_body(waits, *refs, links):
-    sources, pick, out = (refs[:2], refs[2:4]), refs[4], refs[5]
-    tall, edges = refs[6:]
+def pack_halo_body(*refs, links):
+    sources, out = (refs[:2], refs[2:4]), refs[4]
+    tall, edges = refs[5:]
     _, core = place()
-    for wait in waits:
-        wait()
+    count, cols, _ = tall.shape
+    strip = cols // (2 * links)
+    shape = (2 * links * CORNERS, count * cols)
+    line = lax.broadcasted_iota(jnp.int32, shape, 0)
+    spot = lax.broadcasted_iota(jnp.int32, shape, 1)
+    j, q = line // CORNERS, line % CORNERS
+    left = (q < count) & (j > 0) & (spot == q * cols + j * strip - 1)
+    right = (q >= count) & (q < 2 * count) & (j < 2 * links - 1)
+    right = right & (spot == (q - count) * cols + (j + 1) * strip)
+    pick = jnp.where(left | right, 1.0, 0.0).astype(BF16)
     index = lax.axis_index("space")
     first, last = index == 0, index == lax.axis_size("space") - 1
     for s, (above, below) in enumerate(sources):
@@ -132,13 +141,12 @@
     strip = cols // (2 * links)
     return call(
         functools.partial(pack_halo_body, links=links),
-        [jax.ShapeDtypeStruct((links, 2, 2 * strip + EDGES, chan), BF16)],
-        (*own, *partner, edge_picker(2, cols, strip)),
+        [jax.ShapeDtypeStruct((links, 2, 2 * strip + CORNERS, chan), BF16)],
+        (*own, *partner),
         scratch=[
             pltpu.VMEM((2, cols, chan), BF16),
-            pltpu.VMEM((2 * links, EDGES, chan), BF16),
+            pltpu.VMEM((2 * links, CORNERS, chan), BF16),
         ],
-        manual=(4,),
     )[0]
 
 
@@ -183,7 +191,7 @@
     main = rows * strip
     halo = main + EDGES
     corner = halo + 2 * strip
-    left = np.zeros((rows + 2, strip, corner + EDGES), np.float32)
+    left = np.zeros((rows + 2, strip, corner + CORNERS), np.float32)
     right = np.zeros_like(left)
     for q in range(rows + 2):
         if q == 0:
@@ -339,7 +347,7 @@
     ] + [jax.ShapeDtypeStruct((2, points, width), BF16)] * links
     scratch = [
         pltpu.VMEM((rows + 2, frames, strip, 3 * chan), BF16),
-        pltpu.VMEM((rows * strip + 2 * strip + 2 * EDGES, chan), BF16),
+        pltpu.VMEM((rows * strip + EDGES + 2 * strip + CORNERS, chan), BF16),
         pltpu.VMEM((frames * points, 4 * chan), BF16),
         pltpu.VMEM((4, rows // 2, frames, half, width), F32),
     ]
@@ -533,10 +541,7 @@
     ]
     part = lax.all_to_all(part, ("tm", "space"), 0, 0, axis_index_groups=groups, tiled=True)
     part = jnp.sum(part.astype(F32), 0)
-    others = [
-        lax.ppermute(part, "dp", [(i, (i + k) % clips) for i in range(clips)])
-        for k in range(1, clips)
-    ]
+    others = [lax.ppermute(part, "dp", [(i, i ^ k) for i in range(clips)]) for k in range(1, clips)]
     n_top = width // (frames * spaces)
     grad_temporal, grad_out = call(
         finish_body,

time: 116 us -> 114 us (0.983)
  waiting for transfers between devices: 38.9 us -> 37 us
  starting transfers between devices: 46.1 us -> 47.4 us
    ppermute x9, starting transfers between devices: 24.4 us -> 26.5 us  [spread(): lax.ppermute(pieces[k], 'tm', [(i, (i + 2 * k) % frames) for i in range(f...]
    all_to_all x1, starting transfers between devices: 7.57 us -> 5.76 us  [gather(): lax.all_to_all(pieces, 'tm', 0, 0, axis_index_groups=columns, tiled=True)]
    ppermute x7, waiting for transfers between devices: 3.05 us -> 1.81 us  [swap(): return lax.ppermute(block, 'tm', [(i, i ^ 1) for i in range(frames)])]
  transfers between devices with their start and end apart: 23 -> 23, of which waited for: 11 -> 9; matrix products, arithmetic and copies ran while one was open for 1% -> 1% of each run, Pallas kernels for 11% -> 11%
where the time goes in v6:
time: 114 us; the launch traced here: 112 us
  starting transfers between devices  47.4 us (42%)
  waiting for transfers between devices  37 us (32%)
  Pallas kernels  13.7 us (12%)
  blocking collectives  11.7 us (10%)
    ppermute x9, waiting for transfers between devices, spread(): lax.ppermute(pieces[k], 'tm', [(i, (i + 2 * k) % frames) for i in range(f...  26.6 us
    ppermute x9, starting transfers between devices, spread(): lax.ppermute(pieces[k], 'tm', [(i, (i + 2 * k) % frames) for i in range(f...  26.5 us
    pallas_call x7, Pallas kernels, call(): pl.pallas_call(run, out_shape=out_shape, in_specs=specs, out_specs=outs,...  13.7 us
    all_to_all x1, blocking collectives, local(): lax.all_to_all(part, 'space', 0, 0, axis_index_groups=lines, tiled=True)  11.7 us
    all_to_all x1, starting transfers between devices, gather(): lax.all_to_all(pieces, 'tm', 0, 0, axis_index_groups=columns, tiled=True)  5.76 us
    all_to_all x1, starting transfers between devices, local(): lax.all_to_all(part, ('tm', 'space'), 0, 0, axis_index_groups=groups, til...  5.6 us
    ppermute x1, starting transfers between devices, local(): below = lax.ppermute(own[0], 'space', [(j, i) for i, j in ring])  4.44 us
    ppermute x3, starting transfers between devices, local(): lax.ppermute(part, 'dp', [(i, i ^ k) for i in range(clips)])  4.18 us
  transfers between devices with their start and end apart: 23, of which 9 were waited for; matrix products, arithmetic and copies ran while one was open for 1% of the time, Pallas kernels for 11%

profile of v6, /device:TPU:4, one launch (start us, length us, event | category | flops | bytes accessed | tf_op | source)
XLA Modules:
  0.0 112.3 jit_solution(7804875212694187125)
XLA Ops:
  0.6 0.1 collective-permute-start.4
  0.7 0.5 collective-permute-start.12
  1.2 0.1 collective-permute-start.13
  1.3 0.9 slice_bitcast_fusion
  2.2 4.4 %collective-permute-start.1 = (bf16[128,256]{1,0:T(8,128)(2,1)S(1)}, bf16[128,256]{1,0:T(8,128)(2,1)S(1)}, u32[]{:S(2)}, u32[]{:S(2)}) collective-permute-start(bf16[128,256]{1,0:T(8,128)(2,1)S(1)} %get-tuple-element.43), channel_id=1, source_target_pairs={{1,0},{2,1},{3,2},{4,3},{5,4},{6,5},{7,6},{0,7},{9,8},{10,9},{11,1... | collective-permute-start | bytes 196616 | tf_op jit(solution)/shard_map/ppermute | solution.py:502
  6.7 0.0 collective-permute-start
  6.7 2.5 %collective-permute-done.1.refs_1_ = bf16[128,256]{1,0:T(8,128)(2,1)S(1)} collective-permute-done((bf16[128,256]{1,0:T(8,128)(2,1)S(1)}, bf16[128,256]{1,0:T(8,128)(2,1)S(1)}, u32[]{:S(2)}, u32[]{:S(2)}) %collective-permute-start.1) | collective-permute-done | bytes 65568 | tf_op jit(solution)/shard_map/ppermute | solution.py:502
  9.1 0.0 collective-permute-start.3
  9.1 3.9 %collective-permute-done.refs_0_ = bf16[128,256]{1,0:T(8,128)(2,1)S(1)} collective-permute-done((bf16[128,256]{1,0:T(8,128)(2,1)S(1)}, bf16[128,256]{1,0:T(8,128)(2,1)S(1)}, u32[]{:S(2)}, u32[]{:S(2)}) %collective-permute-start) | collective-permute-done | bytes 65568 | tf_op jit(solution)/shard_map/ppermute | solution.py:501
  13.0 0.0 collective-permute-start.2
  13.0 0.0 collective-permute-done.4.refs_1_
  13.0 1.5 %shard_map.149 = (bf16[2,144,256]{2,1,0:T(8,128)(2,1)S(1)}, bf16[2,144,256]{2,1,0:T(8,128)(2,1)S(1)}, bf16[2,144,256]{2,1,0:T(8,128)(2,1)S(1)}, bf16[2,144,256]{2,1,0:T(8,128)(2,1)S(1)}) custom-call(bf16[8,128,256]{2,1,0:T(8,128)(2,1)} %bitcast.14, bf16[8,128,256]{2,1,0:T(8,128)(2,1)S(1)} %collective-permute-done.4.refs_1_, ...), custom_call_target="tpu_custom_call" | custom-call | tf_op jit(solution)/shard_map/pallas_call | solution.py:41
  14.5 3.3 %collective-permute-start.5 = (bf16[2,144,256]{2,1,0:T(8,128)(2,1)S(1)}, bf16[2,144,256]{2,1,0:T(8,128)(2,1)S(1)}, u32[]{:S(2)}, u32[]{:S(2)}) collective-permute-start(bf16[2,144,256]{2,1,0:T(8,128)(2,1)S(1)} %get-tuple-element.24), channel_id=1, source_target_pairs={{0,16},{8,24},{16,32},{24,40},{32,48},{40,56},{48,0},{56,8},{1,17}... | collective-permute-start | bytes 442376 | tf_op jit(solution)/shard_map/ppermute | solution.py:491
  17.9 0.0 collective-permute-done.3.refs_3_
  17.9 0.0 collective-permute-done.2.refs_2_
  17.9 0.9 shard_map.148
  18.7 5.8 %all-to-all-start = ((bf16[4,2,40,256]{3,2,1,0:T(8,128)(2,1)}), bf16[4,2,40,256]{3,2,1,0:T(8,128)(2,1)S(1)}, u32[]{:S(2)}, u32[]{:S(2)}) async-start(bf16[4,2,40,256]{3,2,1,0:T(8,128)(2,1)} %shard_map.148), calls=%async_computation | async-start | bytes 327680 | tf_op jit(solution)/shard_map/all_to_all | solution.py:498
  24.5 0.0 collective-permute-done.13.refs_3_
  24.5 0.0 collective-permute-done.12.refs_1_
  24.5 1.2 %shard_map.152 = (bf16[2,192,256]{2,1,0:T(8,128)(2,1)S(1)}, bf16[2,192,256]{2,1,0:T(8,128)(2,1)S(1)}, bf16[2,192,256]{2,1,0:T(8,128)(2,1)S(1)}, bf16[2,192,256]{2,1,0:T(8,128)(2,1)S(1)}) custom-call(bf16[8,128,256]{2,1,0:T(8,128)(2,1)} %bitcast.16, bf16[8,128,256]{2,1,0:T(8,128)(2,1)S(1)} %collective-permute-done.12.refs_1_, bf16[4,64,512]{2,1,0:T(8,128)(2,1)} %bitcast.19, ...), custom_call_target="tpu_custom_call" | custom-call | tf_op jit(solution)/shard_map/pallas_call | solution.py:41
  25.7 3.0 %collective-permute-start.14 = (bf16[2,192,256]{2,1,0:T(8,128)(2,1)S(1)}, bf16[2,192,256]{2,1,0:T(8,128)(2,1)S(1)}, u32[]{:S(2)}, u32[]{:S(2)}) collective-permute-start(bf16[2,192,256]{2,1,0:T(8,128)(2,1)S(1)} %get-tuple-element.32), channel_id=1, source_target_pairs={{0,16},{8,24},{16,32},{24,40},{32,48},{40,56},{48,0},{56,8},{1,17}... | collective-permute-start | bytes 589832 | tf_op jit(solution)/shard_map/ppermute | solution.py:491
  28.7 3.6 %collective-permute-start.15 = (bf16[2,192,256]{2,1,0:T(8,128)(2,1)S(1)}, bf16[2,192,256]{2,1,0:T(8,128)(2,1)S(1)}, u32[]{:S(2)}, u32[]{:S(2)}) collective-permute-start(bf16[2,192,256]{2,1,0:T(8,128)(2,1)S(1)} %get-tuple-element.33), channel_id=1, source_target_pairs={{0,32},{8,40},{16,48},{24,56},{32,0},{40,8},{48,16},{56,24},{1,33}... | collective-permute-start | bytes 589832 | tf_op jit(solution)/shard_map/ppermute | solution.py:491
  32.3 3.6 %collective-permute-start.16 = (bf16[2,192,256]{2,1,0:T(8,128)(2,1)S(1)}, bf16[2,192,256]{2,1,0:T(8,128)(2,1)S(1)}, u32[]{:S(2)}, u32[]{:S(2)}) collective-permute-start(bf16[2,192,256]{2,1,0:T(8,128)(2,1)S(1)} %get-tuple-element.34), channel_id=1, source_target_pairs={{0,48},{8,56},{16,0},{24,8},{32,16},{40,24},{48,32},{56,40},{1,49}... | collective-permute-start | bytes 589832 | tf_op jit(solution)/shard_map/ppermute | solution.py:491
  35.9 0.1 collective-permute-start.6
  36.0 0.0 collective-permute-done.5.refs_7_
  36.0 2.8 %collective-permute-start.7 = (bf16[2,144,256]{2,1,0:T(8,128)(2,1)S(1)}, bf16[2,144,256]{2,1,0:T(8,128)(2,1)S(1)}, u32[]{:S(2)}, u32[]{:S(2)}) collective-permute-start(bf16[2,144,256]{2,1,0:T(8,128)(2,1)S(1)} %get-tuple-element.26), channel_id=1, source_target_pairs={{0,48},{8,56},{16,0},{24,8},{32,16},{40,24},{48,32},{56,40},{1,49}... | collective-permute-start | bytes 442376 | tf_op jit(solution)/shard_map/ppermute | solution.py:491
  38.8 0.0 all-to-all-done.refs_0_
  38.8 12.1 %collective-permute-done.6.refs_8_ = bf16[2,144,256]{2,1,0:T(8,128)(2,1)S(1)} collective-permute-done((bf16[2,144,256]{2,1,0:T(8,128)(2,1)S(1)}, bf16[2,144,256]{2,1,0:T(8,128)(2,1)S(1)}, u32[]{:S(2)}, u32[]{:S(2)}) %collective-permute-start.6) | collective-permute-done | bytes 147488 | tf_op jit(solution)/shard_map/ppermute | solution.py:491
  50.9 11.3 %collective-permute-done.7.refs_9_ = bf16[2,144,256]{2,1,0:T(8,128)(2,1)S(1)} collective-permute-done((bf16[2,144,256]{2,1,0:T(8,128)(2,1)S(1)}, bf16[2,144,256]{2,1,0:T(8,128)(2,1)S(1)}, u32[]{:S(2)}, u32[]{:S(2)}) %collective-permute-start.7) | collective-permute-done | bytes 147488 | tf_op jit(solution)/shard_map/ppermute | solution.py:491
  62.2 7.8 %shard_map.150 = (bf16[8,10,16,256]{3,2,1,0:T(8,128)(2,1)S(1)}, bf16[1024,256]{1,0:T(8,128)(2,1)S(1)}, bf16[256,512]{1,0:T(8,128)(2,1)S(1)}, bf16[256,512]{1,0:T...) custom-call(bf16[4,2,40,256]{3,2,1,0:T(8,128)(2,1)S(1)} %all-to-all-, ...), custom_call_target="tpu_custom_call" | custom-call | tf_op jit(solution)/shard_map/pallas_call | solution.py:41
  70.0 0.0 collective-permute-done.14.refs_1_
  70.0 0.0 collective-permute-done.15.refs_2_
  70.0 0.0 collective-permute-done.16.refs_3_
  70.1 0.9 shard_map.153
  71.0 0.1 collective-permute-start.17
  71.1 1.8 %collective-permute-done.17 = bf16[4,4,2,56,128]{4,3,2,1,0:T(8,128)(2,1)S(1)} collective-permute-done((bf16[4,4,2,56,128]{4,3,2,1,0:T(8,128)(2,1)S(1)}, bf16[4,4,2,56,128]{4,3,2,1,0:T(8,128)(2,1)S(1)}, u32[]{:S(2)}, u32[]{:S(2)}) %collective-permute-start.17) | collective-permute-done | bytes 458784 | tf_op jit(solution)/shard_map/ppermute | solution.py:487
  72.9 0.1 add_convert_fusion
  73.0 11.7 %all_to_all.15 = bf16[4,4,2,56,128]{4,3,2,1,0:T(8,128)(2,1)S(1)} all-to-all(bf16[4,4,2,56,128]{4,3,2,1,0:T(8,128)(2,1)S(1)} %add_convert_fusion), channel_id=1, replica_groups={{0,2,4,6},{1,3,5,7},{8,10,12,14},{9,11,13,15},{16,18,20,22},{17,19,21,2..., dimensions={0} | all-to-all | bytes 917504 | tf_op jit(solution)/shard_map/all_to_all | solution.py:534
  84.7 0.7 reduce_sum.21
  85.4 5.6 %all-to-all-start.2 = ((bf16[8,56,128]{2,1,0:T(8,128)(2,1)}), bf16[8,56,128]{2,1,0:T(8,128)(2,1)S(1)}, u32[]{:S(2)}, u32[]{:S(2)}) async-start(bf16[8,56,128]{2,1,0:T(8,128)(2,1)} %bitcast.8), calls=%async_computation.2 | async-start | bytes 229376 | tf_op jit(solution)/shard_map/all_to_all | solution.py:542
  91.0 2.9 %collective-permute-start.8 = (bf16[2,32,512]{2,1,0:T(8,128)(2,1)S(1)}, bf16[2,32,512]{2,1,0:T(8,128)(2,1)S(1)}, u32[]{:S(2)}, u32[]{:S(2)}) collective-permute-start(bf16[2,32,512]{2,1,0:T(8,128)(2,1)S(1)} %get-tuple-element.28), channel_id=1, source_target_pairs={{0,16},{8,24},{16,32},{24,40},{32,48},{40,56},{48,0},{56,8},{1,17}... | collective-permute-start | bytes 196616 | tf_op jit(solution)/shard_map/ppermute | solution.py:491
  94.0 3.6 %collective-permute-start.9 = (bf16[2,32,512]{2,1,0:T(8,128)(2,1)S(1)}, bf16[2,32,512]{2,1,0:T(8,128)(2,1)S(1)}, u32[]{:S(2)}, u32[]{:S(2)}) collective-permute-start(bf16[2,32,512]{2,1,0:T(8,128)(2,1)S(1)} %get-tuple-element.29), channel_id=1, source_target_pairs={{0,32},{8,40},{16,48},{24,56},{32,0},{40,8},{48,16},{56,24},{1,33}... | collective-permute-start | bytes 196616 | tf_op jit(solution)/shard_map/ppermute | solution.py:491
  97.5 3.6 %collective-permute-start.10 = (bf16[2,32,512]{2,1,0:T(8,128)(2,1)S(1)}, bf16[2,32,512]{2,1,0:T(8,128)(2,1)S(1)}, u32[]{:S(2)}, u32[]{:S(2)}) collective-permute-start(bf16[2,32,512]{2,1,0:T(8,128)(2,1)S(1)} %get-tuple-element.30), channel_id=1, source_target_pairs={{0,48},{8,56},{16,0},{24,8},{32,16},{40,24},{48,32},{56,40},{1,49}... | collective-permute-start | bytes 196616 | tf_op jit(solution)/shard_map/ppermute | solution.py:491
  101.1 0.0 collective-permute-done.8.refs_1_
  101.1 2.8 %collective-permute-done.9.refs_2_ = bf16[2,32,512]{2,1,0:T(8,128)(2,1)S(1)} collective-permute-done((bf16[2,32,512]{2,1,0:T(8,128)(2,1)S(1)}, bf16[2,32,512]{2,1,0:T(8,128)(2,1)S(1)}, u32[]{:S(2)}, u32[]{:S(2)}) %collective-permute-start.9) | collective-permute-done | bytes 65568 | tf_op jit(solution)/shard_map/ppermute | solution.py:491
  103.9 0.3 collective-permute-done.10.refs_3_
  104.3 0.1 collective-permute-start.11
  104.4 0.0 all-to-all-done.2
  104.4 0.6 collective-permute-start.20
  105.1 2.7 %collective-permute-start.19 = (f32[56,128]{1,0:T(8,128)S(1)}, f32[56,128]{1,0:T(8,128)S(1)}, u32[]{:S(2)}, u32[]{:S(2)}) collective-permute-start(f32[56,128]{1,0:T(8,128)S(1)} %convert_reduce_fusion.refs_0_), channel_id=1, source_target_pairs={{0,128},{64,192},{128,0},{192,64},{1,129},{65,193},{129,1},{193,65... | collective-permute-start | bytes 86024 | tf_op jit(solution)/shard_map/ppermute | solution.py:544
  107.8 0.8 collective-permute-start.18
  108.6 0.0 collective-permute-done.11.refs_4_
  108.6 0.8 shard_map.151
  109.4 0.0 collective-permute-done.20.refs_3_
  109.4 1.0 collective-permute-done.19.refs_2_
  110.4 1.2 %collective-permute-done.18.refs_1_ = f32[56,128]{1,0:T(8,128)S(1)} collective-permute-done((f32[56,128]{1,0:T(8,128)S(1)}, f32[56,128]{1,0:T(8,128)S(1)}, u32[]{:S(2)}, u32[]{:S(2)}) %collective-permute-start.18) | collective-permute-done | bytes 28704 | tf_op jit(solution)/shard_map/ppermute | solution.py:544
  111.6 0.6 shard_map.154
  (6 shorter events, 0.1 us)
Async XLA Ops:
  0.6 12.4 %collective-permute-start.4 = (bf16[8,128,256]{2,1,0:T(8,128)(2,1)}, bf16[8,128,256]{2,1,0:T(8,128)(2,1)S(1)}, u32[]{:S(2)}, u32[]{:S(2)}) collective-permute-start(bf16[8,128,256]{2,1,0:T(8,128)(2,1)} %bitcast.13), channel_id=1, source_target_pairs={{0,8},{8,0},{16,24},{24,16},{32,40},{40,32},{48,56},{56,48},{1,9},... | collective-permute-start | bytes 1572872 | tf_op jit(solution)/shard_map/ppermute | solution.py:487
  0.7 23.8 %collective-permute-start.12 = (bf16[8,128,256]{2,1,0:T(8,128)(2,1)}, bf16[8,128,256]{2,1,0:T(8,128)(2,1)S(1)}, u32[]{:S(2)}, u32[]{:S(2)}) collective-permute-start(bf16[8,128,256]{2,1,0:T(8,128)(2,1)} %bitcast.15), channel_id=1, source_target_pairs={{0,8},{8,0},{16,24},{24,16},{32,40},{40,32},{48,56},{56,48},{1,9},... | collective-permute-start | bytes 1572872 | tf_op jit(solution)/shard_map/ppermute | solution.py:487
  1.2 23.3 %collective-permute-start.13 = (bf16[4,64,512]{2,1,0:T(8,128)(2,1)}, bf16[4,64,512]{2,1,0:T(8,128)(2,1)S(1)}, u32[]{:S(2)}, u32[]{:S(2)}) collective-permute-start(bf16[4,64,512]{2,1,0:T(8,128)(2,1)} %bitcast.18), channel_id=1, source_target_pairs={{0,8},{8,0},{16,24},{24,16},{32,40},{40,32},{48,56},{56,48},{1,9},... | collective-permute-start | bytes 786440 | tf_op jit(solution)/shard_map/ppermute | solution.py:487
  2.2 6.9 %collective-permute-start.1 = (bf16[128,256]{1,0:T(8,128)(2,1)S(1)}, bf16[128,256]{1,0:T(8,128)(2,1)S(1)}, u32[]{:S(2)}, u32[]{:S(2)}) collective-permute-start(bf16[128,256]{1,0:T(8,128)(2,1)S(1)} %get-tuple-element.43), channel_id=1, source_target_pairs={{1,0},{2,1},{3,2},{4,3},{5,4},{6,5},{7,6},{0,7},{9,8},{10,9},{11,1... | collective-permute-start | bytes 196616 | tf_op jit(solution)/shard_map/ppermute | solution.py:502
  6.7 6.4 %collective-permute-start = (bf16[128,256]{1,0:T(8,128)(2,1)S(1)}, bf16[128,256]{1,0:T(8,128)(2,1)S(1)}, u32[]{:S(2)}, u32[]{:S(2)}) collective-permute-start(bf16[128,256]{1,0:T(8,128)(2,1)S(1)} %get-tuple-element.44), channel_id=1, source_target_pairs={{0,1},{1,2},{2,3},{3,4},{4,5},{5,6},{6,7},{7,0},{8,9},{9,10},{10,1... | collective-permute-start | bytes 196616 | tf_op jit(solution)/shard_map/ppermute | solution.py:501
  9.1 8.7 %collective-permute-start.3 = (bf16[128,256]{1,0:T(8,128)(2,1)S(1)}, bf16[128,256]{1,0:T(8,128)(2,1)S(1)}, u32[]{:S(2)}, u32[]{:S(2)}) collective-permute-start(bf16[128,256]{1,0:T(8,128)(2,1)S(1)} %collective-permute-done.1.refs_1_), channel_id=1, source_target_pairs={{0,8},{8,0},{16,24},{24,16},{32,40},{40,32},{48,56},{56,48},{1,9},... | collective-permute-start | bytes 196616 | tf_op jit(solution)/shard_map/ppermute | solution.py:487
  13.0 4.8 %collective-permute-start.2 = (bf16[128,256]{1,0:T(8,128)(2,1)S(1)}, bf16[128,256]{1,0:T(8,128)(2,1)S(1)}, u32[]{:S(2)}, u32[]{:S(2)}) collective-permute-start(bf16[128,256]{1,0:T(8,128)(2,1)S(1)} %collective-permute-done.refs_0_), channel_id=1, source_target_pairs={{0,8},{8,0},{16,24},{24,16},{32,40},{40,32},{48,56},{56,48},{1,9},... | collective-permute-start | bytes 196616 | tf_op jit(solution)/shard_map/ppermute | solution.py:487
  14.5 21.5 %collective-permute-start.5 = (bf16[2,144,256]{2,1,0:T(8,128)(2,1)S(1)}, bf16[2,144,256]{2,1,0:T(8,128)(2,1)S(1)}, u32[]{:S(2)}, u32[]{:S(2)}) collective-permute-start(bf16[2,144,256]{2,1,0:T(8,128)(2,1)S(1)} %get-tuple-element.24), channel_id=1, source_target_pairs={{0,16},{8,24},{16,32},{24,40},{32,48},{40,56},{48,0},{56,8},{1,17}... | collective-permute-start | bytes 442376 | tf_op jit(solution)/shard_map/ppermute | solution.py:491
  18.7 20.1 %all-to-all-start = ((bf16[4,2,40,256]{3,2,1,0:T(8,128)(2,1)}), bf16[4,2,40,256]{3,2,1,0:T(8,128)(2,1)S(1)}, u32[]{:S(2)}, u32[]{:S(2)}) async-start(bf16[4,2,40,256]{3,2,1,0:T(8,128)(2,1)} %shard_map.148), calls=%async_computation | async-start | bytes 327680 | tf_op jit(solution)/shard_map/all_to_all | solution.py:498
  25.7 44.3 %collective-permute-start.14 = (bf16[2,192,256]{2,1,0:T(8,128)(2,1)S(1)}, bf16[2,192,256]{2,1,0:T(8,128)(2,1)S(1)}, u32[]{:S(2)}, u32[]{:S(2)}) collective-permute-start(bf16[2,192,256]{2,1,0:T(8,128)(2,1)S(1)} %get-tuple-element.32), channel_id=1, source_target_pairs={{0,16},{8,24},{16,32},{24,40},{32,48},{40,56},{48,0},{56,8},{1,17}... | collective-permute-start | bytes 589832 | tf_op jit(solution)/shard_map/ppermute | solution.py:491
  28.7 41.3 %collective-permute-start.15 = (bf16[2,192,256]{2,1,0:T(8,128)(2,1)S(1)}, bf16[2,192,256]{2,1,0:T(8,128)(2,1)S(1)}, u32[]{:S(2)}, u32[]{:S(2)}) collective-permute-start(bf16[2,192,256]{2,1,0:T(8,128)(2,1)S(1)} %get-tuple-element.33), channel_id=1, source_target_pairs={{0,32},{8,40},{16,48},{24,56},{32,0},{40,8},{48,16},{56,24},{1,33}... | collective-permute-start | bytes 589832 | tf_op jit(solution)/shard_map/ppermute | solution.py:491
  32.3 37.8 %collective-permute-start.16 = (bf16[2,192,256]{2,1,0:T(8,128)(2,1)S(1)}, bf16[2,192,256]{2,1,0:T(8,128)(2,1)S(1)}, u32[]{:S(2)}, u32[]{:S(2)}) collective-permute-start(bf16[2,192,256]{2,1,0:T(8,128)(2,1)S(1)} %get-tuple-element.34), channel_id=1, source_target_pairs={{0,48},{8,56},{16,0},{24,8},{32,16},{40,24},{48,32},{56,40},{1,49}... | collective-permute-start | bytes 589832 | tf_op jit(solution)/shard_map/ppermute | solution.py:491
  35.9 15.1 %collective-permute-start.6 = (bf16[2,144,256]{2,1,0:T(8,128)(2,1)S(1)}, bf16[2,144,256]{2,1,0:T(8,128)(2,1)S(1)}, u32[]{:S(2)}, u32[]{:S(2)}) collective-permute-start(bf16[2,144,256]{2,1,0:T(8,128)(2,1)S(1)} %get-tuple-element.25), channel_id=1, source_target_pairs={{0,32},{8,40},{16,48},{24,56},{32,0},{40,8},{48,16},{56,24},{1,33}... | collective-permute-start | bytes 442376 | tf_op jit(solution)/shard_map/ppermute | solution.py:491
  36.0 26.3 %collective-permute-start.7 = (bf16[2,144,256]{2,1,0:T(8,128)(2,1)S(1)}, bf16[2,144,256]{2,1,0:T(8,128)(2,1)S(1)}, u32[]{:S(2)}, u32[]{:S(2)}) collective-permute-start(bf16[2,144,256]{2,1,0:T(8,128)(2,1)S(1)} %get-tuple-element.26), channel_id=1, source_target_pairs={{0,48},{8,56},{16,0},{24,8},{32,16},{40,24},{48,32},{56,40},{1,49}... | collective-permute-start | bytes 442376 | tf_op jit(solution)/shard_map/ppermute | solution.py:491
  71.0 1.9 %collective-permute-start.17 = (bf16[4,4,2,56,128]{4,3,2,1,0:T(8,128)(2,1)S(1)}, bf16[4,4,2,56,128]{4,3,2,1,0:T(8,128)(2,1)S(1)}, u32[]{:S(2)}, u32[]{:S(2)}) collective-permute-start(bf16[4,4,2,56,128]{4,3,2,1,0:T(8,128)(2,1)S(1)} %get-tuple-element.40), channel_id=1, source_target_pairs={{0,8},{8,0},{16,24},{24,16},{32,40},{40,32},{48,56},{56,48},{1,9},... | collective-permute-start | bytes 1376264 | tf_op jit(solution)/shard_map/ppermute | solution.py:487
  85.4 18.9 %all-to-all-start.2 = ((bf16[8,56,128]{2,1,0:T(8,128)(2,1)}), bf16[8,56,128]{2,1,0:T(8,128)(2,1)S(1)}, u32[]{:S(2)}, u32[]{:S(2)}) async-start(bf16[8,56,128]{2,1,0:T(8,128)(2,1)} %bitcast.8), calls=%async_computation.2 | async-start | bytes 229376 | tf_op jit(solution)/shard_map/all_to_all | solution.py:542
  91.0 10.1 %collective-permute-start.8 = (bf16[2,32,512]{2,1,0:T(8,128)(2,1)S(1)}, bf16[2,32,512]{2,1,0:T(8,128)(2,1)S(1)}, u32[]{:S(2)}, u32[]{:S(2)}) collective-permute-start(bf16[2,32,512]{2,1,0:T(8,128)(2,1)S(1)} %get-tuple-element.28), channel_id=1, source_target_pairs={{0,16},{8,24},{16,32},{24,40},{32,48},{40,56},{48,0},{56,8},{1,17}... | collective-permute-start | bytes 196616 | tf_op jit(solution)/shard_map/ppermute | solution.py:491
  94.0 9.9 %collective-permute-start.9 = (bf16[2,32,512]{2,1,0:T(8,128)(2,1)S(1)}, bf16[2,32,512]{2,1,0:T(8,128)(2,1)S(1)}, u32[]{:S(2)}, u32[]{:S(2)}) collective-permute-start(bf16[2,32,512]{2,1,0:T(8,128)(2,1)S(1)} %get-tuple-element.29), channel_id=1, source_target_pairs={{0,32},{8,40},{16,48},{24,56},{32,0},{40,8},{48,16},{56,24},{1,33}... | collective-permute-start | bytes 196616 | tf_op jit(solution)/shard_map/ppermute | solution.py:491
  97.5 6.7 %collective-permute-start.10 = (bf16[2,32,512]{2,1,0:T(8,128)(2,1)S(1)}, bf16[2,32,512]{2,1,0:T(8,128)(2,1)S(1)}, u32[]{:S(2)}, u32[]{:S(2)}) collective-permute-start(bf16[2,32,512]{2,1,0:T(8,128)(2,1)S(1)} %get-tuple-element.30), channel_id=1, source_target_pairs={{0,48},{8,56},{16,0},{24,8},{32,16},{40,24},{48,32},{56,40},{1,49}... | collective-permute-start | bytes 196616 | tf_op jit(solution)/shard_map/ppermute | solution.py:491
  104.3 4.3 %collective-permute-start.11 = (bf16[4,32,512]{2,1,0:T(8,128)(2,1)S(1)}, bf16[4,32,512]{2,1,0:T(8,128)(2,1)S(1)}, u32[]{:S(2)}, u32[]{:S(2)}) collective-permute-start(bf16[4,32,512]{2,1,0:T(8,128)(2,1)S(1)} %pad_maximum_fusion), channel_id=1, source_target_pairs={{0,8},{8,0},{16,24},{24,16},{32,40},{40,32},{48,56},{56,48},{1,9},... | collective-permute-start | bytes 393224 | tf_op jit(solution)/shard_map/ppermute | solution.py:487
  104.4 5.0 %collective-permute-start.20 = (f32[56,128]{1,0:T(8,128)S(1)}, f32[56,128]{1,0:T(8,128)S(1)}, u32[]{:S(2)}, u32[]{:S(2)}) collective-permute-start(f32[56,128]{1,0:T(8,128)S(1)} %convert_reduce_fusion.refs_0_), channel_id=1, source_target_pairs={{0,192},{64,128},{128,64},{192,0},{1,193},{65,129},{129,65},{193,1... | collective-permute-start | bytes 86024 | tf_op jit(solution)/shard_map/ppermute | solution.py:544
  105.1 5.4 %collective-permute-start.19 = (f32[56,128]{1,0:T(8,128)S(1)}, f32[56,128]{1,0:T(8,128)S(1)}, u32[]{:S(2)}, u32[]{:S(2)}) collective-permute-start(f32[56,128]{1,0:T(8,128)S(1)} %convert_reduce_fusion.refs_0_), channel_id=1, source_target_pairs={{0,128},{64,192},{128,0},{192,64},{1,129},{65,193},{129,1},{193,65... | collective-permute-start | bytes 86024 | tf_op jit(solution)/shard_map/ppermute | solution.py:544
  107.8 3.9 %collective-permute-start.18 = (f32[56,128]{1,0:T(8,128)S(1)}, f32[56,128]{1,0:T(8,128)S(1)}, u32[]{:S(2)}, u32[]{:S(2)}) collective-permute-start(f32[56,128]{1,0:T(8,128)S(1)} %convert_reduce_fusion.refs_0_), channel_id=1, source_target_pairs={{0,64},{64,0},{128,192},{192,128},{1,65},{65,1},{129,193},{193,129... | collective-permute-start | bytes 86024 | tf_op jit(solution)/shard_map/ppermute | solution.py:544

commit v7 on v6

--- a/solution.py
+++ b/solution.py
@@ -62,18 +62,6 @@
 CORNERS = 8
 
 
-def edge_picker(count, cols, strip, height):
-    strips = cols // strip
-    pick = np.zeros((strips, height, count * cols), np.float32)
-    for j in range(strips):
-        for r in range(count):
-            if j > 0:
-                pick[j, r, r * cols + j * strip - 1] = 1
-            if j < strips - 1:
-                pick[j, count + r, r * cols + (j + 1) * strip] = 1
-    return jnp.asarray(pick.reshape(strips * height, count * cols), BF16)
-
-
 def pack_piece(tall, edges, out, s, j):
     count, cols, chan = tall.shape
     strip = cols // edges.shape[0]
@@ -82,6 +70,18 @@
     out[s, count * strip :] = edges[j]
 
 
+def make_picker(count, cols, strips, height):
+    strip = cols // strips
+    shape = (strips * height, count * cols)
+    line = lax.broadcasted_iota(jnp.int32, shape, 0)
+    spot = lax.broadcasted_iota(jnp.int32, shape, 1)
+    j, q = line // height, line % height
+    left = (q < count) & (j > 0) & (spot == q * cols + j * strip - 1)
+    right = (q >= count) & (q < 2 * count) & (j < strips - 1)
+    right = right & (spot == (q - count) * cols + (j + 1) * strip)
+    return jnp.where(left | right, 1.0, 0.0).astype(BF16)
+
+
 def find_edges(tall, pick, edges):
     count, cols, chan = tall.shape
     flat = tall[...].reshape(count * cols, chan)
@@ -89,13 +89,16 @@
     edges[...] = found.reshape(edges.shape)
 
 
-def pack_main_body(waits, own, partner, pick, *refs, links):
+def pack_main_body(waits, own, partner, *refs, links):
     outs, edges = refs[:links], refs[links]
     zhi, core = place()
-    for wait in waits:
-        wait()
-    for s, source in enumerate((own, partner)):
-        find_edges(source, pick[...], edges)
+    count, cols, _ = own.shape
+    pick = make_picker(count, cols, 2 * links, EDGES)
+    for s, source in ((1, partner), (0, own)):
+        if s == 0:
+            for wait in waits:
+                wait()
+        find_edges(source, pick, edges)
         for k in range(links):
             pack_piece(source, edges, outs[k], s, 2 * lax.rem(zhi + k, links) + core)
 
@@ -106,9 +109,9 @@
     return call(
         functools.partial(pack_main_body, links=links),
         [jax.ShapeDtypeStruct((2, rows * strip + EDGES, chan), BF16)] * links,
-        (own, partner, edge_picker(rows, cols, strip, EDGES)),
+        (own, partner),
         scratch=[pltpu.VMEM((2 * links, EDGES, chan), BF16)],
-        manual=(0, 2),
+        manual=(0,),
     )
 
 
@@ -117,15 +120,7 @@
     tall, edges = refs[5:]
     _, core = place()
     count, cols, _ = tall.shape
-    strip = cols // (2 * links)
-    shape = (2 * links * CORNERS, count * cols)
-    line = lax.broadcasted_iota(jnp.int32, shape, 0)
-    spot = lax.broadcasted_iota(jnp.int32, shape, 1)
-    j, q = line // CORNERS, line % CORNERS
-    left = (q < count) & (j > 0) & (spot == q * cols + j * strip - 1)
-    right = (q >= count) & (q < 2 * count) & (j < 2 * links - 1)
-    right = right & (spot == (q - count) * cols + (j + 1) * strip)
-    pick = jnp.where(left | right, 1.0, 0.0).astype(BF16)
+    pick = make_picker(count, cols, 2 * links, CORNERS)
     index = lax.axis_index("space")
     first, last = index == 0, index == lax.axis_size("space") - 1
     for s, (above, below) in enumerate(sources):
@@ -152,18 +147,19 @@
 
 def pack_teacher_body(waits, own_mid, partner_mid, own_top, partner_top, *outs, links):
     zhi, core = place()
-    for wait in waits:
-        wait()
     rows, cols, chan = own_mid.shape
     half_rows, half_cols, width = own_top.shape
     strip = cols // (2 * links)
     half = half_cols // (2 * links)
     base = rows * strip
     points = half_rows * half
-    for k in range(links):
-        dest = lax.rem(zhi + k, links)
-        j = 2 * dest + core
-        for s, (mid, top) in enumerate(((own_mid, own_top), (partner_mid, partner_top))):
+    for s, mid, top in ((1, partner_mid, partner_top), (0, own_mid, own_top)):
+        if s == 0:
+            for wait in waits:
+                wait()
+        for k in range(links):
+            dest = lax.rem(zhi + k, links)
+            j = 2 * dest + core
             begin = pl.multiple_of(j * strip, strip)
             outs[k][s, :base] = mid[:, pl.ds(begin, strip), :].reshape(base, chan)
             begin = pl.multiple_of(dest * 2 * half, 2 * half)

time: 114 us -> 114 us (level)
  no operation moved by 1% of the time
where the time goes in v7:
time: 114 us; the launch traced here: 112 us
  starting transfers between devices  47.4 us (42%)
  waiting for transfers between devices  37 us (32%)
  Pallas kernels  13.5 us (12%)
  blocking collectives  11.7 us (10%)
    ppermute x9, waiting for transfers between devices, spread(): lax.ppermute(pieces[k], 'tm', [(i, (i + 2 * k) % frames) for i in range(f...  26.6 us
    ppermute x9, starting transfers between devices, spread(): lax.ppermute(pieces[k], 'tm', [(i, (i + 2 * k) % frames) for i in range(f...  26.5 us
    pallas_call x7, Pallas kernels, call(): pl.pallas_call(run, out_shape=out_shape, in_specs=specs, out_specs=outs,...  13.5 us
    all_to_all x1, blocking collectives, local(): lax.all_to_all(part, 'space', 0, 0, axis_index_groups=lines, tiled=True)  11.7 us
    all_to_all x1, starting transfers between devices, gather(): lax.all_to_all(pieces, 'tm', 0, 0, axis_index_groups=columns, tiled=True)  5.76 us
    all_to_all x1, starting transfers between devices, local(): lax.all_to_all(part, ('tm', 'space'), 0, 0, axis_index_groups=groups, til...  5.6 us
    ppermute x1, starting transfers between devices, local(): below = lax.ppermute(own[0], 'space', [(j, i) for i, j in ring])  4.44 us
    ppermute x3, starting transfers between devices, local(): lax.ppermute(part, 'dp', [(i, i ^ k) for i in range(clips)])  4.18 us
  transfers between devices with their start and end apart: 23, of which 9 were waited for; matrix products, arithmetic and copies ran while one was open for 1% of the time, Pallas kernels for 11%

profile of v7, /device:TPU:4, one launch (start us, length us, event | category | flops | bytes accessed | tf_op | source)
XLA Modules:
  0.0 112.1 jit_solution(16182842525874018965)
XLA Ops:
  0.6 0.1 collective-permute-start.4
  0.7 0.5 collective-permute-start.12
  1.2 0.1 collective-permute-start.13
  1.3 0.9 slice_bitcast_fusion
  2.2 4.4 %collective-permute-start.1 = (bf16[128,256]{1,0:T(8,128)(2,1)S(1)}, bf16[128,256]{1,0:T(8,128)(2,1)S(1)}, u32[]{:S(2)}, u32[]{:S(2)}) collective-permute-start(bf16[128,256]{1,0:T(8,128)(2,1)S(1)} %get-tuple-element.43), channel_id=1, source_target_pairs={{1,0},{2,1},{3,2},{4,3},{5,4},{6,5},{7,6},{0,7},{9,8},{10,9},{11,1... | collective-permute-start | bytes 196616 | tf_op jit(solution)/shard_map/ppermute | solution.py:498
  6.7 0.0 collective-permute-start
  6.7 2.5 %collective-permute-done.1.refs_1_ = bf16[128,256]{1,0:T(8,128)(2,1)S(1)} collective-permute-done((bf16[128,256]{1,0:T(8,128)(2,1)S(1)}, bf16[128,256]{1,0:T(8,128)(2,1)S(1)}, u32[]{:S(2)}, u32[]{:S(2)}) %collective-permute-start.1) | collective-permute-done | bytes 65568 | tf_op jit(solution)/shard_map/ppermute | solution.py:498
  9.1 0.0 collective-permute-start.3
  9.1 3.9 %collective-permute-done.refs_0_ = bf16[128,256]{1,0:T(8,128)(2,1)S(1)} collective-permute-done((bf16[128,256]{1,0:T(8,128)(2,1)S(1)}, bf16[128,256]{1,0:T(8,128)(2,1)S(1)}, u32[]{:S(2)}, u32[]{:S(2)}) %collective-permute-start) | collective-permute-done | bytes 65568 | tf_op jit(solution)/shard_map/ppermute | solution.py:497
  13.0 0.0 collective-permute-start.2
  13.0 0.0 collective-permute-done.4.refs_1_
  13.0 1.4 %shard_map.140 = (bf16[2,144,256]{2,1,0:T(8,128)(2,1)S(1)}, bf16[2,144,256]{2,1,0:T(8,128)(2,1)S(1)}, bf16[2,144,256]{2,1,0:T(8,128)(2,1)S(1)}, bf16[2,144,256]{2,1,0:T(8,128)(2,1)S(1)}) custom-call(bf16[8,128,256]{2,1,0:T(8,128)(2,1)} %bitcast.14, bf16[8,128,256]{2,1,0:T(8,128)(2,1)S(1)} %collective-permute-done.4.refs_1_), custom_call_target="tpu_custom_call" | custom-call | tf_op jit(solution)/shard_map/pallas_call | solution.py:41
  14.4 3.3 %collective-permute-start.5 = (bf16[2,144,256]{2,1,0:T(8,128)(2,1)S(1)}, bf16[2,144,256]{2,1,0:T(8,128)(2,1)S(1)}, u32[]{:S(2)}, u32[]{:S(2)}) collective-permute-start(bf16[2,144,256]{2,1,0:T(8,128)(2,1)S(1)} %get-tuple-element.24), channel_id=1, source_target_pairs={{0,16},{8,24},{16,32},{24,40},{32,48},{40,56},{48,0},{56,8},{1,17}... | collective-permute-start | bytes 442376 | tf_op jit(solution)/shard_map/ppermute | solution.py:487
  17.8 0.0 collective-permute-done.3.refs_3_
  17.8 0.0 collective-permute-done.2.refs_2_
  17.8 0.9 shard_map.139
  18.7 5.8 %all-to-all-start = ((bf16[4,2,40,256]{3,2,1,0:T(8,128)(2,1)}), bf16[4,2,40,256]{3,2,1,0:T(8,128)(2,1)S(1)}, u32[]{:S(2)}, u32[]{:S(2)}) async-start(bf16[4,2,40,256]{3,2,1,0:T(8,128)(2,1)} %shard_map.139), calls=%async_computation | async-start | bytes 327680 | tf_op jit(solution)/shard_map/all_to_all | solution.py:494
  24.4 0.0 collective-permute-done.13.refs_3_
  24.4 0.0 collective-permute-done.12.refs_1_
  24.4 1.2 %shard_map.143 = (bf16[2,192,256]{2,1,0:T(8,128)(2,1)S(1)}, bf16[2,192,256]{2,1,0:T(8,128)(2,1)S(1)}, bf16[2,192,256]{2,1,0:T(8,128)(2,1)S(1)}, bf16[2,192,256]{2,1,0:T(8,128)(2,1)S(1)}) custom-call(bf16[8,128,256]{2,1,0:T(8,128)(2,1)} %bitcast.16, bf16[8,128,256]{2,1,0:T(8,128)(2,1)S(1)} %collective-permute-done.12.refs_1_, bf16[4,64,512]{2,1,0:T(8,128)(2,1)} %bitcast.19, ...), custom_call_target="tpu_custom_call" | custom-call | tf_op jit(solution)/shard_map/pallas_call | solution.py:41
  25.6 3.0 %collective-permute-start.14 = (bf16[2,192,256]{2,1,0:T(8,128)(2,1)S(1)}, bf16[2,192,256]{2,1,0:T(8,128)(2,1)S(1)}, u32[]{:S(2)}, u32[]{:S(2)}) collective-permute-start(bf16[2,192,256]{2,1,0:T(8,128)(2,1)S(1)} %get-tuple-element.32), channel_id=1, source_target_pairs={{0,16},{8,24},{16,32},{24,40},{32,48},{40,56},{48,0},{56,8},{1,17}... | collective-permute-start | bytes 589832 | tf_op jit(solution)/shard_map/ppermute | solution.py:487
  28.6 3.6 %collective-permute-start.15 = (bf16[2,192,256]{2,1,0:T(8,128)(2,1)S(1)}, bf16[2,192,256]{2,1,0:T(8,128)(2,1)S(1)}, u32[]{:S(2)}, u32[]{:S(2)}) collective-permute-start(bf16[2,192,256]{2,1,0:T(8,128)(2,1)S(1)} %get-tuple-element.33), channel_id=1, source_target_pairs={{0,32},{8,40},{16,48},{24,56},{32,0},{40,8},{48,16},{56,24},{1,33}... | collective-permute-start | bytes 589832 | tf_op jit(solution)/shard_map/ppermute | solution.py:487
  32.2 3.6 %collective-permute-start.16 = (bf16[2,192,256]{2,1,0:T(8,128)(2,1)S(1)}, bf16[2,192,256]{2,1,0:T(8,128)(2,1)S(1)}, u32[]{:S(2)}, u32[]{:S(2)}) collective-permute-start(bf16[2,192,256]{2,1,0:T(8,128)(2,1)S(1)} %get-tuple-element.34), channel_id=1, source_target_pairs={{0,48},{8,56},{16,0},{24,8},{32,16},{40,24},{48,32},{56,40},{1,49}... | collective-permute-start | bytes 589832 | tf_op jit(solution)/shard_map/ppermute | solution.py:487
  35.7 0.1 collective-permute-start.6
  35.9 0.0 collective-permute-done.5.refs_7_
  35.9 2.8 %collective-permute-start.7 = (bf16[2,144,256]{2,1,0:T(8,128)(2,1)S(1)}, bf16[2,144,256]{2,1,0:T(8,128)(2,1)S(1)}, u32[]{:S(2)}, u32[]{:S(2)}) collective-permute-start(bf16[2,144,256]{2,1,0:T(8,128)(2,1)S(1)} %get-tuple-element.26), channel_id=1, source_target_pairs={{0,48},{8,56},{16,0},{24,8},{32,16},{40,24},{48,32},{56,40},{1,49}... | collective-permute-start | bytes 442376 | tf_op jit(solution)/shard_map/ppermute | solution.py:487
  38.7 0.0 all-to-all-done.refs_0_
  38.7 12.4 %collective-permute-done.6.refs_8_ = bf16[2,144,256]{2,1,0:T(8,128)(2,1)S(1)} collective-permute-done((bf16[2,144,256]{2,1,0:T(8,128)(2,1)S(1)}, bf16[2,144,256]{2,1,0:T(8,128)(2,1)S(1)}, u32[]{:S(2)}, u32[]{:S(2)}) %collective-permute-start.6) | collective-permute-done | bytes 147488 | tf_op jit(solution)/shard_map/ppermute | solution.py:487
  51.1 11.0 %collective-permute-done.7.refs_9_ = bf16[2,144,256]{2,1,0:T(8,128)(2,1)S(1)} collective-permute-done((bf16[2,144,256]{2,1,0:T(8,128)(2,1)S(1)}, bf16[2,144,256]{2,1,0:T(8,128)(2,1)S(1)}, u32[]{:S(2)}, u32[]{:S(2)}) %collective-permute-start.7) | collective-permute-done | bytes 147488 | tf_op jit(solution)/shard_map/ppermute | solution.py:487
  62.1 7.8 %shard_map.141 = (bf16[8,10,16,256]{3,2,1,0:T(8,128)(2,1)S(1)}, bf16[1024,256]{1,0:T(8,128)(2,1)S(1)}, bf16[256,512]{1,0:T(8,128)(2,1)S(1)}, bf16[256,512]{1,0:T...) custom-call(bf16[4,2,40,256]{3,2,1,0:T(8,128)(2,1)S(1)} %all-to-all-, ...), custom_call_target="tpu_custom_call" | custom-call | tf_op jit(solution)/shard_map/pallas_call | solution.py:41
  69.9 0.0 collective-permute-done.14.refs_1_
  69.9 0.0 collective-permute-done.15.refs_2_
  69.9 0.0 collective-permute-done.16.refs_3_
  69.9 0.9 shard_map.144
  70.9 0.1 collective-permute-start.17
  71.0 1.8 %collective-permute-done.17 = bf16[4,4,2,56,128]{4,3,2,1,0:T(8,128)(2,1)S(1)} collective-permute-done((bf16[4,4,2,56,128]{4,3,2,1,0:T(8,128)(2,1)S(1)}, bf16[4,4,2,56,128]{4,3,2,1,0:T(8,128)(2,1)S(1)}, u32[]{:S(2)}, u32[]{:S(2)}) %collective-permute-start.17) | collective-permute-done | bytes 458784 | tf_op jit(solution)/shard_map/ppermute | solution.py:483
  72.8 0.1 add_convert_fusion
  72.9 11.7 %all_to_all.15 = bf16[4,4,2,56,128]{4,3,2,1,0:T(8,128)(2,1)S(1)} all-to-all(bf16[4,4,2,56,128]{4,3,2,1,0:T(8,128)(2,1)S(1)} %add_convert_fusion), channel_id=1, replica_groups={{0,2,4,6},{1,3,5,7},{8,10,12,14},{9,11,13,15},{16,18,20,22},{17,19,21,2..., dimensions={0} | all-to-all | bytes 917504 | tf_op jit(solution)/shard_map/all_to_all | solution.py:530
  84.6 0.7 reduce_sum.21
  85.3 5.6 %all-to-all-start.2 = ((bf16[8,56,128]{2,1,0:T(8,128)(2,1)}), bf16[8,56,128]{2,1,0:T(8,128)(2,1)S(1)}, u32[]{:S(2)}, u32[]{:S(2)}) async-start(bf16[8,56,128]{2,1,0:T(8,128)(2,1)} %bitcast.8), calls=%async_computation.2 | async-start | bytes 229376 | tf_op jit(solution)/shard_map/all_to_all | solution.py:538
  90.9 2.9 %collective-permute-start.8 = (bf16[2,32,512]{2,1,0:T(8,128)(2,1)S(1)}, bf16[2,32,512]{2,1,0:T(8,128)(2,1)S(1)}, u32[]{:S(2)}, u32[]{:S(2)}) collective-permute-start(bf16[2,32,512]{2,1,0:T(8,128)(2,1)S(1)} %get-tuple-element.28), channel_id=1, source_target_pairs={{0,16},{8,24},{16,32},{24,40},{32,48},{40,56},{48,0},{56,8},{1,17}... | collective-permute-start | bytes 196616 | tf_op jit(solution)/shard_map/ppermute | solution.py:487
  93.8 3.6 %collective-permute-start.9 = (bf16[2,32,512]{2,1,0:T(8,128)(2,1)S(1)}, bf16[2,32,512]{2,1,0:T(8,128)(2,1)S(1)}, u32[]{:S(2)}, u32[]{:S(2)}) collective-permute-start(bf16[2,32,512]{2,1,0:T(8,128)(2,1)S(1)} %get-tuple-element.29), channel_id=1, source_target_pairs={{0,32},{8,40},{16,48},{24,56},{32,0},{40,8},{48,16},{56,24},{1,33}... | collective-permute-start | bytes 196616 | tf_op jit(solution)/shard_map/ppermute | solution.py:487
  97.4 3.6 %collective-permute-start.10 = (bf16[2,32,512]{2,1,0:T(8,128)(2,1)S(1)}, bf16[2,32,512]{2,1,0:T(8,128)(2,1)S(1)}, u32[]{:S(2)}, u32[]{:S(2)}) collective-permute-start(bf16[2,32,512]{2,1,0:T(8,128)(2,1)S(1)} %get-tuple-element.30), channel_id=1, source_target_pairs={{0,48},{8,56},{16,0},{24,8},{32,16},{40,24},{48,32},{56,40},{1,49}... | collective-permute-start | bytes 196616 | tf_op jit(solution)/shard_map/ppermute | solution.py:487
  101.0 0.0 collective-permute-done.8.refs_1_
  101.0 2.8 %collective-permute-done.9.refs_2_ = bf16[2,32,512]{2,1,0:T(8,128)(2,1)S(1)} collective-permute-done((bf16[2,32,512]{2,1,0:T(8,128)(2,1)S(1)}, bf16[2,32,512]{2,1,0:T(8,128)(2,1)S(1)}, u32[]{:S(2)}, u32[]{:S(2)}) %collective-permute-start.9) | collective-permute-done | bytes 65568 | tf_op jit(solution)/shard_map/ppermute | solution.py:487
  103.8 0.3 collective-permute-done.10.refs_3_
  104.2 0.1 collective-permute-start.11
  104.3 0.0 all-to-all-done.2
  104.3 0.6 collective-permute-start.20
  104.9 2.7 %collective-permute-start.19 = (f32[56,128]{1,0:T(8,128)S(1)}, f32[56,128]{1,0:T(8,128)S(1)}, u32[]{:S(2)}, u32[]{:S(2)}) collective-permute-start(f32[56,128]{1,0:T(8,128)S(1)} %convert_reduce_fusion.refs_0_), channel_id=1, source_target_pairs={{0,128},{64,192},{128,0},{192,64},{1,129},{65,193},{129,1},{193,65... | collective-permute-start | bytes 86024 | tf_op jit(solution)/shard_map/ppermute | solution.py:540
  107.6 0.8 collective-permute-start.18
  108.5 0.0 collective-permute-done.11.refs_4_
  108.5 0.8 shard_map.142
  109.3 0.0 collective-permute-done.20.refs_3_
  109.3 1.0 collective-permute-done.19.refs_2_
  110.3 1.2 %collective-permute-done.18.refs_1_ = f32[56,128]{1,0:T(8,128)S(1)} collective-permute-done((f32[56,128]{1,0:T(8,128)S(1)}, f32[56,128]{1,0:T(8,128)S(1)}, u32[]{:S(2)}, u32[]{:S(2)}) %collective-permute-start.18) | collective-permute-done | bytes 28704 | tf_op jit(solution)/shard_map/ppermute | solution.py:540
  111.5 0.6 shard_map.145
  (6 shorter events, 0.1 us)
Async XLA Ops:
  0.6 12.4 %collective-permute-start.4 = (bf16[8,128,256]{2,1,0:T(8,128)(2,1)}, bf16[8,128,256]{2,1,0:T(8,128)(2,1)S(1)}, u32[]{:S(2)}, u32[]{:S(2)}) collective-permute-start(bf16[8,128,256]{2,1,0:T(8,128)(2,1)} %bitcast.13), channel_id=1, source_target_pairs={{0,8},{8,0},{16,24},{24,16},{32,40},{40,32},{48,56},{56,48},{1,9},... | collective-permute-start | bytes 1572872 | tf_op jit(solution)/shard_map/ppermute | solution.py:483
  0.7 23.7 %collective-permute-start.12 = (bf16[8,128,256]{2,1,0:T(8,128)(2,1)}, bf16[8,128,256]{2,1,0:T(8,128)(2,1)S(1)}, u32[]{:S(2)}, u32[]{:S(2)}) collective-permute-start(bf16[8,128,256]{2,1,0:T(8,128)(2,1)} %bitcast.15), channel_id=1, source_target_pairs={{0,8},{8,0},{16,24},{24,16},{32,40},{40,32},{48,56},{56,48},{1,9},... | collective-permute-start | bytes 1572872 | tf_op jit(solution)/shard_map/ppermute | solution.py:483
  1.2 23.2 %collective-permute-start.13 = (bf16[4,64,512]{2,1,0:T(8,128)(2,1)}, bf16[4,64,512]{2,1,0:T(8,128)(2,1)S(1)}, u32[]{:S(2)}, u32[]{:S(2)}) collective-permute-start(bf16[4,64,512]{2,1,0:T(8,128)(2,1)} %bitcast.18), channel_id=1, source_target_pairs={{0,8},{8,0},{16,24},{24,16},{32,40},{40,32},{48,56},{56,48},{1,9},... | collective-permute-start | bytes 786440 | tf_op jit(solution)/shard_map/ppermute | solution.py:483
  2.2 6.9 %collective-permute-start.1 = (bf16[128,256]{1,0:T(8,128)(2,1)S(1)}, bf16[128,256]{1,0:T(8,128)(2,1)S(1)}, u32[]{:S(2)}, u32[]{:S(2)}) collective-permute-start(bf16[128,256]{1,0:T(8,128)(2,1)S(1)} %get-tuple-element.43), channel_id=1, source_target_pairs={{1,0},{2,1},{3,2},{4,3},{5,4},{6,5},{7,6},{0,7},{9,8},{10,9},{11,1... | collective-permute-start | bytes 196616 | tf_op jit(solution)/shard_map/ppermute | solution.py:498
  6.7 6.4 %collective-permute-start = (bf16[128,256]{1,0:T(8,128)(2,1)S(1)}, bf16[128,256]{1,0:T(8,128)(2,1)S(1)}, u32[]{:S(2)}, u32[]{:S(2)}) collective-permute-start(bf16[128,256]{1,0:T(8,128)(2,1)S(1)} %get-tuple-element.44), channel_id=1, source_target_pairs={{0,1},{1,2},{2,3},{3,4},{4,5},{5,6},{6,7},{7,0},{8,9},{9,10},{10,1... | collective-permute-start | bytes 196616 | tf_op jit(solution)/shard_map/ppermute | solution.py:497
  9.1 8.6 %collective-permute-start.3 = (bf16[128,256]{1,0:T(8,128)(2,1)S(1)}, bf16[128,256]{1,0:T(8,128)(2,1)S(1)}, u32[]{:S(2)}, u32[]{:S(2)}) collective-permute-start(bf16[128,256]{1,0:T(8,128)(2,1)S(1)} %collective-permute-done.1.refs_1_), channel_id=1, source_target_pairs={{0,8},{8,0},{16,24},{24,16},{32,40},{40,32},{48,56},{56,48},{1,9},... | collective-permute-start | bytes 196616 | tf_op jit(solution)/shard_map/ppermute | solution.py:483
  13.0 4.8 %collective-permute-start.2 = (bf16[128,256]{1,0:T(8,128)(2,1)S(1)}, bf16[128,256]{1,0:T(8,128)(2,1)S(1)}, u32[]{:S(2)}, u32[]{:S(2)}) collective-permute-start(bf16[128,256]{1,0:T(8,128)(2,1)S(1)} %collective-permute-done.refs_0_), channel_id=1, source_target_pairs={{0,8},{8,0},{16,24},{24,16},{32,40},{40,32},{48,56},{56,48},{1,9},... | collective-permute-start | bytes 196616 | tf_op jit(solution)/shard_map/ppermute | solution.py:483
  14.4 21.4 %collective-permute-start.5 = (bf16[2,144,256]{2,1,0:T(8,128)(2,1)S(1)}, bf16[2,144,256]{2,1,0:T(8,128)(2,1)S(1)}, u32[]{:S(2)}, u32[]{:S(2)}) collective-permute-start(bf16[2,144,256]{2,1,0:T(8,128)(2,1)S(1)} %get-tuple-element.24), channel_id=1, source_target_pairs={{0,16},{8,24},{16,32},{24,40},{32,48},{40,56},{48,0},{56,8},{1,17}... | collective-permute-start | bytes 442376 | tf_op jit(solution)/shard_map/ppermute | solution.py:487
  18.7 20.0 %all-to-all-start = ((bf16[4,2,40,256]{3,2,1,0:T(8,128)(2,1)}), bf16[4,2,40,256]{3,2,1,0:T(8,128)(2,1)S(1)}, u32[]{:S(2)}, u32[]{:S(2)}) async-start(bf16[4,2,40,256]{3,2,1,0:T(8,128)(2,1)} %shard_map.139), calls=%async_computation | async-start | bytes 327680 | tf_op jit(solution)/shard_map/all_to_all | solution.py:494
  25.6 44.3 %collective-permute-start.14 = (bf16[2,192,256]{2,1,0:T(8,128)(2,1)S(1)}, bf16[2,192,256]{2,1,0:T(8,128)(2,1)S(1)}, u32[]{:S(2)}, u32[]{:S(2)}) collective-permute-start(bf16[2,192,256]{2,1,0:T(8,128)(2,1)S(1)} %get-tuple-element.32), channel_id=1, source_target_pairs={{0,16},{8,24},{16,32},{24,40},{32,48},{40,56},{48,0},{56,8},{1,17}... | collective-permute-start | bytes 589832 | tf_op jit(solution)/shard_map/ppermute | solution.py:487
  28.6 41.3 %collective-permute-start.15 = (bf16[2,192,256]{2,1,0:T(8,128)(2,1)S(1)}, bf16[2,192,256]{2,1,0:T(8,128)(2,1)S(1)}, u32[]{:S(2)}, u32[]{:S(2)}) collective-permute-start(bf16[2,192,256]{2,1,0:T(8,128)(2,1)S(1)} %get-tuple-element.33), channel_id=1, source_target_pairs={{0,32},{8,40},{16,48},{24,56},{32,0},{40,8},{48,16},{56,24},{1,33}... | collective-permute-start | bytes 589832 | tf_op jit(solution)/shard_map/ppermute | solution.py:487
  32.2 37.7 %collective-permute-start.16 = (bf16[2,192,256]{2,1,0:T(8,128)(2,1)S(1)}, bf16[2,192,256]{2,1,0:T(8,128)(2,1)S(1)}, u32[]{:S(2)}, u32[]{:S(2)}) collective-permute-start(bf16[2,192,256]{2,1,0:T(8,128)(2,1)S(1)} %get-tuple-element.34), channel_id=1, source_target_pairs={{0,48},{8,56},{16,0},{24,8},{32,16},{40,24},{48,32},{56,40},{1,49}... | collective-permute-start | bytes 589832 | tf_op jit(solution)/shard_map/ppermute | solution.py:487
  35.7 15.4 %collective-permute-start.6 = (bf16[2,144,256]{2,1,0:T(8,128)(2,1)S(1)}, bf16[2,144,256]{2,1,0:T(8,128)(2,1)S(1)}, u32[]{:S(2)}, u32[]{:S(2)}) collective-permute-start(bf16[2,144,256]{2,1,0:T(8,128)(2,1)S(1)} %get-tuple-element.25), channel_id=1, source_target_pairs={{0,32},{8,40},{16,48},{24,56},{32,0},{40,8},{48,16},{56,24},{1,33}... | collective-permute-start | bytes 442376 | tf_op jit(solution)/shard_map/ppermute | solution.py:487
  35.9 26.2 %collective-permute-start.7 = (bf16[2,144,256]{2,1,0:T(8,128)(2,1)S(1)}, bf16[2,144,256]{2,1,0:T(8,128)(2,1)S(1)}, u32[]{:S(2)}, u32[]{:S(2)}) collective-permute-start(bf16[2,144,256]{2,1,0:T(8,128)(2,1)S(1)} %get-tuple-element.26), channel_id=1, source_target_pairs={{0,48},{8,56},{16,0},{24,8},{32,16},{40,24},{48,32},{56,40},{1,49}... | collective-permute-start | bytes 442376 | tf_op jit(solution)/shard_map/ppermute | solution.py:487
  70.9 1.9 %collective-permute-start.17 = (bf16[4,4,2,56,128]{4,3,2,1,0:T(8,128)(2,1)S(1)}, bf16[4,4,2,56,128]{4,3,2,1,0:T(8,128)(2,1)S(1)}, u32[]{:S(2)}, u32[]{:S(2)}) collective-permute-start(bf16[4,4,2,56,128]{4,3,2,1,0:T(8,128)(2,1)S(1)} %get-tuple-element.40), channel_id=1, source_target_pairs={{0,8},{8,0},{16,24},{24,16},{32,40},{40,32},{48,56},{56,48},{1,9},... | collective-permute-start | bytes 1376264 | tf_op jit(solution)/shard_map/ppermute | solution.py:483
  85.3 18.9 %all-to-all-start.2 = ((bf16[8,56,128]{2,1,0:T(8,128)(2,1)}), bf16[8,56,128]{2,1,0:T(8,128)(2,1)S(1)}, u32[]{:S(2)}, u32[]{:S(2)}) async-start(bf16[8,56,128]{2,1,0:T(8,128)(2,1)} %bitcast.8), calls=%async_computation.2 | async-start | bytes 229376 | tf_op jit(solution)/shard_map/all_to_all | solution.py:538
  90.9 10.1 %collective-permute-start.8 = (bf16[2,32,512]{2,1,0:T(8,128)(2,1)S(1)}, bf16[2,32,512]{2,1,0:T(8,128)(2,1)S(1)}, u32[]{:S(2)}, u32[]{:S(2)}) collective-permute-start(bf16[2,32,512]{2,1,0:T(8,128)(2,1)S(1)} %get-tuple-element.28), channel_id=1, source_target_pairs={{0,16},{8,24},{16,32},{24,40},{32,48},{40,56},{48,0},{56,8},{1,17}... | collective-permute-start | bytes 196616 | tf_op jit(solution)/shard_map/ppermute | solution.py:487
  93.8 9.9 %collective-permute-start.9 = (bf16[2,32,512]{2,1,0:T(8,128)(2,1)S(1)}, bf16[2,32,512]{2,1,0:T(8,128)(2,1)S(1)}, u32[]{:S(2)}, u32[]{:S(2)}) collective-permute-start(bf16[2,32,512]{2,1,0:T(8,128)(2,1)S(1)} %get-tuple-element.29), channel_id=1, source_target_pairs={{0,32},{8,40},{16,48},{24,56},{32,0},{40,8},{48,16},{56,24},{1,33}... | collective-permute-start | bytes 196616 | tf_op jit(solution)/shard_map/ppermute | solution.py:487
  97.4 6.7 %collective-permute-start.10 = (bf16[2,32,512]{2,1,0:T(8,128)(2,1)S(1)}, bf16[2,32,512]{2,1,0:T(8,128)(2,1)S(1)}, u32[]{:S(2)}, u32[]{:S(2)}) collective-permute-start(bf16[2,32,512]{2,1,0:T(8,128)(2,1)S(1)} %get-tuple-element.30), channel_id=1, source_target_pairs={{0,48},{8,56},{16,0},{24,8},{32,16},{40,24},{48,32},{56,40},{1,49}... | collective-permute-start | bytes 196616 | tf_op jit(solution)/shard_map/ppermute | solution.py:487
  104.2 4.3 %collective-permute-start.11 = (bf16[4,32,512]{2,1,0:T(8,128)(2,1)S(1)}, bf16[4,32,512]{2,1,0:T(8,128)(2,1)S(1)}, u32[]{:S(2)}, u32[]{:S(2)}) collective-permute-start(bf16[4,32,512]{2,1,0:T(8,128)(2,1)S(1)} %pad_maximum_fusion), channel_id=1, source_target_pairs={{0,8},{8,0},{16,24},{24,16},{32,40},{40,32},{48,56},{56,48},{1,9},... | collective-permute-start | bytes 393224 | tf_op jit(solution)/shard_map/ppermute | solution.py:483
  104.3 5.0 %collective-permute-start.20 = (f32[56,128]{1,0:T(8,128)S(1)}, f32[56,128]{1,0:T(8,128)S(1)}, u32[]{:S(2)}, u32[]{:S(2)}) collective-permute-start(f32[56,128]{1,0:T(8,128)S(1)} %convert_reduce_fusion.refs_0_), channel_id=1, source_target_pairs={{0,192},{64,128},{128,64},{192,0},{1,193},{65,129},{129,65},{193,1... | collective-permute-start | bytes 86024 | tf_op jit(solution)/shard_map/ppermute | solution.py:540
  104.9 5.4 %collective-permute-start.19 = (f32[56,128]{1,0:T(8,128)S(1)}, f32[56,128]{1,0:T(8,128)S(1)}, u32[]{:S(2)}, u32[]{:S(2)}) collective-permute-start(f32[56,128]{1,0:T(8,128)S(1)} %convert_reduce_fusion.refs_0_), channel_id=1, source_target_pairs={{0,128},{64,192},{128,0},{192,64},{1,129},{65,193},{129,1},{193,65... | collective-permute-start | bytes 86024 | tf_op jit(solution)/shard_map/ppermute | solution.py:540
  107.6 3.9 %collective-permute-start.18 = (f32[56,128]{1,0:T(8,128)S(1)}, f32[56,128]{1,0:T(8,128)S(1)}, u32[]{:S(2)}, u32[]{:S(2)}) collective-permute-start(f32[56,128]{1,0:T(8,128)S(1)} %convert_reduce_fusion.refs_0_), channel_id=1, source_target_pairs={{0,64},{64,0},{128,192},{192,128},{1,65},{65,1},{129,193},{193,129... | collective-permute-start | bytes 86024 | tf_op jit(solution)/shard_map/ppermute | solution.py:540
